TPU v7x, 32 devices: a whole 2x2x4 slice. The times are simulated.
32 devices in a mesh: seq: 8 (over z, x), head: 4 (over y, core).
Axes of the slice: x: 2, y: 2, z: 4, core: 2. Of those that a mesh axis runs over, the one named last changes fastest.
Arguments:
- qkv_heads: bfloat16 [8192, 8, 384], P('seq', 'head'), may hold values from -6 to 6
- clusters: int32 [8, 64], P('head'), may hold values from 0 to 7, as said below
- out_weight: bfloat16 [1024, 4096], P(None, 'head'), may hold values from -0.5 to 0.5
Outputs:
- projected: bfloat16 [8192, 4096], P('seq', 'head')
Inputs may be any that keep to these rules, and one draw needn't show every extreme that they name: For every head, a cluster holds at most 16 blocks and one cluster holds exactly 16; the 8 blocks of one head on one index of seq put at most 2 into any one cluster, and for every head some index puts exactly 2 into one. Counting the 2 heads of a head group together, the blocks of one index of seq put at most 4 into clusters with one number, and for every group some index puts exactly 4 there.
All inputs are finite; a program needn't handle non-finite values.
Results may differ from a plain program's by a relative error of at most 0.0054.
Values may be sent and summed in bfloat16 or wider, within the bound.
No kernel may reach another device: no remote copies, remote signals or barrier semaphores. Data moves between devices by JAX's collectives and lax.ppermute only.
A program may use at most 64 MiB of HBM per device.

v0:
```python
import math

import jax
import jax.numpy as jnp
from jax import lax
from jax.sharding import PartitionSpec as P


def softmax_rows(query_part, query_pos, key_rows, value_rows, key_pos, usable, score_scale):
    scores = jnp.dot(query_part, key_rows.T, preferred_element_type=jnp.float32) * score_scale
    allowed = usable[None, :] & (key_pos[None, :] <= query_pos[:, None])
    scores = jnp.where(allowed, scores, -1e30)
    highest = jnp.max(scores, axis=1, keepdims=True)
    weights = jnp.exp(scores - highest)
    totals = jnp.sum(weights, axis=1, keepdims=True)
    probabilities = weights.astype(jnp.bfloat16)
    attended = jnp.dot(probabilities, value_rows, preferred_element_type=jnp.float32) / totals
    return attended.astype(jnp.bfloat16)


def attend_all(queries, key_rows, value_rows, positions, usable):
    length = queries.shape[0]
    rows_step = min(512, length)
    score_scale = 1.0 / math.sqrt(queries.shape[1])
    pieces = []
    for step_index in range(length // rows_step):
        first_row = step_index * rows_step
        key_end = first_row + rows_step
        pieces.append(
            softmax_rows(
                queries[first_row : first_row + rows_step],
                positions[first_row : first_row + rows_step],
                key_rows[:key_end],
                value_rows[:key_end],
                positions[:key_end],
                usable[:key_end],
                score_scale,
            )
        )
    return jnp.concatenate(pieces, axis=0)


def slot_tables(owners, myself, pair_slots):
    source_count, item_count = owners.shape
    item_ids = jnp.arange(item_count, dtype=jnp.int32)
    before = item_ids[None, :] < item_ids[:, None]
    same_owner = owners[:, :, None] == owners[:, None, :]
    rank_within = jnp.sum((same_owner & before[None]).astype(jnp.int32), axis=2)
    own_owner = lax.dynamic_index_in_dim(owners, myself, 0, keepdims=False)
    own_rank = lax.dynamic_index_in_dim(rank_within, myself, 0, keepdims=False)
    own_slot = own_owner * pair_slots + own_rank
    slot_ids = jnp.arange(source_count * pair_slots, dtype=jnp.int32)
    slot_match = own_slot[None, :] == slot_ids[:, None]
    source_item = jnp.sum(slot_match.astype(jnp.int32) * item_ids[None, :], axis=1)
    filled = jnp.any(slot_match, axis=1)
    rank_ids = jnp.arange(pair_slots, dtype=jnp.int32)
    arriving = (owners == myself)[:, None, :] & (rank_within[:, None, :] == rank_ids[None, :, None])
    arrived_item = jnp.sum(arriving.astype(jnp.int32) * item_ids[None, None, :], axis=2).reshape(-1)
    arrived = jnp.any(arriving, axis=2).reshape(-1)
    return (own_slot, source_item, filled, arrived_item, arrived)


def per_device(qkv_heads, clusters, out_weight):
    seq_count = lax.axis_size("seq")
    myself = lax.axis_index("seq")
    tok_rows, head_local, triple = qkv_heads.shape
    head_width = triple // 3
    block_total = clusters.shape[1]
    per_shard = block_total // seq_count
    block_len = tok_rows // per_shard
    capacity = 2 * per_shard
    cluster_table = clusters.reshape(head_local, seq_count, per_shard)
    blocks = qkv_heads.reshape(per_shard, block_len, head_local, triple).transpose(2, 0, 1, 3)
    pair_slots = (head_local * capacity + seq_count - 1) // seq_count
    owners = cluster_table.transpose(1, 0, 2).reshape(seq_count, head_local * per_shard)
    own_slot, source_item, filled, arrived_item, arrived = slot_tables(owners, myself, pair_slots)
    flat_blocks = blocks.reshape(head_local * per_shard, block_len, triple)
    outgoing = jnp.take(flat_blocks, source_item, axis=0)
    outgoing = jnp.where(filled[:, None, None], outgoing, jnp.zeros((), outgoing.dtype))
    incoming = lax.all_to_all(outgoing, "seq", split_axis=0, concat_axis=0, tiled=True)
    slot_head = arrived_item // per_shard
    slot_source = jnp.arange(seq_count * pair_slots, dtype=jnp.int32) // pair_slots
    slot_block = slot_source * per_shard + arrived_item % per_shard
    slot_count = incoming.shape[0]
    slot_ids = jnp.arange(slot_count, dtype=jnp.int32)
    compact_ids = jnp.arange(capacity, dtype=jnp.int32)
    place_all = jnp.zeros((slot_count,), jnp.int32)
    padded_parts = []
    for head_index in range(head_local):
        belongs = arrived & (slot_head == head_index)
        belongs_int = belongs.astype(jnp.int32)
        places = jnp.cumsum(belongs_int) - belongs_int
        chosen = belongs[None, :] & (places[None, :] == compact_ids[:, None])
        chosen_int = chosen.astype(jnp.int32)
        pick_slot = jnp.sum(chosen_int * slot_ids[None, :], axis=1)
        kept_valid = jnp.any(chosen, axis=1)
        kept_ids = jnp.sum(chosen_int * slot_block[None, :], axis=1)
        gathered = jnp.take(incoming, pick_slot, axis=0).reshape(capacity * block_len, triple)
        positions = (
            kept_ids[:, None] * block_len + jnp.arange(block_len, dtype=jnp.int32)[None, :]
        ).reshape(-1)
        usable = jnp.repeat(kept_valid, block_len)
        attended = attend_all(
            gathered[:, :head_width],
            gathered[:, head_width : 2 * head_width],
            gathered[:, 2 * head_width :],
            positions,
            usable,
        )
        padded_parts.append(attended.reshape(capacity, block_len, head_width))
        padded_parts.append(jnp.zeros((1, block_len, head_width), jnp.bfloat16))
        place_all = place_all + jnp.where(belongs, places, 0)
    padded_all = jnp.concatenate(padded_parts, axis=0)
    back_index = jnp.where(arrived, slot_head * (capacity + 1) + place_all, capacity)
    outbound = jnp.take(padded_all, back_index, axis=0)
    home_slots = lax.all_to_all(outbound, "seq", split_axis=0, concat_axis=0, tiled=True)
    own_blocks = jnp.take(home_slots, own_slot, axis=0).reshape(
        head_local, per_shard, block_len, head_width
    )
    features = own_blocks.transpose(1, 2, 0, 3).reshape(tok_rows, head_local * head_width)
    summed = jnp.dot(
        lax.all_gather(features, "head", axis=1, tiled=True),
        out_weight,
        preferred_element_type=jnp.float32,
    )
    return summed.astype(jnp.bfloat16)


def solution(mesh):
    in_specs = (P("seq", "head", None), P("head", None), P(None, "head"))
    out_specs = P("seq", "head")
    return jax.shard_map(
        per_device, mesh=mesh, in_specs=in_specs, out_specs=out_specs, check_vma=False
    )
```

profile of v0, /device:TPU:0, one launch (start us, length us, event | category | flops | bytes accessed | tf_op | source)
XLA Modules:
  0.0 197.5 jit_solution(17026624275354825182)
XLA Ops:
  6.5 0.9 reshape.564
  8.3 0.7 fusion.110
  9.4 2.8 %copy.51 = bf16[1024,2,384]{2,0,1:T(8,128)(2,1)} copy(bf16[1024,2,384]{2,1,0:T(2,128)(2,1)} %param.5) | data formatting | bytes 3145728 | tf_op args[0]
  12.2 4.1 %gather_fusion = bf16[32,128,384]{2,1,0:T(8,128)(2,1)} fusion(bf16[16,128,384]{2,1,0:T(8,128)(2,1)} %bitcast.78, s32[1024]{0:T(1024)S(1)} %pad_clamp_fusion.4), kind=kCustom, calls=%fused_computation.2 | custom fusion | bytes 6291584 | tf_op jit(solution)/shard_map/jit(_take)/gather | solution.py:78
  16.3 4.1 %select_select_fusion = bf16[32,128,384]{2,1,0:T(8,128)(2,1)} fusion(bf16[32,128,384]{2,1,0:T(8,128)(2,1)} %gather_fusion, pred[32]{0:T(512)(128)(4,1)S(1)} %compare_and_fusion.4, pred[32]{0:T(512)(128)(4,1)S(1)} %fusion.100), kind=kLoop, calls=%fused_computation.19 | loop fusion | flops 3145728 | bytes 6291520 | tf_op jit(solution)/shard_map/jit(_where)/select_n | solution.py:79
  20.4 7.3 %all-to-all-start = ((bf16[32,128,384]{2,1,0:T(8,128)(2,1)}), bf16[32,128,384]{2,1,0:T(8,128)(2,1)}, u32[]{:S(2)}, u32[]{:S(2)}) async-start(bf16[32,128,384]{2,1,0:T(8,128)(2,1)} %select_select_fusion), calls=%async_computation | async-start | bytes 6291456 | tf_op jit(solution)/shard_map/all_to_all | solution.py:80
  30.0 68.5 %all-to-all-done = bf16[32,128,384]{2,1,0:T(8,128)(2,1)} async-done(((bf16[32,128,384]{2,1,0:T(8,128)(2,1)}), bf16[32,128,384]{2,1,0:T(8,128)(2,1)}, u32[]{:S(2)}, u32[]{:S(2)}) %all-to-all-start) | async-done | bytes 3145760 | tf_op jit(solution)/shard_map/all_to_all | solution.py:80
  98.5 3.8 %gather_fusion.3 = bf16[16,128,384]{2,1,0:T(8,128)(2,1)} fusion(bf16[32,128,384]{2,1,0:T(8,128)(2,1)} %all-to-all-done, s32[1024]{0:T(1024)S(1)} %pad_clamp_fusion.3), kind=kCustom, calls=%fused_computation.clone | custom fusion | bytes 3145792 | tf_op jit(solution)/shard_map/jit(_take)/gather | solution.py:98
  102.3 1.6 broadcast_select_fusion.1
  105.4 3.8 %gather_fusion.4 = bf16[16,128,384]{2,1,0:T(8,128)(2,1)} fusion(bf16[32,128,384]{2,1,0:T(8,128)(2,1)} %all-to-all-done, s32[1024]{0:T(1024)S(1)} %pad_clamp_fusion.2), kind=kCustom, calls=%fused_computation.1.clone | custom fusion | bytes 3145792 | tf_op jit(solution)/shard_map/jit(_take)/gather | solution.py:98
  109.2 1.6 broadcast_select_fusion
  112.3 0.7 fusion.117
  114.0 0.7 fusion.113
  115.8 1.0 fusion.116
  117.3 0.7 fusion.45
  118.0 1.0 fusion.112
  119.6 0.7 fusion.42
  120.2 1.2 fusion.115
  121.5 0.9 fusion
  122.4 0.8 fusion.53
  123.1 1.2 fusion.111
  124.4 0.7 fusion.2
  125.1 0.8 fusion.50
  126.2 1.7 gather_fusion.1
  127.8 2.4 %broadcast_select_fusion.2 = bf16[32,128,128]{2,1,0:T(8,128)(2,1)} fusion(bf16[32,128,128]{2,1,0:T(8,128)(2,1)} %gather_fusion.1, pred[32]{0:T(512)(128)(4,1)S(1)} %get-tuple-element.15), kind=kLoop, calls=%fused_computation.68 | loop fusion | flops 524288 | bytes 2097184 | tf_op jit(solution)/shard_map/jit(_take)/select_n | solution.py:115
  130.2 3.6 %all-to-all-start.1 = ((bf16[32,128,128]{2,1,0:T(8,128)(2,1)}), bf16[32,128,128]{2,1,0:T(8,128)(2,1)S(1)}, u32[]{:S(2)}, u32[]{:S(2)}) async-start(bf16[32,128,128]{2,1,0:T(8,128)(2,1)} %broadcast_select_fusion.2), calls=%async_computation.1 | async-start | bytes 2097152 | tf_op jit(solution)/shard_map/all_to_all | solution.py:116
  133.9 25.8 %all-to-all-done.1 = bf16[32,128,128]{2,1,0:T(8,128)(2,1)S(1)} async-done(((bf16[32,128,128]{2,1,0:T(8,128)(2,1)}), bf16[32,128,128]{2,1,0:T(8,128)(2,1)S(1)}, u32[]{:S(2)}, u32[]{:S(2)}) %all-to-all-start.1) | async-done | bytes 1048608 | tf_op jit(solution)/shard_map/all_to_all | solution.py:116
  159.7 1.4 gather_fusion.2
  161.2 1.2 select_bitcast_fusion
  162.6 0.9 copy.59
  163.5 21.8 %all-gather.2.cloned.1.call-done = bf16[1024,1024]{0,1:T(8,128)(2,1)} async-done(((bf16[1024,256]{0,1:T(8,128)(2,1)}), bf16[1024,1024]{0,1:T(8,128)(2,1)}) %all-gather.2.cloned.1.call-update) | async-done | bytes 2097168 | tf_op jit(solution)/shard_map/all_gather | solution.py:122
  185.3 5.3 %convolution_convert_fusion = bf16[1024,1024]{1,0:T(8,128)(2,1)} fusion(bf16[1024,1024]{0,1:T(8,128)(2,1)} %all-gather.2.cloned.1.call-done, bf16[1024,1024]{1,0:T(8,128)(2,1)S(1)} %copy-done), kind=kOutput, calls=%fused_computation.32 | convolution fusion | flops 2148532224 | bytes 6291456 | tf_op jit(solution)/shard_map/dot_general | solution.py:121
  (81 shorter events, 10.3 us)
Async XLA Ops:
  6.5 178.8 %copy-start = (bf16[1024,1024]{1,0:T(8,128)(2,1)S(1)}, bf16[1024,1024]{1,0:T(8,128)(2,1)}, u32[]{:S(2)}) copy-start(bf16[1024,1024]{1,0:T(8,128)(2,1)} %param.7) | copy-start | bytes 6291460
  20.4 78.1 %all-to-all-start = ((bf16[32,128,384]{2,1,0:T(8,128)(2,1)}), bf16[32,128,384]{2,1,0:T(8,128)(2,1)}, u32[]{:S(2)}, u32[]{:S(2)}) async-start(bf16[32,128,384]{2,1,0:T(8,128)(2,1)} %select_select_fusion), calls=%async_computation | async-start | bytes 6291456 | tf_op jit(solution)/shard_map/all_to_all | solution.py:80
  103.9 1.1 copy-start.1
  110.9 1.4 copy-start.2
  130.2 29.6 %all-to-all-start.1 = ((bf16[32,128,128]{2,1,0:T(8,128)(2,1)}), bf16[32,128,128]{2,1,0:T(8,128)(2,1)S(1)}, u32[]{:S(2)}, u32[]{:S(2)}) async-start(bf16[32,128,128]{2,1,0:T(8,128)(2,1)} %broadcast_select_fusion.2), calls=%async_computation.1 | async-start | bytes 2097152 | tf_op jit(solution)/shard_map/all_to_all | solution.py:116
  133.8 51.5 %all-gather.2.cloned.1.call-start = ((), (), s32[]{:S(2)}) async-start(), calls=%async_computation.2 | async-start | bytes 2621440 | tf_op jit(solution)/shard_map/all_gather | solution.py:122
Sparse Core Ops, SparseCore 0:
  163.7 21.6 all-gather.1
where the time goes:
time: 198 us; the launch traced here: 197 us
  waiting for transfers between devices  116 us (59%)
  local copies, waits for them, and re-layouts  22.4 us (11%)
  other arithmetic  17.7 us (9%)
  matrix products  16.6 us (8%)
  between operations  13.7 us (7%)
  starting transfers between devices  10.9 us (6%)
    all_to_all x1, waiting for transfers between devices, per_device(): lax.all_to_all(outgoing, 'seq', split_axis=0, concat_axis=0, tiled=True)  68.5 us
    all_to_all x1, waiting for transfers between devices, per_device(): lax.all_to_all(outbound, 'seq', split_axis=0, concat_axis=0, tiled=True)  25.8 us
    all_gather x1, waiting for transfers between devices, per_device(): lax.all_gather(features, 'head', axis=1, tiled=True)  21.8 us
    gather x2, local copies, waits for them, and re-layouts, per_device(): jnp.take(incoming, pick_slot, axis=0).reshape(capacity * block_len, triple)  7.59 us
    all_to_all x1, starting transfers between devices, per_device(): lax.all_to_all(outgoing, 'seq', split_axis=0, concat_axis=0, tiled=True)  7.28 us
    dot_general x8, matrix products, softmax_rows(): jnp.dot(query_part, key_rows.T, preferred_element_type=jnp.float32)  6.67 us
    dot_general x1, matrix products, per_device(): jnp.dot(lax.all_gather(features, 'head', axis=1, tiled=True), out_weight,...  5.3 us
    dot_general x8, matrix products, softmax_rows(): jnp.dot(probabilities, value_rows, preferred_element_type=jnp.float32)  4.65 us
  transfers between devices with their start and end apart: 3, of which 3 were waited for; matrix products, arithmetic and copies ran while one was open for 1% of the time, Pallas kernels for 0%

commit v1 on v0

--- a/solution.py
+++ b/solution.py
@@ -1,9 +1,15 @@
+import functools
 import math
 
 import jax
 import jax.numpy as jnp
 from jax import lax
+from jax.experimental import pallas as pl
+from jax.experimental.pallas import tpu as pltpu
 from jax.sharding import PartitionSpec as P
+
+
+NEG = -1e30
 
 
 def softmax_rows(query_part, query_pos, key_rows, value_rows, key_pos, usable, score_scale):
@@ -60,7 +66,7 @@
     return (own_slot, source_item, filled, arrived_item, arrived)
 
 
-def per_device(qkv_heads, clusters, out_weight):
+def routed_plan(qkv_heads, clusters, out_weight):
     seq_count = lax.axis_size("seq")
     myself = lax.axis_index("seq")
     tok_rows, head_local, triple = qkv_heads.shape
@@ -126,9 +132,491 @@
     return summed.astype(jnp.bfloat16)
 
 
+VMEM_BYTES = 24 * 1024 * 1024
+
+
+def split_kernel(ids_ref, qkv_ref, q_keep, kv_keep, first, second, third):
+    column = ids_ref[0, 0]
+    plane = ids_ref[0, 1]
+    rows, width = q_keep.shape
+
+    def pieces(head):
+        yield lambda: qkv_ref[head, :, :width]
+        yield lambda: qkv_ref[head, :, width : 2 * width]
+        yield lambda: jnp.concatenate(
+            [
+                qkv_ref[head, b * width : (b + 1) * width, 2 * width :].T
+                for b in range(rows // width)
+            ],
+            axis=0,
+        )
+
+    query, key, value = pieces(column)
+    q_keep[...] = query()
+    kv_keep[0] = key()
+    kv_keep[1] = value()
+    query, key, value = pieces(1 - column)
+
+    @pl.when(plane == 0)
+    def _():
+        first[...] = key()
+        second[...] = value()
+        third[...] = query()
+
+    @pl.when(plane > 0)
+    def _():
+        first[...] = query()
+        second[...] = key()
+        third[...] = value()
+
+
+def split_heads(ids, by_head):
+    heads, rows, triple = by_head.shape
+    width = triple // 3
+    step = rows // 4
+    one = jax.ShapeDtypeStruct((rows, width), by_head.dtype)
+    two = jax.ShapeDtypeStruct((2, rows, width), by_head.dtype)
+    spec = pl.BlockSpec((step, width), lambda i: (i, 0))
+    return pl.pallas_call(
+        split_kernel,
+        grid=(rows // step,),
+        in_specs=[
+            pl.BlockSpec(memory_space=pltpu.SMEM),
+            pl.BlockSpec((heads, step, triple), lambda i: (0, i, 0)),
+        ],
+        out_specs=[spec, pl.BlockSpec((2, step, width), lambda i: (0, i, 0)), spec, spec, spec],
+        out_shape=[one, two, one, one, one],
+        compiler_params=pltpu.CompilerParams(vmem_limit_bytes=VMEM_BYTES),
+        name="split_heads",
+    )(ids, by_head)
+
+
+OWN, LOW, BOTH, NEAR, KEPT, SWAPPED = range(0, 18, 3)
+TABLE_ROWS = 24
+
+
+def tables_kernel(per_shard, cluster_count, ids_ref, table_ref, out_ref):
+    column = ids_ref[0, 0]
+    plane = ids_ref[0, 1]
+    blocks = table_ref.shape[1]
+    span = 2 * per_shard
+    out_ref[...] = jnp.zeros_like(out_ref)
+    labels = jnp.where(column == 0, table_ref[0:1, :], table_ref[1:2, :])
+    down = lax.broadcasted_iota(jnp.int32, (blocks, blocks), 0)
+    along = lax.broadcasted_iota(jnp.int32, (blocks, blocks), 1)
+    wide = jnp.broadcast_to(labels, (blocks, blocks))
+    tall = jnp.sum(jnp.where(down == along, wide, 0), axis=1, keepdims=True)
+    before = (tall < wide) | ((tall == wide) & (down < along))
+    cluster = lax.broadcasted_iota(jnp.int32, (blocks, cluster_count), 1)
+    block = lax.broadcasted_iota(jnp.int32, (blocks, 1), 0)
+    in_plane = block // span
+    side = lax.rem(block // per_shard, 2)
+    high = (in_plane == 2) | (in_plane == 3)
+    for row, member in (
+        (OWN, in_plane == plane),
+        (LOW, in_plane == plane - 1),
+        (BOTH, (in_plane == plane) | (in_plane == plane - 1)),
+        (NEAR, in_plane == plane + 1),
+        (KEPT, high & (side == column)),
+        (SWAPPED, high & (side != column)),
+    ):
+        one = member.astype(jnp.int32)
+        place = jnp.sum(jnp.where(before, one, 0), axis=0, keepdims=True)
+        start = jnp.sum(jnp.where(tall < cluster, one, 0), axis=0, keepdims=True)
+        count = jnp.sum(jnp.where(tall == cluster, one, 0), axis=0, keepdims=True)
+        out_ref[row : row + 1, :blocks] = place
+        out_ref[row + 1 : row + 2, :cluster_count] = start
+        out_ref[row + 2 : row + 3, :cluster_count] = count
+
+
+def block_tables(ids, table, per_shard):
+    cluster_count = table.shape[1] // per_shard
+    vmem = pl.BlockSpec(memory_space=pltpu.VMEM)
+    return pl.pallas_call(
+        functools.partial(tables_kernel, per_shard, cluster_count),
+        in_specs=[pl.BlockSpec(memory_space=pltpu.SMEM), vmem],
+        out_specs=vmem,
+        out_shape=jax.ShapeDtypeStruct((TABLE_ROWS, 2 * table.shape[1]), jnp.int32),
+        compiler_params=pltpu.CompilerParams(vmem_limit_bytes=VMEM_BYTES),
+        name="block_tables",
+    )(ids, table)
+
+
+KINDS = {
+    "own": (OWN, OWN, 1),
+    "near": (OWN, NEAR, 1),
+    "far_high": (OWN, KEPT, 1),
+    "far_low": (LOW, KEPT, 1),
+    "far_both": (BOTH, SWAPPED, 2),
+}
+
+
+def attend_kernel(kind, per_shard, cluster_count, sizes, ids_ref, tab, *refs):
+    own = kind == "own"
+    kv_row, q_row, _ = KINDS[kind]
+    upper, lower = kind != "far_low", kind in ("far_low", "far_both")
+    merging = kind == "far_low"
+    q_count = 1 if own else 2
+    kv_count = 4 * upper + 3 * lower
+    q_refs = refs[:q_count]
+    kv_refs = refs[q_count : q_count + kv_count]
+    refs = refs[q_count + kv_count :]
+    earlier, refs = (refs[:2], refs[2:]) if merging else ((), refs)
+    out_refs = refs[:2]
+    keys, values, queries, outs, logs, mine = refs[2:]
+    column = ids_ref[0, 0]
+    plane = ids_ref[0, 1]
+    width = keys.shape[2]
+    scale = 1.0 / math.sqrt(width)
+    log_scale = scale / math.log(2.0)
+
+    def body():
+        used = tab[kv_row + 1, cluster_count - 1] + tab[kv_row + 2, cluster_count - 1]
+
+        def bring(shard, key_ref, value_ref):
+            for b in range(per_shard):
+                to = tab[kv_row, shard * per_shard + b]
+                keys[to] = key_ref[b * width : (b + 1) * width, :]
+                values[to] = value_ref[b * width : (b + 1) * width, :]
+
+        if upper:
+            next_shard = 2 * plane + 1 - column
+            kept, first, second, third = kv_refs[:4]
+            bring(2 * plane + column, kept.at[0], kept.at[1])
+
+            @pl.when(plane == 0)
+            def _():
+                bring(next_shard, first, second)
+
+            @pl.when(plane > 0)
+            def _():
+                bring(next_shard, second, third)
+
+        if lower:
+            low_keep, low_first, low_second = kv_refs[-3:]
+            bring(2 * plane - 2 + column, low_keep.at[0], low_keep.at[1])
+            bring(2 * plane - 1 - column, low_first, low_second)
+
+        def blank(i, carry):
+            keys[used + i] = jnp.zeros(keys.shape[1:], keys.dtype)
+            values[used + i] = jnp.zeros(values.shape[1:], values.dtype)
+            return carry
+
+        lax.fori_loop(0, sizes[-1], blank, 0)
+
+        if own:
+            shards = (2 * plane + column, 2 * plane + 1 - column)
+        elif kind == "near":
+            shards = (2 * plane + 2 + column, 2 * plane + 3 - column)
+        elif kind == "far_both":
+            shards = (2 * plane + 3 - column, 2 * plane + 5 - column)
+        else:
+            shards = (2 * plane + 2 + column, 2 * plane + 4 + column)
+
+        def bring_query(shard, q_ref):
+            for b in range(per_shard):
+                to = tab[q_row, shard * per_shard + b]
+                queries[to] = q_ref[b * width : (b + 1) * width, :]
+
+        bring_query(shards[0], q_refs[0])
+        if own:
+
+            @pl.when(plane == 0)
+            def _():
+                bring_query(shards[1], third)
+
+            @pl.when(plane > 0)
+            def _():
+                bring_query(shards[1], first)
+        else:
+            bring_query(shards[1], q_refs[1])
+
+        row = lax.broadcasted_iota(jnp.int32, (width, 2 * width), 0)
+        lane = lax.broadcasted_iota(jnp.int32, (width, 2 * width), 1)
+
+        def cluster(c, carry):
+            begin = tab[kv_row + 1, c]
+            length = tab[kv_row + 2, c]
+            q_begin = tab[q_row + 1, c]
+            q_count = tab[q_row + 2, c]
+
+            def pair(p, carry):
+                at_q = q_begin + 2 * p
+                blocks = jnp.minimum(2 * p + 2, length) if own else length
+
+                def tile(most, surely):
+                    query = queries[pl.ds(at_q, 2)].reshape(2 * width, width)
+                    parts = []
+                    for u in range(most):
+                        part = lax.dot_general(
+                            keys[begin + u],
+                            query,
+                            (((1,), (1,)), ((), ())),
+                            preferred_element_type=jnp.float32,
+                        )
+                        if own:
+                            part = jnp.where(row - lane <= (2 * p - u) * width, part, NEG)
+                        elif u >= surely:
+                            part = jnp.where(u < length, part, NEG)
+                        parts.append(part)
+                    scores = jnp.concatenate(parts, axis=0)
+                    top = jnp.max(scores, axis=0, keepdims=True)
+                    weights = jnp.exp2((scores - top) * log_scale)
+                    total = jnp.sum(weights, axis=0, keepdims=True)
+                    acc = jnp.dot(
+                        jnp.concatenate([values[begin + u] for u in range(most)], axis=1),
+                        weights.astype(jnp.bfloat16),
+                        preferred_element_type=jnp.float32,
+                    )
+                    result = (acc / total).astype(outs.dtype)
+                    log = top * scale + jnp.log(total)
+                    for j in range(2):
+                        outs[at_q + j] = result[:, j * width : (j + 1) * width]
+                        logs[pl.ds(at_q + j, 1), :] = log[:, j * width : (j + 1) * width]
+
+                for k, most in enumerate(sizes):
+                    below = sizes[k - 1] if k else 0
+
+                    @pl.when((blocks > below) & (blocks <= most))
+                    def _(most=most, below=below):
+                        tile(most, below + 1)
+
+                if not own:
+
+                    @pl.when(blocks == 0)
+                    def _():
+                        for j in range(2):
+                            outs[at_q + j] = jnp.zeros((width, width), outs.dtype)
+                            logs[pl.ds(at_q + j, 1), :] = jnp.full((1, width), NEG, jnp.float32)
+
+                return carry
+
+            return lax.fori_loop(0, (q_count + 1) // 2, pair, carry)
+
+        lax.fori_loop(0, cluster_count, cluster, 0)
+        for g, out_ref in enumerate(out_refs):
+            for b in range(per_shard):
+                mine[b : b + 1, :] = logs[pl.ds(tab[q_row, shards[g] * per_shard + b], 1), :]
+            rest = mine[...]
+            if merging:
+                other = log_of(earlier[g], per_shard * width)
+                top = jnp.maximum(rest, other)
+                share, other_share = jnp.exp(rest - top), jnp.exp(other - top)
+                total = share + other_share
+                share, other_share = share / total, other_share / total
+                rest = jnp.maximum(top + jnp.log(total), NEG)
+            for b in range(per_shard):
+                lines = slice(b * width, (b + 1) * width)
+                block = outs[tab[q_row, shards[g] * per_shard + b]]
+                if merging:
+                    block = block.astype(jnp.float32) * share[b : b + 1]
+                    block += earlier[g][lines, :].astype(jnp.float32) * other_share[b : b + 1]
+                out_ref[lines, :] = block.astype(jnp.bfloat16)
+            pieces = []
+            for _ in range(3):
+                piece = rest.astype(jnp.bfloat16).astype(jnp.float32)
+                rest = rest - piece
+                pieces.append(piece)
+            pieces.append(jnp.zeros_like(rest))
+            out_ref[per_shard * width :, :] = jnp.concatenate(pieces, axis=0).astype(jnp.bfloat16)
+
+    if own:
+        body()
+    else:
+
+        @pl.when(lax.rem(plane, 2) == 0 if kind == "near" else plane == 1)
+        def _():
+            body()
+
+
+def log_of(ref, rows):
+    tail = ref[rows:, :].astype(jnp.float32)
+    step = tail.shape[0] // 4
+    return tail[:step] + tail[step : 2 * step] + tail[2 * step : 3 * step]
+
+
+def attend(kind, cluster_count, ids, tables, queries, key_values, earlier=()):
+    rows, width = queries[0].shape
+    per_shard = rows // width
+    most = KINDS[kind][2] * (per_shard // 2)
+    sizes = (most // 2, most)
+    held = KINDS[kind][2] * 2 * per_shard + most
+    smem = pl.BlockSpec(memory_space=pltpu.SMEM)
+    vmem = pl.BlockSpec(memory_space=pltpu.VMEM)
+    out = jax.ShapeDtypeStruct((per_shard * (width + 4), width), jnp.bfloat16)
+    tile = (width, width)
+    return pl.pallas_call(
+        functools.partial(attend_kernel, kind, per_shard, cluster_count, sizes),
+        in_specs=[smem, smem] + [vmem] * (len(queries) + len(key_values) + len(earlier)),
+        out_specs=[vmem] * 2,
+        out_shape=[out] * 2,
+        scratch_shapes=[
+            pltpu.VMEM((held,) + tile, jnp.bfloat16),
+            pltpu.VMEM((held,) + tile, jnp.bfloat16),
+            pltpu.VMEM((2 * per_shard + 2,) + tile, jnp.bfloat16),
+            pltpu.VMEM((2 * per_shard + 2,) + tile, jnp.bfloat16),
+            pltpu.VMEM((2 * per_shard + 8, width), jnp.float32),
+            pltpu.VMEM((per_shard, width), jnp.float32),
+        ],
+        compiler_params=pltpu.CompilerParams(vmem_limit_bytes=VMEM_BYTES),
+    )(ids, tables, *queries, *key_values, *earlier)
+
+
+def combine_kernel(ids_ref, own, near, second, third, out_ref):
+    plane = ids_ref[0, 1]
+    width, rows = out_ref.shape
+    own_log = log_of(own, rows)
+    near_log = jnp.where(lax.rem(plane, 2) == 1, log_of(near, rows), NEG)
+    far_log = jnp.where(plane == 3, log_of(third, rows), log_of(second, rows))
+    far_log = jnp.where(plane > 1, far_log, NEG)
+    top = jnp.maximum(jnp.maximum(own_log, near_log), far_log)
+    own_part = jnp.exp(own_log - top)
+    near_part = jnp.exp(near_log - top)
+    far_part = jnp.exp(far_log - top)
+    share = 1.0 / (own_part + near_part + far_part)
+    own_part, near_part, far_part = own_part * share, near_part * share, far_part * share
+    for b in range(rows // width):
+        lines = slice(b * width, (b + 1) * width)
+        far = jnp.where(plane == 3, third[lines, :], second[lines, :])
+        mixed = (
+            own[lines, :].astype(jnp.float32) * own_part[b : b + 1]
+            + near[lines, :].astype(jnp.float32) * near_part[b : b + 1]
+            + far.astype(jnp.float32) * far_part[b : b + 1]
+        )
+        out_ref[:, lines] = mixed.astype(jnp.bfloat16)
+
+
+def combine(ids, values):
+    size, width = values[-1].shape
+    rows = size // (width + 4) * width
+    vmem = pl.BlockSpec(memory_space=pltpu.VMEM)
+    return pl.pallas_call(
+        combine_kernel,
+        in_specs=[pl.BlockSpec(memory_space=pltpu.SMEM)] + [vmem] * len(values),
+        out_specs=vmem,
+        out_shape=jax.ShapeDtypeStruct((width, rows), jnp.bfloat16),
+        compiler_params=pltpu.CompilerParams(vmem_limit_bytes=VMEM_BYTES),
+        name="combine",
+    )(ids, *values)
+
+
+def project_kernel(other, ids_ref, weight_ref, *refs):
+    group = ids_ref[0, 2]
+    column = ids_ref[0, 0]
+    head = 1 - column if other else column
+    out_ref = refs[-1]
+    features = refs[:4]
+    given = refs[4] if len(refs) == 6 else None
+    depth, rows = features[0].shape
+    lines = [pl.ds(pl.multiple_of(((group ^ j) * 2 + head) * depth, depth), depth) for j in range(4)]
+    chunk = 256
+    for line in range(0, rows, chunk):
+        left = jnp.concatenate([f[:, line : line + chunk] for f in features], axis=0)
+        for col in range(0, out_ref.shape[1], 2 * chunk):
+            cols = slice(col, col + 2 * chunk)
+            right = jnp.concatenate([weight_ref[at, cols] for at in lines], axis=0)
+            acc = lax.dot_general(
+                left, right, (((0,), (0,)), ((), ())), preferred_element_type=jnp.float32
+            )
+            if given is not None:
+                acc = acc + given[line : line + chunk, cols]
+            out_ref[line : line + chunk, cols] = acc.astype(out_ref.dtype)
+
+
+def project(other, ids, weight, features, given):
+    rows = features[0].shape[1]
+    vmem = pl.BlockSpec(memory_space=pltpu.VMEM)
+    given = [] if given is None else [given]
+    last = bool(given)
+    return pl.pallas_call(
+        functools.partial(project_kernel, other),
+        in_specs=[pl.BlockSpec(memory_space=pltpu.SMEM)] + [vmem] * (5 + len(given)),
+        out_specs=vmem,
+        out_shape=jax.ShapeDtypeStruct(
+            (rows, weight.shape[1]), jnp.bfloat16 if last else jnp.float32
+        ),
+        compiler_params=pltpu.CompilerParams(vmem_limit_bytes=VMEM_BYTES),
+        name="project",
+    )(ids, weight, *features, *given)
+
+
+def planes_plan(qkv_heads, clusters, out_weight):
+    seq_count = lax.axis_size("seq")
+    head_count = lax.axis_size("head")
+    shard = lax.axis_index("seq")
+    group = lax.axis_index("head")
+    tok_rows, _, triple = qkv_heads.shape
+    width = triple // 3
+    ids = jnp.stack([shard % 2, shard // 2, group]).astype(jnp.int32).reshape(1, 3)
+
+    swap = [(c, c ^ 1) for c in range(seq_count)]
+
+    def hop(*moves, cross=0):
+        return [(2 * a + x, 2 * b + (x ^ cross)) for a, b in moves for x in range(2)]
+
+    def send(value, pairs):
+        return lax.ppermute(value, "seq", pairs)
+
+    def across(value, flip):
+        return lax.ppermute(value, "head", [(g, g ^ flip) for g in range(head_count)])
+
+    by_head = qkv_heads.transpose(1, 0, 2)
+    q_keep, kv_keep, give1, give2, give3 = split_heads(ids, by_head)
+
+    first = send(give1, swap)
+    low_keep = send(kv_keep, hop((0, 1)))
+    far2_keep = send(q_keep, hop((2, 1)))
+    far3_keep = send(q_keep, hop((3, 1)))
+    second = send(give2, swap)
+    third = send(give3, swap)
+    near_keep = send(q_keep, hop((1, 0), (3, 2)))
+    low_first = send(first, hop((0, 1)))
+    far2_swap = send(first, hop((2, 1)))
+    far3_swap = send(first, hop((3, 1)))
+    low_second = send(second, hop((0, 1)))
+    near_swap = send(first, hop((1, 0), (3, 2)))
+
+    per_shard = tok_rows // width
+    cluster_count = clusters.shape[1] // per_shard
+    tables = block_tables(ids, clusters, per_shard)
+
+    def meet(kind, queries, key_values, earlier=()):
+        return attend(kind, cluster_count, ids, tables, queries, key_values, earlier)
+
+    plane_kv = (kv_keep, first, second, third)
+    low_kv = (low_keep, low_first, low_second)
+    own_keep, own_swap = meet("own", (q_keep,), plane_kv)
+    own_other = send(own_swap, swap)
+    started = meet("far_high", (far2_keep, far3_keep), plane_kv)
+    back2_keep, back3_keep = meet("far_low", (far2_keep, far3_keep), low_kv, started)
+    back3_keep = send(back3_keep, hop((1, 3)))
+    back2_keep = send(back2_keep, hop((1, 2)))
+    down_keep, down_swap = meet("near", (near_keep, near_swap), plane_kv)
+    down_keep = send(down_keep, hop((0, 1), (2, 3)))
+    down_other = send(down_swap, hop((0, 1), (2, 3), cross=1))
+    back2_swap, back3_swap = meet("far_both", (far2_swap, far3_swap), plane_kv + low_kv)
+    back3_other = send(back3_swap, hop((1, 3), cross=1))
+    back2_other = send(back2_swap, hop((1, 2), cross=1))
+    half = head_count // 2
+    out = None
+    for part, values in enumerate(
+        (
+            (own_keep, down_keep, back2_keep, back3_keep),
+            (own_other, down_other, back2_other, back3_other),
+        )
+    ):
+        local = combine(ids, values)
+        over = across(local, half)
+        beside = across(local, 1)
+        over_beside = across(over, 1)
+        out = project(part == 1, ids, out_weight, (local, beside, over, over_beside), out)
+    return out
+
+
 def solution(mesh):
     in_specs = (P("seq", "head", None), P("head", None), P(None, "head"))
     out_specs = P("seq", "head")
-    return jax.shard_map(
-        per_device, mesh=mesh, in_specs=in_specs, out_specs=out_specs, check_vma=False
-    )
+    by_planes = mesh.shape["seq"] == 8 and mesh.shape["head"] == 4
+    plan = planes_plan if by_planes else routed_plan
+
+    return jax.shard_map(plan, mesh=mesh, in_specs=in_specs, out_specs=out_specs, check_vma=False)

time: 198 us -> 98.5 us (0.50)
  the two profiles are of different devices: /device:TPU:0 before, /device:TPU:25 now
where the time goes in v1:
time: 98.5 us; the launch traced here: 98.2 us
  starting transfers between devices  40.6 us (41%)
  waiting for transfers between devices  38.6 us (39%)
  Pallas kernels  16.9 us (17%)
  local copies, waits for them, and re-layouts  1.63 us (2%)
    ppermute x19, waiting for transfers between devices, send(): return lax.ppermute(value, 'seq', pairs)  35.3 us
    ppermute x19, starting transfers between devices, send(): return lax.ppermute(value, 'seq', pairs)  35 us
    pallas_call x5, Pallas kernels, attend(): pl.pallas_call(functools.partial(attend_kernel, kind, per_shard, cluster_...  8.3 us
    ppermute x6, starting transfers between devices, across(): lax.ppermute(value, 'head', [(g, g ^ flip) for g in range(head_count)])  5.59 us
    pallas_call x2, Pallas kernels, project(): pl.pallas_call(functools.partial(project_kernel, other), in_specs=[pl.Blo...  5.06 us
    ppermute x6, waiting for transfers between devices, across(): lax.ppermute(value, 'head', [(g, g ^ flip) for g in range(head_count)])  3.27 us
  transfers between devices with their start and end apart: 25, of which 7 were waited for; matrix products, arithmetic and copies ran while one was open for 0% of the time, Pallas kernels for 13%

profile of v1, /device:TPU:25, one launch (start us, length us, event | category | flops | bytes accessed | tf_op | source)
XLA Modules:
  0.0 98.2 jit_solution(15992554307205021580)
XLA Ops:
  0.0 1.6 %copy.6 = bf16[1024,2,384]{2,0,1:T(8,128)(2,1)S(1)} copy(bf16[1024,2,384]{2,1,0:T(2,128)(2,1)} %param.3) | data formatting | bytes 3145728 | tf_op args[0]
  1.7 1.4 %split_heads.1 = (bf16[1024,128]{1,0:T(8,128)(2,1)S(1)}, bf16[2,1024,128]{2,1,0:T(8,128)(2,1)S(1)}, bf16[1024,128]{1,0:T(8,128)(2,1)S(1)}, bf16[1024,128]{1,0:T(8,128)(2,1)S(1)}, bf16[1024,128]{1,0:T(8,128)(2,1)S(1)}) custom-call(s32[1,3]{1,0:T(1,128)S(1)} %add_bitcast_fusion.ids_ref, bf16[2,1024,384]{2,1,0:T(8,128)(2,1)S(1)} %bitcast.8), custom_call_target="tpu_custom_call" | custom-call | tf_op jit(solution)/shard_map/split_heads/pallas_call | solution.py:180
  3.1 1.3 %collective-permute-start = (bf16[1024,128]{1,0:T(8,128)(2,1)S(1)}, bf16[1024,128]{1,0:T(8,128)(2,1)S(1)}, u32[]{:S(2)}, u32[]{:S(2)}) collective-permute-start(bf16[1024,128]{1,0:T(8,128)(2,1)S(1)} %get-tuple-element.22), channel_id=1, source_target_pairs={{0,4},{4,0},{8,12},{12,8},{16,20},{20,16},{24,28},{28,24},{1,5},{5... | collective-permute-start | bytes 786440 | tf_op jit(solution)/shard_map/ppermute | solution.py:558
  4.6 1.2 %collective-permute-start.2 = (bf16[1024,128]{1,0:T(8,128)(2,1)S(1)}, bf16[1024,128]{1,0:T(8,128)(2,1)S(1)}, u32[]{:S(2)}, u32[]{:S(2)}) collective-permute-start(bf16[1024,128]{1,0:T(8,128)(2,1)S(1)} %get-tuple-element.24), channel_id=1, source_target_pairs={{0,4},{4,0},{8,12},{12,8},{16,20},{20,16},{24,28},{28,24},{1,5},{5... | collective-permute-start | bytes 786440 | tf_op jit(solution)/shard_map/ppermute | solution.py:558
  5.9 2.0 %collective-permute-start.19 = (bf16[1024,128]{1,0:T(8,128)(2,1)S(1)}, bf16[1024,128]{1,0:T(8,128)(2,1)S(1)}, u32[]{:S(2)}, u32[]{:S(2)}) collective-permute-start(bf16[1024,128]{1,0:T(8,128)(2,1)S(1)} %get-tuple-element.20.refs_0_), channel_id=1, source_target_pairs={{24,8},{28,12},{25,9},{29,13},{26,10},{30,14},{27,11},{31,15}} | collective-permute-start | bytes 786440 | tf_op jit(solution)/shard_map/ppermute | solution.py:558
  8.5 1.9 %collective-permute-done.refs_2_.refs_3_ = bf16[1024,128]{1,0:T(8,128)(2,1)S(1)} collective-permute-done((bf16[1024,128]{1,0:T(8,128)(2,1)S(1)}, bf16[1024,128]{1,0:T(8,128)(2,1)S(1)}, u32[]{:S(2)}, u32[]{:S(2)}) %collective-permute-start) | collective-permute-done | bytes 262176 | tf_op jit(solution)/shard_map/ppermute | solution.py:558
  11.1 4.9 %collective-permute-done.1.refs_3_.refs_4_ = bf16[1024,128]{1,0:T(8,128)(2,1)S(1)} collective-permute-done((bf16[1024,128]{1,0:T(8,128)(2,1)S(1)}, bf16[1024,128]{1,0:T(8,128)(2,1)S(1)}, u32[]{:S(2)}, u32[]{:S(2)}) %collective-permute-start.1) | collective-permute-done | bytes 262176 | tf_op jit(solution)/shard_map/ppermute | solution.py:558
  16.0 2.1 %collective-permute-start.4 = (bf16[1024,128]{1,0:T(8,128)(2,1)S(1)}, bf16[1024,128]{1,0:T(8,128)(2,1)S(1)}, u32[]{:S(2)}, u32[]{:S(2)}) collective-permute-start(bf16[1024,128]{1,0:T(8,128)(2,1)S(1)} %get-tuple-element.20.refs_0_), channel_id=1, source_target_pairs={{8,0},{12,4},{24,16},{28,20},{9,1},{13,5},{25,17},{29,21},{10,2},{... | collective-permute-start | bytes 786440 | tf_op jit(solution)/shard_map/ppermute | solution.py:558
  18.1 3.5 %collective-permute-done.2.refs_4_.refs_5_ = bf16[1024,128]{1,0:T(8,128)(2,1)S(1)} collective-permute-done((bf16[1024,128]{1,0:T(8,128)(2,1)S(1)}, bf16[1024,128]{1,0:T(8,128)(2,1)S(1)}, u32[]{:S(2)}, u32[]{:S(2)}) %collective-permute-start.2) | collective-permute-done | bytes 262176 | tf_op jit(solution)/shard_map/ppermute | solution.py:558
  21.6 2.1 %collective-permute-start.5 = (bf16[1024,128]{1,0:T(8,128)(2,1)S(1)}, bf16[1024,128]{1,0:T(8,128)(2,1)S(1)}, u32[]{:S(2)}, u32[]{:S(2)}) collective-permute-start(bf16[1024,128]{1,0:T(8,128)(2,1)S(1)} %collective-permute-done.refs_2_.refs_3_), channel_id=1, source_target_pairs={{8,0},{12,4},{24,16},{28,20},{9,1},{13,5},{25,17},{29,21},{10,2},{... | collective-permute-start | bytes 786440 | tf_op jit(solution)/shard_map/ppermute | solution.py:558
  25.1 0.7 block_tables.1.tab
  25.8 0.7 shard_map.40
  26.6 1.8 %collective-permute-done.5.refs_1_ = bf16[1024,128]{1,0:T(8,128)(2,1)S(1)} collective-permute-done((bf16[1024,128]{1,0:T(8,128)(2,1)S(1)}, bf16[1024,128]{1,0:T(8,128)(2,1)S(1)}, u32[]{:S(2)}, u32[]{:S(2)}) %collective-permute-start.5) | collective-permute-done | bytes 262176 | tf_op jit(solution)/shard_map/ppermute | solution.py:558
  28.4 0.7 shard_map.38
  29.2 1.3 %collective-permute-start.17 = (bf16[1056,128]{1,0:T(8,128)(2,1)S(1)}, bf16[1056,128]{1,0:T(8,128)(2,1)S(1)}, u32[]{:S(2)}, u32[]{:S(2)}) collective-permute-start(bf16[1056,128]{1,0:T(8,128)(2,1)S(1)} %get-tuple-element.30), channel_id=1, source_target_pairs={{0,8},{4,12},{16,24},{20,28},{1,9},{5,13},{17,25},{21,29},{2,10},{... | collective-permute-start | bytes 811016 | tf_op jit(solution)/shard_map/ppermute | solution.py:558
  30.5 0.8 shard_map.41
  31.9 14.7 %collective-permute-start.8 = (bf16[1024,128]{1,0:T(8,128)(2,1)S(1)}, bf16[1024,128]{1,0:T(8,128)(2,1)S(1)}, u32[]{:S(2)}, u32[]{:S(2)}) collective-permute-start(bf16[1024,128]{1,0:T(8,128)(2,1)S(1)} %collective-permute-done.refs_2_.refs_3_), channel_id=1, source_target_pairs={{24,8},{28,12},{25,9},{29,13},{26,10},{30,14},{27,11},{31,15}} | collective-permute-start | bytes 786440 | tf_op jit(solution)/shard_map/ppermute | solution.py:558
  47.3 5.3 %shard_map.37 = (bf16[1056,128]{1,0:T(8,128)(2,1)S(1)}, bf16[1056,128]{1,0:T(8,128)(2,1)S(1)}) custom-call(s32[1,3]{1,0:T(1,128)S(1)} %add_bitcast_fusion.ids_ref, s32[24,128]{1,0:T(8,128)S(1)} %block_tables.1.tab, bf16[1024,128]{1,0:T(8,128)(2,1)S(1)} %get-tuple-element.20.refs_0_, bf16[2,1024,128]{2,1,0:T(8,128)(2,1)S(1)} %get-tuple-element.21.refs_1_.refs_2_, ...), custom_call_target="tpu_custom_call" | custom-call | tf_op jit(solution)/shard_map/pallas_call | solution.py:448
  52.6 1.4 %collective-permute-start.3 = (bf16[1056,128]{1,0:T(8,128)(2,1)S(1)}, bf16[1056,128]{1,0:T(8,128)(2,1)S(1)}, u32[]{:S(2)}, u32[]{:S(2)}) collective-permute-start(bf16[1056,128]{1,0:T(8,128)(2,1)S(1)} %get-tuple-element.25), channel_id=1, source_target_pairs={{0,4},{4,0},{8,12},{12,8},{16,20},{20,16},{24,28},{28,24},{1,5},{5... | collective-permute-start | bytes 811016 | tf_op jit(solution)/shard_map/ppermute | solution.py:558
  54.0 1.3 %collective-permute-start.6 = (bf16[1056,128]{1,0:T(8,128)(2,1)S(1)}, bf16[1056,128]{1,0:T(8,128)(2,1)S(1)}, u32[]{:S(2)}, u32[]{:S(2)}) collective-permute-start(bf16[1056,128]{1,0:T(8,128)(2,1)S(1)} %get-tuple-element.26), channel_id=1, source_target_pairs={{0,12},{4,8},{16,28},{20,24},{1,13},{5,9},{17,29},{21,25},{2,14},{... | collective-permute-start | bytes 811016 | tf_op jit(solution)/shard_map/ppermute | solution.py:558
  55.3 1.4 %collective-permute-start.21 = (bf16[1056,128]{1,0:T(8,128)(2,1)S(1)}, bf16[1056,128]{1,0:T(8,128)(2,1)S(1)}, u32[]{:S(2)}, u32[]{:S(2)}) collective-permute-start(bf16[1056,128]{1,0:T(8,128)(2,1)S(1)} %get-tuple-element.34), channel_id=1, source_target_pairs={{8,24},{12,28},{9,25},{13,29},{10,26},{14,30},{11,27},{15,31}} | collective-permute-start | bytes 811016 | tf_op jit(solution)/shard_map/ppermute | solution.py:558
  56.8 0.8 shard_map.39
  58.2 1.3 %collective-permute-start.13 = (bf16[1056,128]{1,0:T(8,128)(2,1)S(1)}, bf16[1056,128]{1,0:T(8,128)(2,1)S(1)}, u32[]{:S(2)}, u32[]{:S(2)}) collective-permute-start(bf16[1056,128]{1,0:T(8,128)(2,1)S(1)} %get-tuple-element.28), channel_id=1, source_target_pairs={{8,28},{12,24},{9,29},{13,25},{10,30},{14,26},{11,31},{15,27}} | collective-permute-start | bytes 811016 | tf_op jit(solution)/shard_map/ppermute | solution.py:558
  59.5 7.1 %collective-permute-done.21.third = bf16[1056,128]{1,0:T(8,128)(2,1)S(1)} collective-permute-done((bf16[1056,128]{1,0:T(8,128)(2,1)S(1)}, bf16[1056,128]{1,0:T(8,128)(2,1)S(1)}, u32[]{:S(2)}, u32[]{:S(2)}) %collective-permute-start.21) | collective-permute-done | bytes 270368 | tf_op jit(solution)/shard_map/ppermute | solution.py:558
  66.7 0.7 combine.3.refs_0_
  67.5 16.0 %collective-permute-done.13.third = bf16[1056,128]{1,0:T(8,128)(2,1)S(1)} collective-permute-done((bf16[1056,128]{1,0:T(8,128)(2,1)S(1)}, bf16[1056,128]{1,0:T(8,128)(2,1)S(1)}, u32[]{:S(2)}, u32[]{:S(2)}) %collective-permute-start.13) | collective-permute-done | bytes 270368 | tf_op jit(solution)/shard_map/ppermute | solution.py:558
  83.5 0.7 combine.2.refs_0_
  84.3 2.1 %collective-permute-start.22 = (bf16[128,1024]{1,0:T(8,128)(2,1)S(1)}, bf16[128,1024]{1,0:T(8,128)(2,1)S(1)}, u32[]{:S(2)}, u32[]{:S(2)}) collective-permute-start(bf16[128,1024]{1,0:T(8,128)(2,1)S(1)} %combine.3.refs_0_), channel_id=1, source_target_pairs={{0,1},{1,0},{2,3},{3,2},{4,5},{5,4},{6,7},{7,6},{8,9},{9,8},{10,11... | collective-permute-start | bytes 786440 | tf_op jit(solution)/shard_map/ppermute | solution.py:561
  86.9 3.3 %collective-permute-done.15.refs_2_ = bf16[128,1024]{1,0:T(8,128)(2,1)S(1)} collective-permute-done((bf16[128,1024]{1,0:T(8,128)(2,1)S(1)}, bf16[128,1024]{1,0:T(8,128)(2,1)S(1)}, u32[]{:S(2)}, u32[]{:S(2)}) %collective-permute-start.15) | collective-permute-done | bytes 262176 | tf_op jit(solution)/shard_map/ppermute | solution.py:561
  90.2 2.9 %collective-permute-start.16 = (bf16[128,1024]{1,0:T(8,128)(2,1)S(1)}, bf16[128,1024]{1,0:T(8,128)(2,1)S(1)}, u32[]{:S(2)}, u32[]{:S(2)}) collective-permute-start(bf16[128,1024]{1,0:T(8,128)(2,1)S(1)} %collective-permute-done.15.refs_2_), channel_id=1, source_target_pairs={{0,1},{1,0},{2,3},{3,2},{4,5},{5,4},{6,7},{7,6},{8,9},{9,8},{10,11... | collective-permute-start | bytes 786440 | tf_op jit(solution)/shard_map/ppermute | solution.py:561
  93.1 1.8 %project.2.refs_4_ = f32[1024,1024]{1,0:T(8,128)S(1)} custom-call(s32[1,3]{1,0:T(1,128)S(1)} %add_bitcast_fusion.ids_ref, bf16[1024,1024]{1,0:T(8,128)(2,1)S(1)} %copy-done, bf16[128,1024]{1,0:T(8,128)(2,1)S(1)} %combine.3.refs_0_, bf16[128,1024]{1,0:T(8,128)(2,1)S(1)} %collective-permute-done.22.refs_1_, ...), custom_call_target="tpu_custom_call" | custom-call | tf_op jit(solution)/shard_map/project/pallas_call | solution.py:531
  94.9 3.2 %project.3 = bf16[1024,1024]{1,0:T(8,128)(2,1)} custom-call(s32[1,3]{1,0:T(1,128)S(1)} %add_bitcast_fusion.ids_ref, bf16[1024,1024]{1,0:T(8,128)(2,1)S(1)} %copy-done, bf16[128,1024]{1,0:T(8,128)(2,1)S(1)} %combine.2.refs_0_, bf16[128,1024]{1,0:T(8,128)(2,1)S(1)} %collective-permute-done.14.refs_1_, bf16[128,1024]{1,0:T(8,128)(2,1)S(1)} %collective-permute-done.15.refs_2_, ...), custom_call_target="tpu_custom_call" | custom-call | tf_op jit(solution)/shard_map/project/pallas_call | solution.py:531
  (35 shorter events, 5.8 us)
Async XLA Ops:
  0.0 25.1 %copy-start.1 = (s32[2,64]{1,0:T(2,128)S(1)}, s32[2,64]{1,0:T(2,128)}, u32[]{:S(2)}) copy-start(s32[2,64]{1,0:T(2,128)} %table_ref.1) | copy-start | bytes 1540
  3.1 7.3 %collective-permute-start = (bf16[1024,128]{1,0:T(8,128)(2,1)S(1)}, bf16[1024,128]{1,0:T(8,128)(2,1)S(1)}, u32[]{:S(2)}, u32[]{:S(2)}) collective-permute-start(bf16[1024,128]{1,0:T(8,128)(2,1)S(1)} %get-tuple-element.22), channel_id=1, source_target_pairs={{0,4},{4,0},{8,12},{12,8},{16,20},{20,16},{24,28},{28,24},{1,5},{5... | collective-permute-start | bytes 786440 | tf_op jit(solution)/shard_map/ppermute | solution.py:558
  4.4 11.6 %collective-permute-start.1 = (bf16[1024,128]{1,0:T(8,128)(2,1)S(1)}, bf16[1024,128]{1,0:T(8,128)(2,1)S(1)}, u32[]{:S(2)}, u32[]{:S(2)}) collective-permute-start(bf16[1024,128]{1,0:T(8,128)(2,1)S(1)} %get-tuple-element.23), channel_id=1, source_target_pairs={{0,4},{4,0},{8,12},{12,8},{16,20},{20,16},{24,28},{28,24},{1,5},{5... | collective-permute-start | bytes 786440 | tf_op jit(solution)/shard_map/ppermute | solution.py:558
  4.6 17.0 %collective-permute-start.2 = (bf16[1024,128]{1,0:T(8,128)(2,1)S(1)}, bf16[1024,128]{1,0:T(8,128)(2,1)S(1)}, u32[]{:S(2)}, u32[]{:S(2)}) collective-permute-start(bf16[1024,128]{1,0:T(8,128)(2,1)S(1)} %get-tuple-element.24), channel_id=1, source_target_pairs={{0,4},{4,0},{8,12},{12,8},{16,20},{20,16},{24,28},{28,24},{1,5},{5... | collective-permute-start | bytes 786440 | tf_op jit(solution)/shard_map/ppermute | solution.py:558
  5.9 17.8 %collective-permute-start.19 = (bf16[1024,128]{1,0:T(8,128)(2,1)S(1)}, bf16[1024,128]{1,0:T(8,128)(2,1)S(1)}, u32[]{:S(2)}, u32[]{:S(2)}) collective-permute-start(bf16[1024,128]{1,0:T(8,128)(2,1)S(1)} %get-tuple-element.20.refs_0_), channel_id=1, source_target_pairs={{24,8},{28,12},{25,9},{29,13},{26,10},{30,14},{27,11},{31,15}} | collective-permute-start | bytes 786440 | tf_op jit(solution)/shard_map/ppermute | solution.py:558
  7.8 16.6 %collective-permute-start.18 = (bf16[1024,128]{1,0:T(8,128)(2,1)S(1)}, bf16[1024,128]{1,0:T(8,128)(2,1)S(1)}, u32[]{:S(2)}, u32[]{:S(2)}) collective-permute-start(bf16[1024,128]{1,0:T(8,128)(2,1)S(1)} %get-tuple-element.20.refs_0_), channel_id=1, source_target_pairs={{16,8},{20,12},{17,9},{21,13},{18,10},{22,14},{19,11},{23,15}} | collective-permute-start | bytes 786440 | tf_op jit(solution)/shard_map/ppermute | solution.py:558
  10.4 20.1 %collective-permute-start.9 = (bf16[2,1024,128]{2,1,0:T(8,128)(2,1)S(1)}, bf16[2,1024,128]{2,1,0:T(8,128)(2,1)S(1)}, u32[]{:S(2)}, u32[]{:S(2)}) collective-permute-start(bf16[2,1024,128]{2,1,0:T(8,128)(2,1)S(1)} %get-tuple-element.21.refs_1_.refs_2_), channel_id=1, source_target_pairs={{0,8},{4,12},{1,9},{5,13},{2,10},{6,14},{3,11},{7,15}} | collective-permute-start | bytes 1572872 | tf_op jit(solution)/shard_map/ppermute | solution.py:558
  16.0 10.6 %collective-permute-start.4 = (bf16[1024,128]{1,0:T(8,128)(2,1)S(1)}, bf16[1024,128]{1,0:T(8,128)(2,1)S(1)}, u32[]{:S(2)}, u32[]{:S(2)}) collective-permute-start(bf16[1024,128]{1,0:T(8,128)(2,1)S(1)} %get-tuple-element.20.refs_0_), channel_id=1, source_target_pairs={{8,0},{12,4},{24,16},{28,20},{9,1},{13,5},{25,17},{29,21},{10,2},{... | collective-permute-start | bytes 786440 | tf_op jit(solution)/shard_map/ppermute | solution.py:558
  21.6 6.8 %collective-permute-start.5 = (bf16[1024,128]{1,0:T(8,128)(2,1)S(1)}, bf16[1024,128]{1,0:T(8,128)(2,1)S(1)}, u32[]{:S(2)}, u32[]{:S(2)}) collective-permute-start(bf16[1024,128]{1,0:T(8,128)(2,1)S(1)} %collective-permute-done.refs_2_.refs_3_), channel_id=1, source_target_pairs={{8,0},{12,4},{24,16},{28,20},{9,1},{13,5},{25,17},{29,21},{10,2},{... | collective-permute-start | bytes 786440 | tf_op jit(solution)/shard_map/ppermute | solution.py:558
  23.7 6.8 %collective-permute-start.10 = (bf16[1024,128]{1,0:T(8,128)(2,1)S(1)}, bf16[1024,128]{1,0:T(8,128)(2,1)S(1)}, u32[]{:S(2)}, u32[]{:S(2)}) collective-permute-start(bf16[1024,128]{1,0:T(8,128)(2,1)S(1)} %collective-permute-done.refs_2_.refs_3_), channel_id=1, source_target_pairs={{0,8},{4,12},{1,9},{5,13},{2,10},{6,14},{3,11},{7,15}} | collective-permute-start | bytes 786440 | tf_op jit(solution)/shard_map/ppermute | solution.py:558
  24.4 6.1 %collective-permute-start.11 = (bf16[1024,128]{1,0:T(8,128)(2,1)S(1)}, bf16[1024,128]{1,0:T(8,128)(2,1)S(1)}, u32[]{:S(2)}, u32[]{:S(2)}) collective-permute-start(bf16[1024,128]{1,0:T(8,128)(2,1)S(1)} %collective-permute-done.1.refs_3_.refs_4_), channel_id=1, source_target_pairs={{0,8},{4,12},{1,9},{5,13},{2,10},{6,14},{3,11},{7,15}} | collective-permute-start | bytes 786440 | tf_op jit(solution)/shard_map/ppermute | solution.py:558
  29.2 28.4 %collective-permute-start.17 = (bf16[1056,128]{1,0:T(8,128)(2,1)S(1)}, bf16[1056,128]{1,0:T(8,128)(2,1)S(1)}, u32[]{:S(2)}, u32[]{:S(2)}) collective-permute-start(bf16[1056,128]{1,0:T(8,128)(2,1)S(1)} %get-tuple-element.30), channel_id=1, source_target_pairs={{0,8},{4,12},{16,24},{20,28},{1,9},{5,13},{17,25},{21,29},{2,10},{... | collective-permute-start | bytes 811016 | tf_op jit(solution)/shard_map/ppermute | solution.py:558
  31.3 27.0 %collective-permute-start.20 = (bf16[1056,128]{1,0:T(8,128)(2,1)S(1)}, bf16[1056,128]{1,0:T(8,128)(2,1)S(1)}, u32[]{:S(2)}, u32[]{:S(2)}) collective-permute-start(bf16[1056,128]{1,0:T(8,128)(2,1)S(1)} %get-tuple-element.33), channel_id=1, source_target_pairs={{8,16},{12,20},{9,17},{13,21},{10,18},{14,22},{11,19},{15,23}} | collective-permute-start | bytes 811016 | tf_op jit(solution)/shard_map/ppermute | solution.py:558
  31.9 22.1 %collective-permute-start.8 = (bf16[1024,128]{1,0:T(8,128)(2,1)S(1)}, bf16[1024,128]{1,0:T(8,128)(2,1)S(1)}, u32[]{:S(2)}, u32[]{:S(2)}) collective-permute-start(bf16[1024,128]{1,0:T(8,128)(2,1)S(1)} %collective-permute-done.refs_2_.refs_3_), channel_id=1, source_target_pairs={{24,8},{28,12},{25,9},{29,13},{26,10},{30,14},{27,11},{31,15}} | collective-permute-start | bytes 786440 | tf_op jit(solution)/shard_map/ppermute | solution.py:558
  46.7 8.7 %collective-permute-start.7 = (bf16[1024,128]{1,0:T(8,128)(2,1)S(1)}, bf16[1024,128]{1,0:T(8,128)(2,1)S(1)}, u32[]{:S(2)}, u32[]{:S(2)}) collective-permute-start(bf16[1024,128]{1,0:T(8,128)(2,1)S(1)} %collective-permute-done.refs_2_.refs_3_), channel_id=1, source_target_pairs={{16,8},{20,12},{17,9},{21,13},{18,10},{22,14},{19,11},{23,15}} | collective-permute-start | bytes 786440 | tf_op jit(solution)/shard_map/ppermute | solution.py:558
  52.6 14.8 %collective-permute-start.3 = (bf16[1056,128]{1,0:T(8,128)(2,1)S(1)}, bf16[1056,128]{1,0:T(8,128)(2,1)S(1)}, u32[]{:S(2)}, u32[]{:S(2)}) collective-permute-start(bf16[1056,128]{1,0:T(8,128)(2,1)S(1)} %get-tuple-element.25), channel_id=1, source_target_pairs={{0,4},{4,0},{8,12},{12,8},{16,20},{20,16},{24,28},{28,24},{1,5},{5... | collective-permute-start | bytes 811016 | tf_op jit(solution)/shard_map/ppermute | solution.py:558
  54.0 13.5 %collective-permute-start.6 = (bf16[1056,128]{1,0:T(8,128)(2,1)S(1)}, bf16[1056,128]{1,0:T(8,128)(2,1)S(1)}, u32[]{:S(2)}, u32[]{:S(2)}) collective-permute-start(bf16[1056,128]{1,0:T(8,128)(2,1)S(1)} %get-tuple-element.26), channel_id=1, source_target_pairs={{0,12},{4,8},{16,28},{20,24},{1,13},{5,9},{17,29},{21,25},{2,14},{... | collective-permute-start | bytes 811016 | tf_op jit(solution)/shard_map/ppermute | solution.py:558
  55.3 37.7 %copy-start = (bf16[1024,1024]{1,0:T(8,128)(2,1)S(1)}, bf16[1024,1024]{1,0:T(8,128)(2,1)}, u32[]{:S(2)}) copy-start(bf16[1024,1024]{1,0:T(8,128)(2,1)} %weight_ref.3) | copy-start | bytes 6291460
  55.3 11.3 %collective-permute-start.21 = (bf16[1056,128]{1,0:T(8,128)(2,1)S(1)}, bf16[1056,128]{1,0:T(8,128)(2,1)S(1)}, u32[]{:S(2)}, u32[]{:S(2)}) collective-permute-start(bf16[1056,128]{1,0:T(8,128)(2,1)S(1)} %get-tuple-element.34), channel_id=1, source_target_pairs={{8,24},{12,28},{9,25},{13,29},{10,26},{14,30},{11,27},{15,31}} | collective-permute-start | bytes 811016 | tf_op jit(solution)/shard_map/ppermute | solution.py:558
  57.6 10.0 %collective-permute-start.12 = (bf16[1056,128]{1,0:T(8,128)(2,1)S(1)}, bf16[1056,128]{1,0:T(8,128)(2,1)S(1)}, u32[]{:S(2)}, u32[]{:S(2)}) collective-permute-start(bf16[1056,128]{1,0:T(8,128)(2,1)S(1)} %get-tuple-element.27), channel_id=1, source_target_pairs={{8,20},{12,16},{9,21},{13,17},{10,22},{14,18},{11,23},{15,19}} | collective-permute-start | bytes 811016 | tf_op jit(solution)/shard_map/ppermute | solution.py:558
  58.2 25.3 %collective-permute-start.13 = (bf16[1056,128]{1,0:T(8,128)(2,1)S(1)}, bf16[1056,128]{1,0:T(8,128)(2,1)S(1)}, u32[]{:S(2)}, u32[]{:S(2)}) collective-permute-start(bf16[1056,128]{1,0:T(8,128)(2,1)S(1)} %get-tuple-element.28), channel_id=1, source_target_pairs={{8,28},{12,24},{9,29},{13,25},{10,30},{14,26},{11,31},{15,27}} | collective-permute-start | bytes 811016 | tf_op jit(solution)/shard_map/ppermute | solution.py:558
  67.4 19.0 %collective-permute-start.23 = (bf16[128,1024]{1,0:T(8,128)(2,1)S(1)}, bf16[128,1024]{1,0:T(8,128)(2,1)S(1)}, u32[]{:S(2)}, u32[]{:S(2)}) collective-permute-start(bf16[128,1024]{1,0:T(8,128)(2,1)S(1)} %combine.3.refs_0_), channel_id=1, source_target_pairs={{0,2},{1,3},{2,0},{3,1},{4,6},{5,7},{6,4},{7,5},{8,10},{9,11},{10,... | collective-permute-start | bytes 786440 | tf_op jit(solution)/shard_map/ppermute | solution.py:561
  84.3 5.9 %collective-permute-start.15 = (bf16[128,1024]{1,0:T(8,128)(2,1)S(1)}, bf16[128,1024]{1,0:T(8,128)(2,1)S(1)}, u32[]{:S(2)}, u32[]{:S(2)}) collective-permute-start(bf16[128,1024]{1,0:T(8,128)(2,1)S(1)} %combine.2.refs_0_), channel_id=1, source_target_pairs={{0,2},{1,3},{2,0},{3,1},{4,6},{5,7},{6,4},{7,5},{8,10},{9,11},{10,... | collective-permute-start | bytes 786440 | tf_op jit(solution)/shard_map/ppermute | solution.py:561
  84.3 8.7 %collective-permute-start.22 = (bf16[128,1024]{1,0:T(8,128)(2,1)S(1)}, bf16[128,1024]{1,0:T(8,128)(2,1)S(1)}, u32[]{:S(2)}, u32[]{:S(2)}) collective-permute-start(bf16[128,1024]{1,0:T(8,128)(2,1)S(1)} %combine.3.refs_0_), channel_id=1, source_target_pairs={{0,1},{1,0},{2,3},{3,2},{4,5},{5,4},{6,7},{7,6},{8,9},{9,8},{10,11... | collective-permute-start | bytes 786440 | tf_op jit(solution)/shard_map/ppermute | solution.py:561
  86.4 6.6 %collective-permute-start.24 = (bf16[128,1024]{1,0:T(8,128)(2,1)S(1)}, bf16[128,1024]{1,0:T(8,128)(2,1)S(1)}, u32[]{:S(2)}, u32[]{:S(2)}) collective-permute-start(bf16[128,1024]{1,0:T(8,128)(2,1)S(1)} %collective-permute-done.23.refs_2_), channel_id=1, source_target_pairs={{0,1},{1,0},{2,3},{3,2},{4,5},{5,4},{6,7},{7,6},{8,9},{9,8},{10,11... | collective-permute-start | bytes 786440 | tf_op jit(solution)/shard_map/ppermute | solution.py:561
  86.5 8.4 %collective-permute-start.14 = (bf16[128,1024]{1,0:T(8,128)(2,1)S(1)}, bf16[128,1024]{1,0:T(8,128)(2,1)S(1)}, u32[]{:S(2)}, u32[]{:S(2)}) collective-permute-start(bf16[128,1024]{1,0:T(8,128)(2,1)S(1)} %combine.2.refs_0_), channel_id=1, source_target_pairs={{0,1},{1,0},{2,3},{3,2},{4,5},{5,4},{6,7},{7,6},{8,9},{9,8},{10,11... | collective-permute-start | bytes 786440 | tf_op jit(solution)/shard_map/ppermute | solution.py:561
  90.2 4.7 %collective-permute-start.16 = (bf16[128,1024]{1,0:T(8,128)(2,1)S(1)}, bf16[128,1024]{1,0:T(8,128)(2,1)S(1)}, u32[]{:S(2)}, u32[]{:S(2)}) collective-permute-start(bf16[128,1024]{1,0:T(8,128)(2,1)S(1)} %collective-permute-done.15.refs_2_), channel_id=1, source_target_pairs={{0,1},{1,0},{2,3},{3,2},{4,5},{5,4},{6,7},{7,6},{8,9},{9,8},{10,11... | collective-permute-start | bytes 786440 | tf_op jit(solution)/shard_map/ppermute | solution.py:561

commit v2 on v1

--- a/solution.py
+++ b/solution.py
@@ -191,7 +191,7 @@
     )(ids, by_head)
 
 
-OWN, LOW, BOTH, NEAR, KEPT, SWAPPED = range(0, 18, 3)
+OWN, UPPER, REST, BOTH, NEAR, KEPT, SWAPPED = range(0, 21, 3)
 TABLE_ROWS = 24
 
 
@@ -214,7 +214,8 @@
     high = (in_plane == 2) | (in_plane == 3)
     for row, member in (
         (OWN, in_plane == plane),
-        (LOW, in_plane == plane - 1),
+        (UPPER, (in_plane == plane) | ((in_plane == plane - 1) & (side == column))),
+        (REST, (in_plane == plane - 1) & (side != column)),
         (BOTH, (in_plane == plane) | (in_plane == plane - 1)),
         (NEAR, in_plane == plane + 1),
         (KEPT, high & (side == column)),
@@ -243,21 +244,23 @@
 
 
 KINDS = {
-    "own": (OWN, OWN, 1),
-    "near": (OWN, NEAR, 1),
-    "far_high": (OWN, KEPT, 1),
-    "far_low": (LOW, KEPT, 1),
-    "far_both": (BOTH, SWAPPED, 2),
+    "own": (OWN, OWN, 4, (1, 2, 4)),
+    "near": (OWN, NEAR, 2, (1, 2)),
+    "far_high": (UPPER, KEPT, 3, (1, 2, 3)),
+    "far_low": (REST, KEPT, 1, (1,)),
+    "far_both": (BOTH, SWAPPED, 4, (2, 4)),
 }
 
 
 def attend_kernel(kind, per_shard, cluster_count, sizes, ids_ref, tab, *refs):
     own = kind == "own"
-    kv_row, q_row, _ = KINDS[kind]
-    upper, lower = kind != "far_low", kind in ("far_low", "far_both")
+    kv_row, q_row = KINDS[kind][:2]
+    plane_keys = kind != "far_low"
+    low_kept = kind in ("own", "far_high", "far_both")
+    low_rest = kind in ("own", "far_low", "far_both")
     merging = kind == "far_low"
     q_count = 1 if own else 2
-    kv_count = 4 * upper + 3 * lower
+    kv_count = 4 * plane_keys + low_kept + 2 * low_rest
     q_refs = refs[:q_count]
     kv_refs = refs[q_count : q_count + kv_count]
     refs = refs[q_count + kv_count :]
@@ -269,6 +272,8 @@
     width = keys.shape[2]
     scale = 1.0 / math.sqrt(width)
     log_scale = scale / math.log(2.0)
+    if own:
+        kv_row = jnp.where(plane == 1, BOTH, OWN)
 
     def body():
         used = tab[kv_row + 1, cluster_count - 1] + tab[kv_row + 2, cluster_count - 1]
@@ -279,7 +284,7 @@
                 keys[to] = key_ref[b * width : (b + 1) * width, :]
                 values[to] = value_ref[b * width : (b + 1) * width, :]
 
-        if upper:
+        if plane_keys:
             next_shard = 2 * plane + 1 - column
             kept, first, second, third = kv_refs[:4]
             bring(2 * plane + column, kept.at[0], kept.at[1])
@@ -292,10 +297,17 @@
             def _():
                 bring(next_shard, second, third)
 
-        if lower:
-            low_keep, low_first, low_second = kv_refs[-3:]
-            bring(2 * plane - 2 + column, low_keep.at[0], low_keep.at[1])
-            bring(2 * plane - 1 - column, low_first, low_second)
+        def bring_low():
+            if low_kept:
+                low_keep = kv_refs[4]
+                bring(2 * plane - 2 + column, low_keep.at[0], low_keep.at[1])
+            if low_rest:
+                bring(2 * plane - 1 - column, kv_refs[-2], kv_refs[-1])
+
+        if own:
+            pl.when(plane == 1)(bring_low)
+        else:
+            bring_low()
 
         def blank(i, carry):
             keys[used + i] = jnp.zeros(keys.shape[1:], keys.dtype)
@@ -342,7 +354,8 @@
 
             def pair(p, carry):
                 at_q = q_begin + 2 * p
-                blocks = jnp.minimum(2 * p + 2, length) if own else length
+                turn = length - q_count + 2 * p
+                blocks = jnp.minimum(turn + 2, length) if own else length
 
                 def tile(most, surely):
                     query = queries[pl.ds(at_q, 2)].reshape(2 * width, width)
@@ -355,7 +368,7 @@
                             preferred_element_type=jnp.float32,
                         )
                         if own:
-                            part = jnp.where(row - lane <= (2 * p - u) * width, part, NEG)
+                            part = jnp.where(row - lane <= (turn - u) * width, part, NEG)
                         elif u >= surely:
                             part = jnp.where(u < length, part, NEG)
                         parts.append(part)
@@ -424,7 +437,7 @@
         body()
     else:
 
-        @pl.when(lax.rem(plane, 2) == 0 if kind == "near" else plane == 1)
+        @pl.when(plane == (2 if kind == "near" else 1))
         def _():
             body()
 
@@ -438,9 +451,9 @@
 def attend(kind, cluster_count, ids, tables, queries, key_values, earlier=()):
     rows, width = queries[0].shape
     per_shard = rows // width
-    most = KINDS[kind][2] * (per_shard // 2)
-    sizes = (most // 2, most)
-    held = KINDS[kind][2] * 2 * per_shard + most
+    shards, quarters = KINDS[kind][2:]
+    sizes = tuple(q * per_shard // 4 for q in quarters)
+    held = shards * per_shard + sizes[-1]
     smem = pl.BlockSpec(memory_space=pltpu.SMEM)
     vmem = pl.BlockSpec(memory_space=pltpu.VMEM)
     out = jax.ShapeDtypeStruct((per_shard * (width + 4), width), jnp.bfloat16)
@@ -466,7 +479,7 @@
     plane = ids_ref[0, 1]
     width, rows = out_ref.shape
     own_log = log_of(own, rows)
-    near_log = jnp.where(lax.rem(plane, 2) == 1, log_of(near, rows), NEG)
+    near_log = jnp.where(plane == 3, log_of(near, rows), NEG)
     far_log = jnp.where(plane == 3, log_of(third, rows), log_of(second, rows))
     far_log = jnp.where(plane > 1, far_log, NEG)
     top = jnp.maximum(jnp.maximum(own_log, near_log), far_log)
@@ -569,12 +582,12 @@
     far3_keep = send(q_keep, hop((3, 1)))
     second = send(give2, swap)
     third = send(give3, swap)
-    near_keep = send(q_keep, hop((1, 0), (3, 2)))
+    near_keep = send(q_keep, hop((3, 2)))
     low_first = send(first, hop((0, 1)))
     far2_swap = send(first, hop((2, 1)))
     far3_swap = send(first, hop((3, 1)))
     low_second = send(second, hop((0, 1)))
-    near_swap = send(first, hop((1, 0), (3, 2)))
+    near_swap = send(first, hop((3, 2)))
 
     per_shard = tok_rows // width
     cluster_count = clusters.shape[1] // per_shard
@@ -584,19 +597,21 @@
         return attend(kind, cluster_count, ids, tables, queries, key_values, earlier)
 
     plane_kv = (kv_keep, first, second, third)
-    low_kv = (low_keep, low_first, low_second)
-    own_keep, own_swap = meet("own", (q_keep,), plane_kv)
-    own_other = send(own_swap, swap)
-    started = meet("far_high", (far2_keep, far3_keep), plane_kv)
-    back2_keep, back3_keep = meet("far_low", (far2_keep, far3_keep), low_kv, started)
+    started = meet("far_high", (far2_keep, far3_keep), plane_kv + (low_keep,))
+    back2_keep, back3_keep = meet(
+        "far_low", (far2_keep, far3_keep), (low_first, low_second), started
+    )
     back3_keep = send(back3_keep, hop((1, 3)))
     back2_keep = send(back2_keep, hop((1, 2)))
-    down_keep, down_swap = meet("near", (near_keep, near_swap), plane_kv)
-    down_keep = send(down_keep, hop((0, 1), (2, 3)))
-    down_other = send(down_swap, hop((0, 1), (2, 3), cross=1))
-    back2_swap, back3_swap = meet("far_both", (far2_swap, far3_swap), plane_kv + low_kv)
+    both_kv = plane_kv + (low_keep, low_first, low_second)
+    back2_swap, back3_swap = meet("far_both", (far2_swap, far3_swap), both_kv)
     back3_other = send(back3_swap, hop((1, 3), cross=1))
     back2_other = send(back2_swap, hop((1, 2), cross=1))
+    down_keep, down_swap = meet("near", (near_keep, near_swap), plane_kv)
+    down_keep = send(down_keep, hop((2, 3)))
+    down_other = send(down_swap, hop((2, 3), cross=1))
+    own_keep, own_swap = meet("own", (q_keep,), both_kv)
+    own_other = send(own_swap, swap)
     half = head_count // 2
     out = None
     for part, values in enumerate(

time: 98.5 us -> 101 us (1.025)
  the two profiles are of different devices: /device:TPU:25 before, /device:TPU:27 now
where the time goes in v2:
time: 101 us
  waiting for transfers between devices  40.9 us (40%)
  starting transfers between devices  40.8 us (40%)
  Pallas kernels  17.1 us (17%)
  local copies, waits for them, and re-layouts  1.63 us (2%)
    ppermute x19, starting transfers between devices, send(): return lax.ppermute(value, 'seq', pairs)  37.6 us
    ppermute x19, waiting for transfers between devices, send(): return lax.ppermute(value, 'seq', pairs)  35 us
    pallas_call x5, Pallas kernels, attend(): pl.pallas_call(functools.partial(attend_kernel, kind, per_shard, cluster_...  8.49 us
    ppermute x6, waiting for transfers between devices, across(): lax.ppermute(value, 'head', [(g, g ^ flip) for g in range(head_count)])  5.86 us
    pallas_call x2, Pallas kernels, project(): pl.pallas_call(functools.partial(project_kernel, other), in_specs=[pl.Blo...  5.06 us
    ppermute x6, starting transfers between devices, across(): lax.ppermute(value, 'head', [(g, g ^ flip) for g in range(head_count)])  3.22 us
  transfers between devices with their start and end apart: 25, of which 6 were waited for; matrix products, arithmetic and copies ran while one was open for 0% of the time, Pallas kernels for 12%

profile of v2, /device:TPU:27, one launch (start us, length us, event | category | flops | bytes accessed | tf_op | source)
XLA Modules:
  0.0 100.8 jit_solution(6101783400502876847)
XLA Ops:
  0.0 1.6 %copy.6 = bf16[1024,2,384]{2,0,1:T(8,128)(2,1)S(1)} copy(bf16[1024,2,384]{2,1,0:T(2,128)(2,1)} %param.3) | data formatting | bytes 3145728 | tf_op args[0]
  1.7 1.4 %split_heads.1 = (bf16[1024,128]{1,0:T(8,128)(2,1)S(1)}, bf16[2,1024,128]{2,1,0:T(8,128)(2,1)S(1)}, bf16[1024,128]{1,0:T(8,128)(2,1)S(1)}, bf16[1024,128]{1,0:T(8,128)(2,1)S(1)}, bf16[1024,128]{1,0:T(8,128)(2,1)S(1)}) custom-call(s32[1,3]{1,0:T(1,128)S(1)} %add_bitcast_fusion.ids_ref, bf16[2,1024,384]{2,1,0:T(8,128)(2,1)S(1)} %bitcast.8), custom_call_target="tpu_custom_call" | custom-call | tf_op jit(solution)/shard_map/split_heads/pallas_call | solution.py:180
  3.4 1.2 %collective-permute-start.1 = (bf16[1024,128]{1,0:T(8,128)(2,1)S(1)}, bf16[1024,128]{1,0:T(8,128)(2,1)S(1)}, u32[]{:S(2)}, u32[]{:S(2)}) collective-permute-start(bf16[1024,128]{1,0:T(8,128)(2,1)S(1)} %get-tuple-element.23), channel_id=1, source_target_pairs={{0,4},{4,0},{8,12},{12,8},{16,20},{20,16},{24,28},{28,24},{1,5},{5... | collective-permute-start | bytes 786440 | tf_op jit(solution)/shard_map/ppermute | solution.py:571
  4.9 2.1 %collective-permute-start.7 = (bf16[1024,128]{1,0:T(8,128)(2,1)S(1)}, bf16[1024,128]{1,0:T(8,128)(2,1)S(1)}, u32[]{:S(2)}, u32[]{:S(2)}) collective-permute-start(bf16[1024,128]{1,0:T(8,128)(2,1)S(1)} %get-tuple-element.20.refs_0_), channel_id=1, source_target_pairs={{24,16},{28,20},{25,17},{29,21},{26,18},{30,22},{27,19},{31,23}} | collective-permute-start | bytes 786440 | tf_op jit(solution)/shard_map/ppermute | solution.py:571
  7.0 0.7 collective-permute-start.3
  7.7 2.7 %collective-permute-done.refs_2_.refs_3_ = bf16[1024,128]{1,0:T(8,128)(2,1)S(1)} collective-permute-done((bf16[1024,128]{1,0:T(8,128)(2,1)S(1)}, bf16[1024,128]{1,0:T(8,128)(2,1)S(1)}, u32[]{:S(2)}, u32[]{:S(2)}) %collective-permute-start) | collective-permute-done | bytes 262176 | tf_op jit(solution)/shard_map/ppermute | solution.py:571
  10.4 2.1 %collective-permute-start.8 = (bf16[1024,128]{1,0:T(8,128)(2,1)S(1)}, bf16[1024,128]{1,0:T(8,128)(2,1)S(1)}, u32[]{:S(2)}, u32[]{:S(2)}) collective-permute-start(bf16[1024,128]{1,0:T(8,128)(2,1)S(1)} %collective-permute-done.refs_2_.refs_3_), channel_id=1, source_target_pairs={{24,16},{28,20},{25,17},{29,21},{26,18},{30,22},{27,19},{31,23}} | collective-permute-start | bytes 786440 | tf_op jit(solution)/shard_map/ppermute | solution.py:571
  12.5 3.5 %collective-permute-done.1.refs_3_.refs_4_ = bf16[1024,128]{1,0:T(8,128)(2,1)S(1)} collective-permute-done((bf16[1024,128]{1,0:T(8,128)(2,1)S(1)}, bf16[1024,128]{1,0:T(8,128)(2,1)S(1)}, u32[]{:S(2)}, u32[]{:S(2)}) %collective-permute-start.1) | collective-permute-done | bytes 262176 | tf_op jit(solution)/shard_map/ppermute | solution.py:571
  16.0 2.0 %collective-permute-start.19 = (bf16[1024,128]{1,0:T(8,128)(2,1)S(1)}, bf16[1024,128]{1,0:T(8,128)(2,1)S(1)}, u32[]{:S(2)}, u32[]{:S(2)}) collective-permute-start(bf16[1024,128]{1,0:T(8,128)(2,1)S(1)} %get-tuple-element.20.refs_0_), channel_id=1, source_target_pairs={{24,8},{28,12},{25,9},{29,13},{26,10},{30,14},{27,11},{31,15}} | collective-permute-start | bytes 786440 | tf_op jit(solution)/shard_map/ppermute | solution.py:571
  18.0 3.6 %collective-permute-done.2.refs_4_.refs_5_ = bf16[1024,128]{1,0:T(8,128)(2,1)S(1)} collective-permute-done((bf16[1024,128]{1,0:T(8,128)(2,1)S(1)}, bf16[1024,128]{1,0:T(8,128)(2,1)S(1)}, u32[]{:S(2)}, u32[]{:S(2)}) %collective-permute-start.2) | collective-permute-done | bytes 262176 | tf_op jit(solution)/shard_map/ppermute | solution.py:571
  23.7 0.7 block_tables.1.tab
  24.4 0.7 shard_map.38
  25.2 1.3 %collective-permute-start.17 = (bf16[1056,128]{1,0:T(8,128)(2,1)S(1)}, bf16[1056,128]{1,0:T(8,128)(2,1)S(1)}, u32[]{:S(2)}, u32[]{:S(2)}) collective-permute-start(bf16[1056,128]{1,0:T(8,128)(2,1)S(1)} %get-tuple-element.30), channel_id=1, source_target_pairs={{16,24},{20,28},{17,25},{21,29},{18,26},{22,30},{19,27},{23,31}} | collective-permute-start | bytes 811016 | tf_op jit(solution)/shard_map/ppermute | solution.py:571
  26.5 0.8 shard_map.40
  27.3 0.8 shard_map.41
  28.0 0.7 collective-permute-start.20
  28.7 18.8 %collective-permute-start.11 = (bf16[1024,128]{1,0:T(8,128)(2,1)S(1)}, bf16[1024,128]{1,0:T(8,128)(2,1)S(1)}, u32[]{:S(2)}, u32[]{:S(2)}) collective-permute-start(bf16[1024,128]{1,0:T(8,128)(2,1)S(1)} %collective-permute-done.refs_2_.refs_3_), channel_id=1, source_target_pairs={{24,8},{28,12},{25,9},{29,13},{26,10},{30,14},{27,11},{31,15}} | collective-permute-start | bytes 786440 | tf_op jit(solution)/shard_map/ppermute | solution.py:571
  48.2 1.3 %collective-permute-start.9 = (bf16[1056,128]{1,0:T(8,128)(2,1)S(1)}, bf16[1056,128]{1,0:T(8,128)(2,1)S(1)}, u32[]{:S(2)}, u32[]{:S(2)}) collective-permute-start(bf16[1056,128]{1,0:T(8,128)(2,1)S(1)} %get-tuple-element.26), channel_id=1, source_target_pairs={{16,28},{20,24},{17,29},{21,25},{18,30},{22,26},{19,31},{23,27}} | collective-permute-start | bytes 811016 | tf_op jit(solution)/shard_map/ppermute | solution.py:571
  49.5 5.5 %shard_map.37 = (bf16[1056,128]{1,0:T(8,128)(2,1)S(1)}, bf16[1056,128]{1,0:T(8,128)(2,1)S(1)}) custom-call(s32[1,3]{1,0:T(1,128)S(1)} %add_bitcast_fusion.ids_ref, s32[24,128]{1,0:T(8,128)S(1)} %block_tables.1.tab, bf16[1024,128]{1,0:T(8,128)(2,1)S(1)} %get-tuple-element.20.refs_0_, bf16[2,1024,128]{2,1,0:T(8,128)(2,1)S(1)} %get-tuple-element.21.refs_1_.refs_2_, ...), custom_call_target="tpu_custom_call" | custom-call | tf_op jit(solution)/shard_map/pallas_call | solution.py:461
  55.0 0.8 collective-permute-start.6
  55.8 1.4 %collective-permute-start.21 = (bf16[1056,128]{1,0:T(8,128)(2,1)S(1)}, bf16[1056,128]{1,0:T(8,128)(2,1)S(1)}, u32[]{:S(2)}, u32[]{:S(2)}) collective-permute-start(bf16[1056,128]{1,0:T(8,128)(2,1)S(1)} %get-tuple-element.34), channel_id=1, source_target_pairs={{8,24},{12,28},{9,25},{13,29},{10,26},{14,30},{11,27},{15,31}} | collective-permute-start | bytes 811016 | tf_op jit(solution)/shard_map/ppermute | solution.py:571
  57.3 0.8 shard_map.39
  58.7 1.3 %collective-permute-start.13 = (bf16[1056,128]{1,0:T(8,128)(2,1)S(1)}, bf16[1056,128]{1,0:T(8,128)(2,1)S(1)}, u32[]{:S(2)}, u32[]{:S(2)}) collective-permute-start(bf16[1056,128]{1,0:T(8,128)(2,1)S(1)} %get-tuple-element.28), channel_id=1, source_target_pairs={{8,28},{12,24},{9,29},{13,25},{10,30},{14,26},{11,31},{15,27}} | collective-permute-start | bytes 811016 | tf_op jit(solution)/shard_map/ppermute | solution.py:571
  60.0 10.0 %collective-permute-done.21.third = bf16[1056,128]{1,0:T(8,128)(2,1)S(1)} collective-permute-done((bf16[1056,128]{1,0:T(8,128)(2,1)S(1)}, bf16[1056,128]{1,0:T(8,128)(2,1)S(1)}, u32[]{:S(2)}, u32[]{:S(2)}) %collective-permute-start.21) | collective-permute-done | bytes 270368 | tf_op jit(solution)/shard_map/ppermute | solution.py:571
  70.0 0.7 combine.3.refs_0_
  71.1 15.1 %collective-permute-done.13.third = bf16[1056,128]{1,0:T(8,128)(2,1)S(1)} collective-permute-done((bf16[1056,128]{1,0:T(8,128)(2,1)S(1)}, bf16[1056,128]{1,0:T(8,128)(2,1)S(1)}, u32[]{:S(2)}, u32[]{:S(2)}) %collective-permute-start.13) | collective-permute-done | bytes 270368 | tf_op jit(solution)/shard_map/ppermute | solution.py:571
  86.2 0.7 combine.2.refs_0_
  87.0 1.1 %collective-permute-start.22 = (bf16[128,1024]{1,0:T(8,128)(2,1)S(1)}, bf16[128,1024]{1,0:T(8,128)(2,1)S(1)}, u32[]{:S(2)}, u32[]{:S(2)}) collective-permute-start(bf16[128,1024]{1,0:T(8,128)(2,1)S(1)} %combine.3.refs_0_), channel_id=1, source_target_pairs={{0,1},{1,0},{2,3},{3,2},{4,5},{5,4},{6,7},{7,6},{8,9},{9,8},{10,11... | collective-permute-start | bytes 786440 | tf_op jit(solution)/shard_map/ppermute | solution.py:574
  88.6 5.8 %collective-permute-done.15.refs_2_ = bf16[128,1024]{1,0:T(8,128)(2,1)S(1)} collective-permute-done((bf16[128,1024]{1,0:T(8,128)(2,1)S(1)}, bf16[128,1024]{1,0:T(8,128)(2,1)S(1)}, u32[]{:S(2)}, u32[]{:S(2)}) %collective-permute-start.15) | collective-permute-done | bytes 262176 | tf_op jit(solution)/shard_map/ppermute | solution.py:574
  94.5 1.2 %collective-permute-start.16 = (bf16[128,1024]{1,0:T(8,128)(2,1)S(1)}, bf16[128,1024]{1,0:T(8,128)(2,1)S(1)}, u32[]{:S(2)}, u32[]{:S(2)}) collective-permute-start(bf16[128,1024]{1,0:T(8,128)(2,1)S(1)} %collective-permute-done.15.refs_2_), channel_id=1, source_target_pairs={{0,1},{1,0},{2,3},{3,2},{4,5},{5,4},{6,7},{7,6},{8,9},{9,8},{10,11... | collective-permute-start | bytes 786440 | tf_op jit(solution)/shard_map/ppermute | solution.py:574
  95.7 1.8 %project.2.refs_4_ = f32[1024,1024]{1,0:T(8,128)S(1)} custom-call(s32[1,3]{1,0:T(1,128)S(1)} %add_bitcast_fusion.ids_ref, bf16[1024,1024]{1,0:T(8,128)(2,1)S(1)} %copy-done, bf16[128,1024]{1,0:T(8,128)(2,1)S(1)} %combine.3.refs_0_, bf16[128,1024]{1,0:T(8,128)(2,1)S(1)} %collective-permute-done.22.refs_1_, ...), custom_call_target="tpu_custom_call" | custom-call | tf_op jit(solution)/shard_map/project/pallas_call | solution.py:544
  97.6 3.2 %project.3 = bf16[1024,1024]{1,0:T(8,128)(2,1)} custom-call(s32[1,3]{1,0:T(1,128)S(1)} %add_bitcast_fusion.ids_ref, bf16[1024,1024]{1,0:T(8,128)(2,1)S(1)} %copy-done, bf16[128,1024]{1,0:T(8,128)(2,1)S(1)} %combine.2.refs_0_, bf16[128,1024]{1,0:T(8,128)(2,1)S(1)} %collective-permute-done.14.refs_1_, bf16[128,1024]{1,0:T(8,128)(2,1)S(1)} %collective-permute-done.15.refs_2_, ...), custom_call_target="tpu_custom_call" | custom-call | tf_op jit(solution)/shard_map/project/pallas_call | solution.py:544
  (35 shorter events, 5.0 us)
Async XLA Ops:
  0.0 23.7 %copy-start.1 = (s32[2,64]{1,0:T(2,128)S(1)}, s32[2,64]{1,0:T(2,128)}, u32[]{:S(2)}) copy-start(s32[2,64]{1,0:T(2,128)} %table_ref.1) | copy-start | bytes 1540
  3.1 7.3 %collective-permute-start = (bf16[1024,128]{1,0:T(8,128)(2,1)S(1)}, bf16[1024,128]{1,0:T(8,128)(2,1)S(1)}, u32[]{:S(2)}, u32[]{:S(2)}) collective-permute-start(bf16[1024,128]{1,0:T(8,128)(2,1)S(1)} %get-tuple-element.22), channel_id=1, source_target_pairs={{0,4},{4,0},{8,12},{12,8},{16,20},{20,16},{24,28},{28,24},{1,5},{5... | collective-permute-start | bytes 786440 | tf_op jit(solution)/shard_map/ppermute | solution.py:571
  3.4 12.6 %collective-permute-start.1 = (bf16[1024,128]{1,0:T(8,128)(2,1)S(1)}, bf16[1024,128]{1,0:T(8,128)(2,1)S(1)}, u32[]{:S(2)}, u32[]{:S(2)}) collective-permute-start(bf16[1024,128]{1,0:T(8,128)(2,1)S(1)} %get-tuple-element.23), channel_id=1, source_target_pairs={{0,4},{4,0},{8,12},{12,8},{16,20},{20,16},{24,28},{28,24},{1,5},{5... | collective-permute-start | bytes 786440 | tf_op jit(solution)/shard_map/ppermute | solution.py:571
  4.6 17.0 %collective-permute-start.2 = (bf16[1024,128]{1,0:T(8,128)(2,1)S(1)}, bf16[1024,128]{1,0:T(8,128)(2,1)S(1)}, u32[]{:S(2)}, u32[]{:S(2)}) collective-permute-start(bf16[1024,128]{1,0:T(8,128)(2,1)S(1)} %get-tuple-element.24), channel_id=1, source_target_pairs={{0,4},{4,0},{8,12},{12,8},{16,20},{20,16},{24,28},{28,24},{1,5},{5... | collective-permute-start | bytes 786440 | tf_op jit(solution)/shard_map/ppermute | solution.py:571
  4.9 17.4 %collective-permute-start.7 = (bf16[1024,128]{1,0:T(8,128)(2,1)S(1)}, bf16[1024,128]{1,0:T(8,128)(2,1)S(1)}, u32[]{:S(2)}, u32[]{:S(2)}) collective-permute-start(bf16[1024,128]{1,0:T(8,128)(2,1)S(1)} %get-tuple-element.20.refs_0_), channel_id=1, source_target_pairs={{24,16},{28,20},{25,17},{29,21},{26,18},{30,22},{27,19},{31,23}} | collective-permute-start | bytes 786440 | tf_op jit(solution)/shard_map/ppermute | solution.py:571
  7.0 19.5 %collective-permute-start.3 = (bf16[2,1024,128]{2,1,0:T(8,128)(2,1)S(1)}, bf16[2,1024,128]{2,1,0:T(8,128)(2,1)S(1)}, u32[]{:S(2)}, u32[]{:S(2)}) collective-permute-start(bf16[2,1024,128]{2,1,0:T(8,128)(2,1)S(1)} %get-tuple-element.21.refs_1_.refs_2_), channel_id=1, source_target_pairs={{0,8},{4,12},{1,9},{5,13},{2,10},{6,14},{3,11},{7,15}} | collective-permute-start | bytes 1572872 | tf_op jit(solution)/shard_map/ppermute | solution.py:571
  10.4 12.6 %collective-permute-start.8 = (bf16[1024,128]{1,0:T(8,128)(2,1)S(1)}, bf16[1024,128]{1,0:T(8,128)(2,1)S(1)}, u32[]{:S(2)}, u32[]{:S(2)}) collective-permute-start(bf16[1024,128]{1,0:T(8,128)(2,1)S(1)} %collective-permute-done.refs_2_.refs_3_), channel_id=1, source_target_pairs={{24,16},{28,20},{25,17},{29,21},{26,18},{30,22},{27,19},{31,23}} | collective-permute-start | bytes 786440 | tf_op jit(solution)/shard_map/ppermute | solution.py:571
  16.0 9.2 %collective-permute-start.19 = (bf16[1024,128]{1,0:T(8,128)(2,1)S(1)}, bf16[1024,128]{1,0:T(8,128)(2,1)S(1)}, u32[]{:S(2)}, u32[]{:S(2)}) collective-permute-start(bf16[1024,128]{1,0:T(8,128)(2,1)S(1)} %get-tuple-element.20.refs_0_), channel_id=1, source_target_pairs={{24,8},{28,12},{25,9},{29,13},{26,10},{30,14},{27,11},{31,15}} | collective-permute-start | bytes 786440 | tf_op jit(solution)/shard_map/ppermute | solution.py:571
  21.6 4.9 %collective-permute-start.18 = (bf16[1024,128]{1,0:T(8,128)(2,1)S(1)}, bf16[1024,128]{1,0:T(8,128)(2,1)S(1)}, u32[]{:S(2)}, u32[]{:S(2)}) collective-permute-start(bf16[1024,128]{1,0:T(8,128)(2,1)S(1)} %get-tuple-element.20.refs_0_), channel_id=1, source_target_pairs={{16,8},{20,12},{17,9},{21,13},{18,10},{22,14},{19,11},{23,15}} | collective-permute-start | bytes 786440 | tf_op jit(solution)/shard_map/ppermute | solution.py:571
  22.3 5.0 %collective-permute-start.4 = (bf16[1024,128]{1,0:T(8,128)(2,1)S(1)}, bf16[1024,128]{1,0:T(8,128)(2,1)S(1)}, u32[]{:S(2)}, u32[]{:S(2)}) collective-permute-start(bf16[1024,128]{1,0:T(8,128)(2,1)S(1)} %collective-permute-done.refs_2_.refs_3_), channel_id=1, source_target_pairs={{0,8},{4,12},{1,9},{5,13},{2,10},{6,14},{3,11},{7,15}} | collective-permute-start | bytes 786440 | tf_op jit(solution)/shard_map/ppermute | solution.py:571
  23.0 4.3 %collective-permute-start.5 = (bf16[1024,128]{1,0:T(8,128)(2,1)S(1)}, bf16[1024,128]{1,0:T(8,128)(2,1)S(1)}, u32[]{:S(2)}, u32[]{:S(2)}) collective-permute-start(bf16[1024,128]{1,0:T(8,128)(2,1)S(1)} %collective-permute-done.1.refs_3_.refs_4_), channel_id=1, source_target_pairs={{0,8},{4,12},{1,9},{5,13},{2,10},{6,14},{3,11},{7,15}} | collective-permute-start | bytes 786440 | tf_op jit(solution)/shard_map/ppermute | solution.py:571
  25.2 32.9 %collective-permute-start.17 = (bf16[1056,128]{1,0:T(8,128)(2,1)S(1)}, bf16[1056,128]{1,0:T(8,128)(2,1)S(1)}, u32[]{:S(2)}, u32[]{:S(2)}) collective-permute-start(bf16[1056,128]{1,0:T(8,128)(2,1)S(1)} %get-tuple-element.30), channel_id=1, source_target_pairs={{16,24},{20,28},{17,25},{21,29},{18,26},{22,30},{19,27},{23,31}} | collective-permute-start | bytes 811016 | tf_op jit(solution)/shard_map/ppermute | solution.py:571
  28.0 30.7 %collective-permute-start.20 = (bf16[1056,128]{1,0:T(8,128)(2,1)S(1)}, bf16[1056,128]{1,0:T(8,128)(2,1)S(1)}, u32[]{:S(2)}, u32[]{:S(2)}) collective-permute-start(bf16[1056,128]{1,0:T(8,128)(2,1)S(1)} %get-tuple-element.33), channel_id=1, source_target_pairs={{8,16},{12,20},{9,17},{13,21},{10,18},{14,22},{11,19},{15,23}} | collective-permute-start | bytes 811016 | tf_op jit(solution)/shard_map/ppermute | solution.py:571
  28.7 26.3 %collective-permute-start.11 = (bf16[1024,128]{1,0:T(8,128)(2,1)S(1)}, bf16[1024,128]{1,0:T(8,128)(2,1)S(1)}, u32[]{:S(2)}, u32[]{:S(2)}) collective-permute-start(bf16[1024,128]{1,0:T(8,128)(2,1)S(1)} %collective-permute-done.refs_2_.refs_3_), channel_id=1, source_target_pairs={{24,8},{28,12},{25,9},{29,13},{26,10},{30,14},{27,11},{31,15}} | collective-permute-start | bytes 786440 | tf_op jit(solution)/shard_map/ppermute | solution.py:571
  47.5 8.3 %collective-permute-start.10 = (bf16[1024,128]{1,0:T(8,128)(2,1)S(1)}, bf16[1024,128]{1,0:T(8,128)(2,1)S(1)}, u32[]{:S(2)}, u32[]{:S(2)}) collective-permute-start(bf16[1024,128]{1,0:T(8,128)(2,1)S(1)} %collective-permute-done.refs_2_.refs_3_), channel_id=1, source_target_pairs={{16,8},{20,12},{17,9},{21,13},{18,10},{22,14},{19,11},{23,15}} | collective-permute-start | bytes 786440 | tf_op jit(solution)/shard_map/ppermute | solution.py:571
  48.2 22.9 %collective-permute-start.9 = (bf16[1056,128]{1,0:T(8,128)(2,1)S(1)}, bf16[1056,128]{1,0:T(8,128)(2,1)S(1)}, u32[]{:S(2)}, u32[]{:S(2)}) collective-permute-start(bf16[1056,128]{1,0:T(8,128)(2,1)S(1)} %get-tuple-element.26), channel_id=1, source_target_pairs={{16,28},{20,24},{17,29},{21,25},{18,30},{22,26},{19,31},{23,27}} | collective-permute-start | bytes 811016 | tf_op jit(solution)/shard_map/ppermute | solution.py:571
  55.0 16.1 %collective-permute-start.6 = (bf16[1056,128]{1,0:T(8,128)(2,1)S(1)}, bf16[1056,128]{1,0:T(8,128)(2,1)S(1)}, u32[]{:S(2)}, u32[]{:S(2)}) collective-permute-start(bf16[1056,128]{1,0:T(8,128)(2,1)S(1)} %get-tuple-element.25), channel_id=1, source_target_pairs={{0,4},{4,0},{8,12},{12,8},{16,20},{20,16},{24,28},{28,24},{1,5},{5... | collective-permute-start | bytes 811016 | tf_op jit(solution)/shard_map/ppermute | solution.py:571
  55.8 39.9 %copy-start = (bf16[1024,1024]{1,0:T(8,128)(2,1)S(1)}, bf16[1024,1024]{1,0:T(8,128)(2,1)}, u32[]{:S(2)}) copy-start(bf16[1024,1024]{1,0:T(8,128)(2,1)} %weight_ref.3) | copy-start | bytes 6291460
  55.8 14.2 %collective-permute-start.21 = (bf16[1056,128]{1,0:T(8,128)(2,1)S(1)}, bf16[1056,128]{1,0:T(8,128)(2,1)S(1)}, u32[]{:S(2)}, u32[]{:S(2)}) collective-permute-start(bf16[1056,128]{1,0:T(8,128)(2,1)S(1)} %get-tuple-element.34), channel_id=1, source_target_pairs={{8,24},{12,28},{9,25},{13,29},{10,26},{14,30},{11,27},{15,31}} | collective-permute-start | bytes 811016 | tf_op jit(solution)/shard_map/ppermute | solution.py:571
  58.0 13.0 %collective-permute-start.12 = (bf16[1056,128]{1,0:T(8,128)(2,1)S(1)}, bf16[1056,128]{1,0:T(8,128)(2,1)S(1)}, u32[]{:S(2)}, u32[]{:S(2)}) collective-permute-start(bf16[1056,128]{1,0:T(8,128)(2,1)S(1)} %get-tuple-element.27), channel_id=1, source_target_pairs={{8,20},{12,16},{9,21},{13,17},{10,22},{14,18},{11,23},{15,19}} | collective-permute-start | bytes 811016 | tf_op jit(solution)/shard_map/ppermute | solution.py:571
  58.7 27.5 %collective-permute-start.13 = (bf16[1056,128]{1,0:T(8,128)(2,1)S(1)}, bf16[1056,128]{1,0:T(8,128)(2,1)S(1)}, u32[]{:S(2)}, u32[]{:S(2)}) collective-permute-start(bf16[1056,128]{1,0:T(8,128)(2,1)S(1)} %get-tuple-element.28), channel_id=1, source_target_pairs={{8,28},{12,24},{9,29},{13,25},{10,30},{14,26},{11,31},{15,27}} | collective-permute-start | bytes 811016 | tf_op jit(solution)/shard_map/ppermute | solution.py:571
  70.8 17.4 %collective-permute-start.23 = (bf16[128,1024]{1,0:T(8,128)(2,1)S(1)}, bf16[128,1024]{1,0:T(8,128)(2,1)S(1)}, u32[]{:S(2)}, u32[]{:S(2)}) collective-permute-start(bf16[128,1024]{1,0:T(8,128)(2,1)S(1)} %combine.3.refs_0_), channel_id=1, source_target_pairs={{0,2},{1,3},{2,0},{3,1},{4,6},{5,7},{6,4},{7,5},{8,10},{9,11},{10,... | collective-permute-start | bytes 786440 | tf_op jit(solution)/shard_map/ppermute | solution.py:574
  86.9 7.6 %collective-permute-start.15 = (bf16[128,1024]{1,0:T(8,128)(2,1)S(1)}, bf16[128,1024]{1,0:T(8,128)(2,1)S(1)}, u32[]{:S(2)}, u32[]{:S(2)}) collective-permute-start(bf16[128,1024]{1,0:T(8,128)(2,1)S(1)} %combine.2.refs_0_), channel_id=1, source_target_pairs={{0,2},{1,3},{2,0},{3,1},{4,6},{5,7},{6,4},{7,5},{8,10},{9,11},{10,... | collective-permute-start | bytes 786440 | tf_op jit(solution)/shard_map/ppermute | solution.py:574
  87.0 8.7 %collective-permute-start.22 = (bf16[128,1024]{1,0:T(8,128)(2,1)S(1)}, bf16[128,1024]{1,0:T(8,128)(2,1)S(1)}, u32[]{:S(2)}, u32[]{:S(2)}) collective-permute-start(bf16[128,1024]{1,0:T(8,128)(2,1)S(1)} %combine.3.refs_0_), channel_id=1, source_target_pairs={{0,1},{1,0},{2,3},{3,2},{4,5},{5,4},{6,7},{7,6},{8,9},{9,8},{10,11... | collective-permute-start | bytes 786440 | tf_op jit(solution)/shard_map/ppermute | solution.py:574
  88.1 7.6 %collective-permute-start.24 = (bf16[128,1024]{1,0:T(8,128)(2,1)S(1)}, bf16[128,1024]{1,0:T(8,128)(2,1)S(1)}, u32[]{:S(2)}, u32[]{:S(2)}) collective-permute-start(bf16[128,1024]{1,0:T(8,128)(2,1)S(1)} %collective-permute-done.23.refs_2_), channel_id=1, source_target_pairs={{0,1},{1,0},{2,3},{3,2},{4,5},{5,4},{6,7},{7,6},{8,9},{9,8},{10,11... | collective-permute-start | bytes 786440 | tf_op jit(solution)/shard_map/ppermute | solution.py:574
  88.1 9.4 %collective-permute-start.14 = (bf16[128,1024]{1,0:T(8,128)(2,1)S(1)}, bf16[128,1024]{1,0:T(8,128)(2,1)S(1)}, u32[]{:S(2)}, u32[]{:S(2)}) collective-permute-start(bf16[128,1024]{1,0:T(8,128)(2,1)S(1)} %combine.2.refs_0_), channel_id=1, source_target_pairs={{0,1},{1,0},{2,3},{3,2},{4,5},{5,4},{6,7},{7,6},{8,9},{9,8},{10,11... | collective-permute-start | bytes 786440 | tf_op jit(solution)/shard_map/ppermute | solution.py:574
  94.5 3.1 %collective-permute-start.16 = (bf16[128,1024]{1,0:T(8,128)(2,1)S(1)}, bf16[128,1024]{1,0:T(8,128)(2,1)S(1)}, u32[]{:S(2)}, u32[]{:S(2)}) collective-permute-start(bf16[128,1024]{1,0:T(8,128)(2,1)S(1)} %collective-permute-done.15.refs_2_), channel_id=1, source_target_pairs={{0,1},{1,0},{2,3},{3,2},{4,5},{5,4},{6,7},{7,6},{8,9},{9,8},{10,11... | collective-permute-start | bytes 786440 | tf_op jit(solution)/shard_map/ppermute | solution.py:574

commit v3 on v2

--- a/solution.py
+++ b/solution.py
@@ -192,6 +192,7 @@
 
 
 OWN, UPPER, REST, BOTH, NEAR, KEPT, SWAPPED = range(0, 21, 3)
+WHERE = 21
 TABLE_ROWS = 24
 
 
@@ -201,6 +202,8 @@
     blocks = table_ref.shape[1]
     span = 2 * per_shard
     out_ref[...] = jnp.zeros_like(out_ref)
+    slot = lax.broadcasted_iota(jnp.int32, (1, 2 * blocks), 1)
+    out_ref[WHERE : WHERE + 1, :] = jnp.where(slot == 0, column, plane)
     labels = jnp.where(column == 0, table_ref[0:1, :], table_ref[1:2, :])
     down = lax.broadcasted_iota(jnp.int32, (blocks, blocks), 0)
     along = lax.broadcasted_iota(jnp.int32, (blocks, blocks), 1)
@@ -252,7 +255,7 @@
 }
 
 
-def attend_kernel(kind, per_shard, cluster_count, sizes, ids_ref, tab, *refs):
+def attend_kernel(kind, per_shard, cluster_count, sizes, tab, *refs):
     own = kind == "own"
     kv_row, q_row = KINDS[kind][:2]
     plane_keys = kind != "far_low"
@@ -267,8 +270,8 @@
     earlier, refs = (refs[:2], refs[2:]) if merging else ((), refs)
     out_refs = refs[:2]
     keys, values, queries, outs, logs, mine = refs[2:]
-    column = ids_ref[0, 0]
-    plane = ids_ref[0, 1]
+    column = tab[WHERE, 0]
+    plane = tab[WHERE, 1]
     width = keys.shape[2]
     scale = 1.0 / math.sqrt(width)
     log_scale = scale / math.log(2.0)
@@ -343,8 +346,9 @@
         else:
             bring_query(shards[1], q_refs[1])
 
-        row = lax.broadcasted_iota(jnp.int32, (width, 2 * width), 0)
-        lane = lax.broadcasted_iota(jnp.int32, (width, 2 * width), 1)
+        if own:
+            ahead = lax.broadcasted_iota(jnp.int32, (width, 4 * width), 0)
+            ahead -= lax.broadcasted_iota(jnp.int32, (width, 4 * width), 1)
 
         def cluster(c, carry):
             begin = tab[kv_row + 1, c]
@@ -352,59 +356,59 @@
             q_begin = tab[q_row + 1, c]
             q_count = tab[q_row + 2, c]
 
-            def pair(p, carry):
-                at_q = q_begin + 2 * p
-                turn = length - q_count + 2 * p
-                blocks = jnp.minimum(turn + 2, length) if own else length
-
-                def tile(most, surely):
-                    query = queries[pl.ds(at_q, 2)].reshape(2 * width, width)
-                    parts = []
-                    for u in range(most):
-                        part = lax.dot_general(
-                            keys[begin + u],
-                            query,
-                            (((1,), (1,)), ((), ())),
-                            preferred_element_type=jnp.float32,
-                        )
-                        if own:
-                            part = jnp.where(row - lane <= (turn - u) * width, part, NEG)
-                        elif u >= surely:
-                            part = jnp.where(u < length, part, NEG)
-                        parts.append(part)
-                    scores = jnp.concatenate(parts, axis=0)
-                    top = jnp.max(scores, axis=0, keepdims=True)
-                    weights = jnp.exp2((scores - top) * log_scale)
-                    total = jnp.sum(weights, axis=0, keepdims=True)
-                    acc = jnp.dot(
-                        jnp.concatenate([values[begin + u] for u in range(most)], axis=1),
-                        weights.astype(jnp.bfloat16),
+            def tile(wide, most, below):
+                query = queries[pl.ds(q_begin, wide)].reshape(wide * width, width)
+                parts = []
+                for u in range(most):
+                    part = lax.dot_general(
+                        keys[begin + u],
+                        query,
+                        (((1,), (1,)), ((), ())),
                         preferred_element_type=jnp.float32,
                     )
-                    result = (acc / total).astype(outs.dtype)
-                    log = top * scale + jnp.log(total)
-                    for j in range(2):
-                        outs[at_q + j] = result[:, j * width : (j + 1) * width]
-                        logs[pl.ds(at_q + j, 1), :] = log[:, j * width : (j + 1) * width]
-
+                    if own:
+                        allowed = ahead[:, : wide * width] <= (length - q_count - u) * width
+                        part = jnp.where(allowed, part, NEG)
+                    elif u > below:
+                        part = jnp.where(u < length, part, NEG)
+                    parts.append(part)
+                scores = jnp.concatenate(parts, axis=0)
+                top = jnp.max(scores, axis=0, keepdims=True)
+                weights = jnp.exp2((scores - top) * log_scale)
+                total = jnp.sum(weights, axis=0, keepdims=True)
+                acc = jnp.dot(
+                    jnp.concatenate([values[begin + u] for u in range(most)], axis=1),
+                    weights.astype(jnp.bfloat16),
+                    preferred_element_type=jnp.float32,
+                )
+                result = (acc / total).astype(outs.dtype)
+                log = top * scale + jnp.log(total)
+                for j in range(wide):
+                    outs[q_begin + j] = result[:, j * width : (j + 1) * width]
+                    logs[pl.ds(q_begin + j, 1), :] = log[:, j * width : (j + 1) * width]
+
+            for wide in (2, 4):
                 for k, most in enumerate(sizes):
                     below = sizes[k - 1] if k else 0
 
-                    @pl.when((blocks > below) & (blocks <= most))
-                    def _(most=most, below=below):
-                        tile(most, below + 1)
-
-                if not own:
-
-                    @pl.when(blocks == 0)
-                    def _():
-                        for j in range(2):
-                            outs[at_q + j] = jnp.zeros((width, width), outs.dtype)
-                            logs[pl.ds(at_q + j, 1), :] = jnp.full((1, width), NEG, jnp.float32)
-
-                return carry
-
-            return lax.fori_loop(0, (q_count + 1) // 2, pair, carry)
+                    fits = (q_count > wide - 2) & (q_count <= wide)
+
+                    @pl.when(fits & (length > below) & (length <= most))
+                    def _(wide=wide, most=most, below=below):
+                        tile(wide, most, below)
+
+            if not own:
+
+                @pl.when(length == 0)
+                def _():
+                    def empty(i, carry):
+                        outs[q_begin + i] = jnp.zeros((width, width), outs.dtype)
+                        logs[pl.ds(q_begin + i, 1), :] = jnp.full((1, width), NEG, jnp.float32)
+                        return carry
+
+                    lax.fori_loop(0, q_count, empty, 0)
+
+            return carry
 
         lax.fori_loop(0, cluster_count, cluster, 0)
         for g, out_ref in enumerate(out_refs):
@@ -448,7 +452,7 @@
     return tail[:step] + tail[step : 2 * step] + tail[2 * step : 3 * step]
 
 
-def attend(kind, cluster_count, ids, tables, queries, key_values, earlier=()):
+def attend(kind, cluster_count, tables, queries, key_values, earlier=()):
     rows, width = queries[0].shape
     per_shard = rows // width
     shards, quarters = KINDS[kind][2:]
@@ -460,19 +464,19 @@
     tile = (width, width)
     return pl.pallas_call(
         functools.partial(attend_kernel, kind, per_shard, cluster_count, sizes),
-        in_specs=[smem, smem] + [vmem] * (len(queries) + len(key_values) + len(earlier)),
+        in_specs=[smem] + [vmem] * (len(queries) + len(key_values) + len(earlier)),
         out_specs=[vmem] * 2,
         out_shape=[out] * 2,
         scratch_shapes=[
             pltpu.VMEM((held,) + tile, jnp.bfloat16),
             pltpu.VMEM((held,) + tile, jnp.bfloat16),
-            pltpu.VMEM((2 * per_shard + 2,) + tile, jnp.bfloat16),
-            pltpu.VMEM((2 * per_shard + 2,) + tile, jnp.bfloat16),
+            pltpu.VMEM((2 * per_shard + 4,) + tile, jnp.bfloat16),
+            pltpu.VMEM((2 * per_shard + 4,) + tile, jnp.bfloat16),
             pltpu.VMEM((2 * per_shard + 8, width), jnp.float32),
             pltpu.VMEM((per_shard, width), jnp.float32),
         ],
         compiler_params=pltpu.CompilerParams(vmem_limit_bytes=VMEM_BYTES),
-    )(ids, tables, *queries, *key_values, *earlier)
+    )(tables, *queries, *key_values, *earlier)
 
 
 def combine_kernel(ids_ref, own, near, second, third, out_ref):
@@ -594,7 +598,7 @@
     tables = block_tables(ids, clusters, per_shard)
 
     def meet(kind, queries, key_values, earlier=()):
-        return attend(kind, cluster_count, ids, tables, queries, key_values, earlier)
+        return attend(kind, cluster_count, tables, queries, key_values, earlier)
 
     plane_kv = (kv_keep, first, second, third)
     started = meet("far_high", (far2_keep, far3_keep), plane_kv + (low_keep,))

time: 101 us -> 97.9 us (0.969)
  waiting for transfers between devices: 40.9 us -> 39.2 us
    ppermute x19, starting transfers between devices: 37.6 us -> 35.2 us  [send(): return lax.ppermute(value, 'seq', pairs)]
    ppermute x6, starting transfers between devices: 3.22 us -> 4.67 us  [across(): lax.ppermute(value, 'head', [(g, g ^ flip) for g in range(head_count)])]
where the time goes in v3:
time: 97.9 us; the launch traced here: 97.5 us
  starting transfers between devices  39.8 us (41%)
  waiting for transfers between devices  39.2 us (40%)
  Pallas kernels  16.4 us (17%)
  local copies, waits for them, and re-layouts  1.63 us (2%)
    ppermute x19, starting transfers between devices, send(): return lax.ppermute(value, 'seq', pairs)  35.2 us
    ppermute x19, waiting for transfers between devices, send(): return lax.ppermute(value, 'seq', pairs)  34.1 us
    pallas_call x5, Pallas kernels, attend(): pl.pallas_call(functools.partial(attend_kernel, kind, per_shard, cluster_...  7.8 us
    ppermute x6, waiting for transfers between devices, across(): lax.ppermute(value, 'head', [(g, g ^ flip) for g in range(head_count)])  5.12 us
    pallas_call x2, Pallas kernels, project(): pl.pallas_call(functools.partial(project_kernel, other), in_specs=[pl.Blo...  5.05 us
    ppermute x6, starting transfers between devices, across(): lax.ppermute(value, 'head', [(g, g ^ flip) for g in range(head_count)])  4.67 us
  transfers between devices with their start and end apart: 25, of which 6 were waited for; matrix products, arithmetic and copies ran while one was open for 0% of the time, Pallas kernels for 12%

profile of v3, /device:TPU:27, one launch (start us, length us, event | category | flops | bytes accessed | tf_op | source)
XLA Modules:
  0.0 97.5 jit_solution(16319718571537407759)
XLA Ops:
  0.0 1.6 %copy.6 = bf16[1024,2,384]{2,0,1:T(8,128)(2,1)S(1)} copy(bf16[1024,2,384]{2,1,0:T(2,128)(2,1)} %param.3) | data formatting | bytes 3145728 | tf_op args[0]
  1.7 1.4 %split_heads.1 = (bf16[1024,128]{1,0:T(8,128)(2,1)S(1)}, bf16[2,1024,128]{2,1,0:T(8,128)(2,1)S(1)}, bf16[1024,128]{1,0:T(8,128)(2,1)S(1)}, bf16[1024,128]{1,0:T(8,128)(2,1)S(1)}, bf16[1024,128]{1,0:T(8,128)(2,1)S(1)}) custom-call(s32[1,3]{1,0:T(1,128)S(1)} %add_bitcast_fusion.ids_ref, bf16[2,1024,384]{2,1,0:T(8,128)(2,1)S(1)} %bitcast.8), custom_call_target="tpu_custom_call" | custom-call | tf_op jit(solution)/shard_map/split_heads/pallas_call | solution.py:180
  3.4 1.2 %collective-permute-start.1 = (bf16[1024,128]{1,0:T(8,128)(2,1)S(1)}, bf16[1024,128]{1,0:T(8,128)(2,1)S(1)}, u32[]{:S(2)}, u32[]{:S(2)}) collective-permute-start(bf16[1024,128]{1,0:T(8,128)(2,1)S(1)} %get-tuple-element.23), channel_id=1, source_target_pairs={{0,4},{4,0},{8,12},{12,8},{16,20},{20,16},{24,28},{28,24},{1,5},{5... | collective-permute-start | bytes 786440 | tf_op jit(solution)/shard_map/ppermute | solution.py:575
  4.9 2.1 %collective-permute-start.7 = (bf16[1024,128]{1,0:T(8,128)(2,1)S(1)}, bf16[1024,128]{1,0:T(8,128)(2,1)S(1)}, u32[]{:S(2)}, u32[]{:S(2)}) collective-permute-start(bf16[1024,128]{1,0:T(8,128)(2,1)S(1)} %get-tuple-element.20.refs_0_), channel_id=1, source_target_pairs={{24,16},{28,20},{25,17},{29,21},{26,18},{30,22},{27,19},{31,23}} | collective-permute-start | bytes 786440 | tf_op jit(solution)/shard_map/ppermute | solution.py:575
  7.0 0.7 collective-permute-start.3
  7.7 2.7 %collective-permute-done.refs_2_.refs_3_ = bf16[1024,128]{1,0:T(8,128)(2,1)S(1)} collective-permute-done((bf16[1024,128]{1,0:T(8,128)(2,1)S(1)}, bf16[1024,128]{1,0:T(8,128)(2,1)S(1)}, u32[]{:S(2)}, u32[]{:S(2)}) %collective-permute-start) | collective-permute-done | bytes 262176 | tf_op jit(solution)/shard_map/ppermute | solution.py:575
  10.4 2.1 %collective-permute-start.8 = (bf16[1024,128]{1,0:T(8,128)(2,1)S(1)}, bf16[1024,128]{1,0:T(8,128)(2,1)S(1)}, u32[]{:S(2)}, u32[]{:S(2)}) collective-permute-start(bf16[1024,128]{1,0:T(8,128)(2,1)S(1)} %collective-permute-done.refs_2_.refs_3_), channel_id=1, source_target_pairs={{24,16},{28,20},{25,17},{29,21},{26,18},{30,22},{27,19},{31,23}} | collective-permute-start | bytes 786440 | tf_op jit(solution)/shard_map/ppermute | solution.py:575
  12.5 3.5 %collective-permute-done.1.refs_3_.refs_4_ = bf16[1024,128]{1,0:T(8,128)(2,1)S(1)} collective-permute-done((bf16[1024,128]{1,0:T(8,128)(2,1)S(1)}, bf16[1024,128]{1,0:T(8,128)(2,1)S(1)}, u32[]{:S(2)}, u32[]{:S(2)}) %collective-permute-start.1) | collective-permute-done | bytes 262176 | tf_op jit(solution)/shard_map/ppermute | solution.py:575
  16.0 2.0 %collective-permute-start.19 = (bf16[1024,128]{1,0:T(8,128)(2,1)S(1)}, bf16[1024,128]{1,0:T(8,128)(2,1)S(1)}, u32[]{:S(2)}, u32[]{:S(2)}) collective-permute-start(bf16[1024,128]{1,0:T(8,128)(2,1)S(1)} %get-tuple-element.20.refs_0_), channel_id=1, source_target_pairs={{24,8},{28,12},{25,9},{29,13},{26,10},{30,14},{27,11},{31,15}} | collective-permute-start | bytes 786440 | tf_op jit(solution)/shard_map/ppermute | solution.py:575
  18.0 3.6 %collective-permute-done.2.refs_4_.refs_5_ = bf16[1024,128]{1,0:T(8,128)(2,1)S(1)} collective-permute-done((bf16[1024,128]{1,0:T(8,128)(2,1)S(1)}, bf16[1024,128]{1,0:T(8,128)(2,1)S(1)}, u32[]{:S(2)}, u32[]{:S(2)}) %collective-permute-start.2) | collective-permute-done | bytes 262176 | tf_op jit(solution)/shard_map/ppermute | solution.py:575
  23.7 0.7 block_tables.1.tab
  24.4 0.7 shard_map.38
  25.2 1.3 %collective-permute-start.17 = (bf16[1056,128]{1,0:T(8,128)(2,1)S(1)}, bf16[1056,128]{1,0:T(8,128)(2,1)S(1)}, u32[]{:S(2)}, u32[]{:S(2)}) collective-permute-start(bf16[1056,128]{1,0:T(8,128)(2,1)S(1)} %get-tuple-element.30), channel_id=1, source_target_pairs={{16,24},{20,28},{17,25},{21,29},{18,26},{22,30},{19,27},{23,31}} | collective-permute-start | bytes 811016 | tf_op jit(solution)/shard_map/ppermute | solution.py:575
  26.5 0.7 shard_map.40
  27.3 0.7 shard_map.41
  28.7 16.3 %collective-permute-start.11 = (bf16[1024,128]{1,0:T(8,128)(2,1)S(1)}, bf16[1024,128]{1,0:T(8,128)(2,1)S(1)}, u32[]{:S(2)}, u32[]{:S(2)}) collective-permute-start(bf16[1024,128]{1,0:T(8,128)(2,1)S(1)} %collective-permute-done.refs_2_.refs_3_), channel_id=1, source_target_pairs={{24,8},{28,12},{25,9},{29,13},{26,10},{30,14},{27,11},{31,15}} | collective-permute-start | bytes 786440 | tf_op jit(solution)/shard_map/ppermute | solution.py:575
  45.7 1.3 %collective-permute-start.9 = (bf16[1056,128]{1,0:T(8,128)(2,1)S(1)}, bf16[1056,128]{1,0:T(8,128)(2,1)S(1)}, u32[]{:S(2)}, u32[]{:S(2)}) collective-permute-start(bf16[1056,128]{1,0:T(8,128)(2,1)S(1)} %get-tuple-element.26), channel_id=1, source_target_pairs={{16,28},{20,24},{17,29},{21,25},{18,30},{22,26},{19,31},{23,27}} | collective-permute-start | bytes 811016 | tf_op jit(solution)/shard_map/ppermute | solution.py:575
  47.0 4.6 %shard_map.37 = (bf16[1056,128]{1,0:T(8,128)(2,1)S(1)}, bf16[1056,128]{1,0:T(8,128)(2,1)S(1)}) custom-call(s32[24,128]{1,0:T(8,128)S(1)} %block_tables.1.tab, bf16[1024,128]{1,0:T(8,128)(2,1)S(1)} %get-tuple-element.20.refs_0_, bf16[2,1024,128]{2,1,0:T(8,128)(2,1)S(1)} %get-tuple-element.21.refs_1_.refs_2_, ...), custom_call_target="tpu_custom_call" | custom-call | tf_op jit(solution)/shard_map/pallas_call | solution.py:465
  51.6 0.9 collective-permute-start.6
  52.5 1.4 %collective-permute-start.21 = (bf16[1056,128]{1,0:T(8,128)(2,1)S(1)}, bf16[1056,128]{1,0:T(8,128)(2,1)S(1)}, u32[]{:S(2)}, u32[]{:S(2)}) collective-permute-start(bf16[1056,128]{1,0:T(8,128)(2,1)S(1)} %get-tuple-element.34), channel_id=1, source_target_pairs={{8,24},{12,28},{9,25},{13,29},{10,26},{14,30},{11,27},{15,31}} | collective-permute-start | bytes 811016 | tf_op jit(solution)/shard_map/ppermute | solution.py:575
  53.9 1.0 shard_map.39
  55.6 1.3 %collective-permute-start.13 = (bf16[1056,128]{1,0:T(8,128)(2,1)S(1)}, bf16[1056,128]{1,0:T(8,128)(2,1)S(1)}, u32[]{:S(2)}, u32[]{:S(2)}) collective-permute-start(bf16[1056,128]{1,0:T(8,128)(2,1)S(1)} %get-tuple-element.28), channel_id=1, source_target_pairs={{8,28},{12,24},{9,29},{13,25},{10,30},{14,26},{11,31},{15,27}} | collective-permute-start | bytes 811016 | tf_op jit(solution)/shard_map/ppermute | solution.py:575
  56.9 10.6 %collective-permute-done.21.third = bf16[1056,128]{1,0:T(8,128)(2,1)S(1)} collective-permute-done((bf16[1056,128]{1,0:T(8,128)(2,1)S(1)}, bf16[1056,128]{1,0:T(8,128)(2,1)S(1)}, u32[]{:S(2)}, u32[]{:S(2)}) %collective-permute-start.21) | collective-permute-done | bytes 270368 | tf_op jit(solution)/shard_map/ppermute | solution.py:575
  67.5 0.7 combine.3.refs_0_
  68.3 1.0 %collective-permute-start.23 = (bf16[128,1024]{1,0:T(8,128)(2,1)S(1)}, bf16[128,1024]{1,0:T(8,128)(2,1)S(1)}, u32[]{:S(2)}, u32[]{:S(2)}) collective-permute-start(bf16[128,1024]{1,0:T(8,128)(2,1)S(1)} %combine.3.refs_0_), channel_id=1, source_target_pairs={{0,2},{1,3},{2,0},{3,1},{4,6},{5,7},{6,4},{7,5},{8,10},{9,11},{10,... | collective-permute-start | bytes 786440 | tf_op jit(solution)/shard_map/ppermute | solution.py:578
  69.3 13.6 %collective-permute-done.13.third = bf16[1056,128]{1,0:T(8,128)(2,1)S(1)} collective-permute-done((bf16[1056,128]{1,0:T(8,128)(2,1)S(1)}, bf16[1056,128]{1,0:T(8,128)(2,1)S(1)}, u32[]{:S(2)}, u32[]{:S(2)}) %collective-permute-start.13) | collective-permute-done | bytes 270368 | tf_op jit(solution)/shard_map/ppermute | solution.py:575
  82.9 0.7 combine.2.refs_0_
  84.1 1.3 %collective-permute-start.22 = (bf16[128,1024]{1,0:T(8,128)(2,1)S(1)}, bf16[128,1024]{1,0:T(8,128)(2,1)S(1)}, u32[]{:S(2)}, u32[]{:S(2)}) collective-permute-start(bf16[128,1024]{1,0:T(8,128)(2,1)S(1)} %combine.3.refs_0_), channel_id=1, source_target_pairs={{0,1},{1,0},{2,3},{3,2},{4,5},{5,4},{6,7},{7,6},{8,9},{9,8},{10,11... | collective-permute-start | bytes 786440 | tf_op jit(solution)/shard_map/ppermute | solution.py:578
  85.9 5.1 %collective-permute-done.15.refs_2_ = bf16[128,1024]{1,0:T(8,128)(2,1)S(1)} collective-permute-done((bf16[128,1024]{1,0:T(8,128)(2,1)S(1)}, bf16[128,1024]{1,0:T(8,128)(2,1)S(1)}, u32[]{:S(2)}, u32[]{:S(2)}) %collective-permute-start.15) | collective-permute-done | bytes 262176 | tf_op jit(solution)/shard_map/ppermute | solution.py:578
  91.0 1.4 %collective-permute-start.16 = (bf16[128,1024]{1,0:T(8,128)(2,1)S(1)}, bf16[128,1024]{1,0:T(8,128)(2,1)S(1)}, u32[]{:S(2)}, u32[]{:S(2)}) collective-permute-start(bf16[128,1024]{1,0:T(8,128)(2,1)S(1)} %collective-permute-done.15.refs_2_), channel_id=1, source_target_pairs={{0,1},{1,0},{2,3},{3,2},{4,5},{5,4},{6,7},{7,6},{8,9},{9,8},{10,11... | collective-permute-start | bytes 786440 | tf_op jit(solution)/shard_map/ppermute | solution.py:578
  92.4 1.8 %project.2.refs_4_ = f32[1024,1024]{1,0:T(8,128)S(1)} custom-call(s32[1,3]{1,0:T(1,128)S(1)} %add_bitcast_fusion.ids_ref, bf16[1024,1024]{1,0:T(8,128)(2,1)S(1)} %copy-done, bf16[128,1024]{1,0:T(8,128)(2,1)S(1)} %combine.3.refs_0_, bf16[128,1024]{1,0:T(8,128)(2,1)S(1)} %collective-permute-done.22.refs_1_, ...), custom_call_target="tpu_custom_call" | custom-call | tf_op jit(solution)/shard_map/project/pallas_call | solution.py:548
  94.3 3.2 %project.3 = bf16[1024,1024]{1,0:T(8,128)(2,1)} custom-call(s32[1,3]{1,0:T(1,128)S(1)} %add_bitcast_fusion.ids_ref, bf16[1024,1024]{1,0:T(8,128)(2,1)S(1)} %copy-done, bf16[128,1024]{1,0:T(8,128)(2,1)S(1)} %combine.2.refs_0_, bf16[128,1024]{1,0:T(8,128)(2,1)S(1)} %collective-permute-done.14.refs_1_, bf16[128,1024]{1,0:T(8,128)(2,1)S(1)} %collective-permute-done.15.refs_2_, ...), custom_call_target="tpu_custom_call" | custom-call | tf_op jit(solution)/shard_map/project/pallas_call | solution.py:548
  (35 shorter events, 5.7 us)
Async XLA Ops:
  0.0 23.7 %copy-start.1 = (s32[2,64]{1,0:T(2,128)S(1)}, s32[2,64]{1,0:T(2,128)}, u32[]{:S(2)}) copy-start(s32[2,64]{1,0:T(2,128)} %table_ref.1) | copy-start | bytes 1540
  3.1 7.3 %collective-permute-start = (bf16[1024,128]{1,0:T(8,128)(2,1)S(1)}, bf16[1024,128]{1,0:T(8,128)(2,1)S(1)}, u32[]{:S(2)}, u32[]{:S(2)}) collective-permute-start(bf16[1024,128]{1,0:T(8,128)(2,1)S(1)} %get-tuple-element.22), channel_id=1, source_target_pairs={{0,4},{4,0},{8,12},{12,8},{16,20},{20,16},{24,28},{28,24},{1,5},{5... | collective-permute-start | bytes 786440 | tf_op jit(solution)/shard_map/ppermute | solution.py:575
  3.4 12.6 %collective-permute-start.1 = (bf16[1024,128]{1,0:T(8,128)(2,1)S(1)}, bf16[1024,128]{1,0:T(8,128)(2,1)S(1)}, u32[]{:S(2)}, u32[]{:S(2)}) collective-permute-start(bf16[1024,128]{1,0:T(8,128)(2,1)S(1)} %get-tuple-element.23), channel_id=1, source_target_pairs={{0,4},{4,0},{8,12},{12,8},{16,20},{20,16},{24,28},{28,24},{1,5},{5... | collective-permute-start | bytes 786440 | tf_op jit(solution)/shard_map/ppermute | solution.py:575
  4.6 17.0 %collective-permute-start.2 = (bf16[1024,128]{1,0:T(8,128)(2,1)S(1)}, bf16[1024,128]{1,0:T(8,128)(2,1)S(1)}, u32[]{:S(2)}, u32[]{:S(2)}) collective-permute-start(bf16[1024,128]{1,0:T(8,128)(2,1)S(1)} %get-tuple-element.24), channel_id=1, source_target_pairs={{0,4},{4,0},{8,12},{12,8},{16,20},{20,16},{24,28},{28,24},{1,5},{5... | collective-permute-start | bytes 786440 | tf_op jit(solution)/shard_map/ppermute | solution.py:575
  4.9 17.4 %collective-permute-start.7 = (bf16[1024,128]{1,0:T(8,128)(2,1)S(1)}, bf16[1024,128]{1,0:T(8,128)(2,1)S(1)}, u32[]{:S(2)}, u32[]{:S(2)}) collective-permute-start(bf16[1024,128]{1,0:T(8,128)(2,1)S(1)} %get-tuple-element.20.refs_0_), channel_id=1, source_target_pairs={{24,16},{28,20},{25,17},{29,21},{26,18},{30,22},{27,19},{31,23}} | collective-permute-start | bytes 786440 | tf_op jit(solution)/shard_map/ppermute | solution.py:575
  7.0 19.5 %collective-permute-start.3 = (bf16[2,1024,128]{2,1,0:T(8,128)(2,1)S(1)}, bf16[2,1024,128]{2,1,0:T(8,128)(2,1)S(1)}, u32[]{:S(2)}, u32[]{:S(2)}) collective-permute-start(bf16[2,1024,128]{2,1,0:T(8,128)(2,1)S(1)} %get-tuple-element.21.refs_1_.refs_2_), channel_id=1, source_target_pairs={{0,8},{4,12},{1,9},{5,13},{2,10},{6,14},{3,11},{7,15}} | collective-permute-start | bytes 1572872 | tf_op jit(solution)/shard_map/ppermute | solution.py:575
  10.4 12.6 %collective-permute-start.8 = (bf16[1024,128]{1,0:T(8,128)(2,1)S(1)}, bf16[1024,128]{1,0:T(8,128)(2,1)S(1)}, u32[]{:S(2)}, u32[]{:S(2)}) collective-permute-start(bf16[1024,128]{1,0:T(8,128)(2,1)S(1)} %collective-permute-done.refs_2_.refs_3_), channel_id=1, source_target_pairs={{24,16},{28,20},{25,17},{29,21},{26,18},{30,22},{27,19},{31,23}} | collective-permute-start | bytes 786440 | tf_op jit(solution)/shard_map/ppermute | solution.py:575
  16.0 9.2 %collective-permute-start.19 = (bf16[1024,128]{1,0:T(8,128)(2,1)S(1)}, bf16[1024,128]{1,0:T(8,128)(2,1)S(1)}, u32[]{:S(2)}, u32[]{:S(2)}) collective-permute-start(bf16[1024,128]{1,0:T(8,128)(2,1)S(1)} %get-tuple-element.20.refs_0_), channel_id=1, source_target_pairs={{24,8},{28,12},{25,9},{29,13},{26,10},{30,14},{27,11},{31,15}} | collective-permute-start | bytes 786440 | tf_op jit(solution)/shard_map/ppermute | solution.py:575
  21.6 4.9 %collective-permute-start.18 = (bf16[1024,128]{1,0:T(8,128)(2,1)S(1)}, bf16[1024,128]{1,0:T(8,128)(2,1)S(1)}, u32[]{:S(2)}, u32[]{:S(2)}) collective-permute-start(bf16[1024,128]{1,0:T(8,128)(2,1)S(1)} %get-tuple-element.20.refs_0_), channel_id=1, source_target_pairs={{16,8},{20,12},{17,9},{21,13},{18,10},{22,14},{19,11},{23,15}} | collective-permute-start | bytes 786440 | tf_op jit(solution)/shard_map/ppermute | solution.py:575
  22.3 5.0 %collective-permute-start.4 = (bf16[1024,128]{1,0:T(8,128)(2,1)S(1)}, bf16[1024,128]{1,0:T(8,128)(2,1)S(1)}, u32[]{:S(2)}, u32[]{:S(2)}) collective-permute-start(bf16[1024,128]{1,0:T(8,128)(2,1)S(1)} %collective-permute-done.refs_2_.refs_3_), channel_id=1, source_target_pairs={{0,8},{4,12},{1,9},{5,13},{2,10},{6,14},{3,11},{7,15}} | collective-permute-start | bytes 786440 | tf_op jit(solution)/shard_map/ppermute | solution.py:575
  23.0 4.3 %collective-permute-start.5 = (bf16[1024,128]{1,0:T(8,128)(2,1)S(1)}, bf16[1024,128]{1,0:T(8,128)(2,1)S(1)}, u32[]{:S(2)}, u32[]{:S(2)}) collective-permute-start(bf16[1024,128]{1,0:T(8,128)(2,1)S(1)} %collective-permute-done.1.refs_3_.refs_4_), channel_id=1, source_target_pairs={{0,8},{4,12},{1,9},{5,13},{2,10},{6,14},{3,11},{7,15}} | collective-permute-start | bytes 786440 | tf_op jit(solution)/shard_map/ppermute | solution.py:575
  25.2 29.8 %collective-permute-start.17 = (bf16[1056,128]{1,0:T(8,128)(2,1)S(1)}, bf16[1056,128]{1,0:T(8,128)(2,1)S(1)}, u32[]{:S(2)}, u32[]{:S(2)}) collective-permute-start(bf16[1056,128]{1,0:T(8,128)(2,1)S(1)} %get-tuple-element.30), channel_id=1, source_target_pairs={{16,24},{20,28},{17,25},{21,29},{18,26},{22,30},{19,27},{23,31}} | collective-permute-start | bytes 811016 | tf_op jit(solution)/shard_map/ppermute | solution.py:575
  28.0 27.6 %collective-permute-start.20 = (bf16[1056,128]{1,0:T(8,128)(2,1)S(1)}, bf16[1056,128]{1,0:T(8,128)(2,1)S(1)}, u32[]{:S(2)}, u32[]{:S(2)}) collective-permute-start(bf16[1056,128]{1,0:T(8,128)(2,1)S(1)} %get-tuple-element.33), channel_id=1, source_target_pairs={{8,16},{12,20},{9,17},{13,21},{10,18},{14,22},{11,19},{15,23}} | collective-permute-start | bytes 811016 | tf_op jit(solution)/shard_map/ppermute | solution.py:575
  28.7 22.9 %collective-permute-start.11 = (bf16[1024,128]{1,0:T(8,128)(2,1)S(1)}, bf16[1024,128]{1,0:T(8,128)(2,1)S(1)}, u32[]{:S(2)}, u32[]{:S(2)}) collective-permute-start(bf16[1024,128]{1,0:T(8,128)(2,1)S(1)} %collective-permute-done.refs_2_.refs_3_), channel_id=1, source_target_pairs={{24,8},{28,12},{25,9},{29,13},{26,10},{30,14},{27,11},{31,15}} | collective-permute-start | bytes 786440 | tf_op jit(solution)/shard_map/ppermute | solution.py:575
  45.0 7.5 %collective-permute-start.10 = (bf16[1024,128]{1,0:T(8,128)(2,1)S(1)}, bf16[1024,128]{1,0:T(8,128)(2,1)S(1)}, u32[]{:S(2)}, u32[]{:S(2)}) collective-permute-start(bf16[1024,128]{1,0:T(8,128)(2,1)S(1)} %collective-permute-done.refs_2_.refs_3_), channel_id=1, source_target_pairs={{16,8},{20,12},{17,9},{21,13},{18,10},{22,14},{19,11},{23,15}} | collective-permute-start | bytes 786440 | tf_op jit(solution)/shard_map/ppermute | solution.py:575
  45.7 23.5 %collective-permute-start.9 = (bf16[1056,128]{1,0:T(8,128)(2,1)S(1)}, bf16[1056,128]{1,0:T(8,128)(2,1)S(1)}, u32[]{:S(2)}, u32[]{:S(2)}) collective-permute-start(bf16[1056,128]{1,0:T(8,128)(2,1)S(1)} %get-tuple-element.26), channel_id=1, source_target_pairs={{16,28},{20,24},{17,29},{21,25},{18,30},{22,26},{19,31},{23,27}} | collective-permute-start | bytes 811016 | tf_op jit(solution)/shard_map/ppermute | solution.py:575
  51.6 17.6 %collective-permute-start.6 = (bf16[1056,128]{1,0:T(8,128)(2,1)S(1)}, bf16[1056,128]{1,0:T(8,128)(2,1)S(1)}, u32[]{:S(2)}, u32[]{:S(2)}) collective-permute-start(bf16[1056,128]{1,0:T(8,128)(2,1)S(1)} %get-tuple-element.25), channel_id=1, source_target_pairs={{0,4},{4,0},{8,12},{12,8},{16,20},{20,16},{24,28},{28,24},{1,5},{5... | collective-permute-start | bytes 811016 | tf_op jit(solution)/shard_map/ppermute | solution.py:575
  52.5 39.9 %copy-start = (bf16[1024,1024]{1,0:T(8,128)(2,1)S(1)}, bf16[1024,1024]{1,0:T(8,128)(2,1)}, u32[]{:S(2)}) copy-start(bf16[1024,1024]{1,0:T(8,128)(2,1)} %weight_ref.3) | copy-start | bytes 6291460
  52.5 15.0 %collective-permute-start.21 = (bf16[1056,128]{1,0:T(8,128)(2,1)S(1)}, bf16[1056,128]{1,0:T(8,128)(2,1)S(1)}, u32[]{:S(2)}, u32[]{:S(2)}) collective-permute-start(bf16[1056,128]{1,0:T(8,128)(2,1)S(1)} %get-tuple-element.34), channel_id=1, source_target_pairs={{8,24},{12,28},{9,25},{13,29},{10,26},{14,30},{11,27},{15,31}} | collective-permute-start | bytes 811016 | tf_op jit(solution)/shard_map/ppermute | solution.py:575
  54.9 14.3 %collective-permute-start.12 = (bf16[1056,128]{1,0:T(8,128)(2,1)S(1)}, bf16[1056,128]{1,0:T(8,128)(2,1)S(1)}, u32[]{:S(2)}, u32[]{:S(2)}) collective-permute-start(bf16[1056,128]{1,0:T(8,128)(2,1)S(1)} %get-tuple-element.27), channel_id=1, source_target_pairs={{8,20},{12,16},{9,21},{13,17},{10,22},{14,18},{11,23},{15,19}} | collective-permute-start | bytes 811016 | tf_op jit(solution)/shard_map/ppermute | solution.py:575
  55.6 27.3 %collective-permute-start.13 = (bf16[1056,128]{1,0:T(8,128)(2,1)S(1)}, bf16[1056,128]{1,0:T(8,128)(2,1)S(1)}, u32[]{:S(2)}, u32[]{:S(2)}) collective-permute-start(bf16[1056,128]{1,0:T(8,128)(2,1)S(1)} %get-tuple-element.28), channel_id=1, source_target_pairs={{8,28},{12,24},{9,29},{13,25},{10,30},{14,26},{11,31},{15,27}} | collective-permute-start | bytes 811016 | tf_op jit(solution)/shard_map/ppermute | solution.py:575
  68.3 17.1 %collective-permute-start.23 = (bf16[128,1024]{1,0:T(8,128)(2,1)S(1)}, bf16[128,1024]{1,0:T(8,128)(2,1)S(1)}, u32[]{:S(2)}, u32[]{:S(2)}) collective-permute-start(bf16[128,1024]{1,0:T(8,128)(2,1)S(1)} %combine.3.refs_0_), channel_id=1, source_target_pairs={{0,2},{1,3},{2,0},{3,1},{4,6},{5,7},{6,4},{7,5},{8,10},{9,11},{10,... | collective-permute-start | bytes 786440 | tf_op jit(solution)/shard_map/ppermute | solution.py:578
  83.6 7.4 %collective-permute-start.15 = (bf16[128,1024]{1,0:T(8,128)(2,1)S(1)}, bf16[128,1024]{1,0:T(8,128)(2,1)S(1)}, u32[]{:S(2)}, u32[]{:S(2)}) collective-permute-start(bf16[128,1024]{1,0:T(8,128)(2,1)S(1)} %combine.2.refs_0_), channel_id=1, source_target_pairs={{0,2},{1,3},{2,0},{3,1},{4,6},{5,7},{6,4},{7,5},{8,10},{9,11},{10,... | collective-permute-start | bytes 786440 | tf_op jit(solution)/shard_map/ppermute | solution.py:578
  84.1 8.4 %collective-permute-start.22 = (bf16[128,1024]{1,0:T(8,128)(2,1)S(1)}, bf16[128,1024]{1,0:T(8,128)(2,1)S(1)}, u32[]{:S(2)}, u32[]{:S(2)}) collective-permute-start(bf16[128,1024]{1,0:T(8,128)(2,1)S(1)} %combine.3.refs_0_), channel_id=1, source_target_pairs={{0,1},{1,0},{2,3},{3,2},{4,5},{5,4},{6,7},{7,6},{8,9},{9,8},{10,11... | collective-permute-start | bytes 786440 | tf_op jit(solution)/shard_map/ppermute | solution.py:578
  85.4 7.0 %collective-permute-start.24 = (bf16[128,1024]{1,0:T(8,128)(2,1)S(1)}, bf16[128,1024]{1,0:T(8,128)(2,1)S(1)}, u32[]{:S(2)}, u32[]{:S(2)}) collective-permute-start(bf16[128,1024]{1,0:T(8,128)(2,1)S(1)} %collective-permute-done.23.refs_2_), channel_id=1, source_target_pairs={{0,1},{1,0},{2,3},{3,2},{4,5},{5,4},{6,7},{7,6},{8,9},{9,8},{10,11... | collective-permute-start | bytes 786440 | tf_op jit(solution)/shard_map/ppermute | solution.py:578
  85.4 8.9 %collective-permute-start.14 = (bf16[128,1024]{1,0:T(8,128)(2,1)S(1)}, bf16[128,1024]{1,0:T(8,128)(2,1)S(1)}, u32[]{:S(2)}, u32[]{:S(2)}) collective-permute-start(bf16[128,1024]{1,0:T(8,128)(2,1)S(1)} %combine.2.refs_0_), channel_id=1, source_target_pairs={{0,1},{1,0},{2,3},{3,2},{4,5},{5,4},{6,7},{7,6},{8,9},{9,8},{10,11... | collective-permute-start | bytes 786440 | tf_op jit(solution)/shard_map/ppermute | solution.py:578
  91.0 3.3 %collective-permute-start.16 = (bf16[128,1024]{1,0:T(8,128)(2,1)S(1)}, bf16[128,1024]{1,0:T(8,128)(2,1)S(1)}, u32[]{:S(2)}, u32[]{:S(2)}) collective-permute-start(bf16[128,1024]{1,0:T(8,128)(2,1)S(1)} %collective-permute-done.15.refs_2_), channel_id=1, source_target_pairs={{0,1},{1,0},{2,3},{3,2},{4,5},{5,4},{6,7},{7,6},{8,9},{9,8},{10,11... | collective-permute-start | bytes 786440 | tf_op jit(solution)/shard_map/ppermute | solution.py:578

commit v4 on v3

--- a/solution.py
+++ b/solution.py
@@ -517,41 +517,44 @@
     )(ids, *values)
 
 
-def project_kernel(other, ids_ref, weight_ref, *refs):
+def project_kernel(other, which, ids_ref, weight_ref, *refs):
     group = ids_ref[0, 2]
     column = ids_ref[0, 0]
     head = 1 - column if other else column
     out_ref = refs[-1]
-    features = refs[:4]
-    given = refs[4] if len(refs) == 6 else None
-    depth, rows = features[0].shape
-    lines = [pl.ds(pl.multiple_of(((group ^ j) * 2 + head) * depth, depth), depth) for j in range(4)]
-    chunk = 256
-    for line in range(0, rows, chunk):
-        left = jnp.concatenate([f[:, line : line + chunk] for f in features], axis=0)
-        for col in range(0, out_ref.shape[1], 2 * chunk):
-            cols = slice(col, col + 2 * chunk)
-            right = jnp.concatenate([weight_ref[at, cols] for at in lines], axis=0)
-            acc = lax.dot_general(
-                left, right, (((0,), (0,)), ((), ())), preferred_element_type=jnp.float32
-            )
-            if given is not None:
-                acc = acc + given[line : line + chunk, cols]
-            out_ref[line : line + chunk, cols] = acc.astype(out_ref.dtype)
-
-
-def project(other, ids, weight, features, given):
+    features = refs[: len(which)]
+    given = refs[len(which)] if len(refs) > len(which) + 1 else None
+    depth = features[0].shape[0]
+    rows = out_ref.shape[0]
+    first = pl.program_id(0) * rows
+    lines = [pl.ds(pl.multiple_of(((group ^ j) * 2 + head) * depth, depth), depth) for j in which]
+    here = pl.ds(pl.multiple_of(first, rows), rows)
+    left = jnp.concatenate([f[:, here] for f in features], axis=0)
+    chunk = 512
+    for col in range(0, out_ref.shape[1], chunk):
+        cols = slice(col, col + chunk)
+        right = jnp.concatenate([weight_ref[at, cols] for at in lines], axis=0)
+        acc = lax.dot_general(
+            left, right, (((0,), (0,)), ((), ())), preferred_element_type=jnp.float32
+        )
+        if given is not None:
+            acc = acc + given[here, cols]
+        out_ref[:, cols] = acc.astype(out_ref.dtype)
+
+
+def project(other, final, which, ids, weight, features, given):
     rows = features[0].shape[1]
+    step = rows // 4
     vmem = pl.BlockSpec(memory_space=pltpu.VMEM)
     given = [] if given is None else [given]
-    last = bool(given)
+    width = weight.shape[1]
     return pl.pallas_call(
-        functools.partial(project_kernel, other),
-        in_specs=[pl.BlockSpec(memory_space=pltpu.SMEM)] + [vmem] * (5 + len(given)),
-        out_specs=vmem,
-        out_shape=jax.ShapeDtypeStruct(
-            (rows, weight.shape[1]), jnp.bfloat16 if last else jnp.float32
-        ),
+        functools.partial(project_kernel, other, which),
+        grid=(rows // step,),
+        in_specs=[pl.BlockSpec(memory_space=pltpu.SMEM)]
+        + [vmem] * (1 + len(features) + len(given)),
+        out_specs=pl.BlockSpec((step, width), lambda i: (i, 0)),
+        out_shape=jax.ShapeDtypeStruct((rows, width), jnp.bfloat16 if final else jnp.float32),
         compiler_params=pltpu.CompilerParams(vmem_limit_bytes=VMEM_BYTES),
         name="project",
     )(ids, weight, *features, *given)
@@ -628,7 +631,14 @@
         over = across(local, half)
         beside = across(local, 1)
         over_beside = across(over, 1)
-        out = project(part == 1, ids, out_weight, (local, beside, over, over_beside), out)
+        if part == 0:
+            out = project(
+                False, False, (0, 1, 2, 3), ids, out_weight,
+                (local, beside, over, over_beside), None,
+            )
+        else:
+            out = project(True, False, (0, 1), ids, out_weight, (local, beside), out)
+            out = project(True, True, (2, 3), ids, out_weight, (over, over_beside), out)
     return out
 
 

time: 97.9 us -> 92.4 us (0.944)
  the two profiles are of different devices: /device:TPU:27 before, /device:TPU:13 now
where the time goes in v4:
time: 92.4 us; the launch traced here: 92 us
  starting transfers between devices  33.4 us (36%)
  Pallas kernels  32.9 us (36%)
  waiting for transfers between devices  23.7 us (26%)
  local copies, waits for them, and re-layouts  1.63 us (2%)
    ppermute x19, waiting for transfers between devices, send(): return lax.ppermute(value, 'seq', pairs)  23.7 us
    pallas_call x5, Pallas kernels, attend(): pl.pallas_call(functools.partial(attend_kernel, kind, per_shard, cluster_...  21.7 us
    ppermute x19, starting transfers between devices, send(): return lax.ppermute(value, 'seq', pairs)  21.2 us
    ppermute x6, starting transfers between devices, across(): lax.ppermute(value, 'head', [(g, g ^ flip) for g in range(head_count)])  12.2 us
    pallas_call x3, Pallas kernels, project(): pl.pallas_call(functools.partial(project_kernel, other, which), grid=(row...  7.61 us
  transfers between devices with their start and end apart: 25, of which 6 were waited for; matrix products, arithmetic and copies ran while one was open for 0% of the time, Pallas kernels for 31%

profile of v4, /device:TPU:13, one launch (start us, length us, event | category | flops | bytes accessed | tf_op | source)
XLA Modules:
  0.0 92.0 jit_solution(2503293175640725414)
XLA Ops:
  0.0 1.6 %copy.6 = bf16[1024,2,384]{2,0,1:T(8,128)(2,1)S(1)} copy(bf16[1024,2,384]{2,1,0:T(2,128)(2,1)} %param.3) | data formatting | bytes 3145728 | tf_op args[0]
  1.7 1.4 %split_heads.1 = (bf16[1024,128]{1,0:T(8,128)(2,1)S(1)}, bf16[2,1024,128]{2,1,0:T(8,128)(2,1)S(1)}, bf16[1024,128]{1,0:T(8,128)(2,1)S(1)}, bf16[1024,128]{1,0:T(8,128)(2,1)S(1)}, bf16[1024,128]{1,0:T(8,128)(2,1)S(1)}) custom-call(s32[1,3]{1,0:T(1,128)S(1)} %add_bitcast_fusion.ids_ref, bf16[2,1024,384]{2,1,0:T(8,128)(2,1)S(1)} %bitcast.8), custom_call_target="tpu_custom_call" | custom-call | tf_op jit(solution)/shard_map/split_heads/pallas_call | solution.py:180
  3.1 1.3 %collective-permute-start = (bf16[1024,128]{1,0:T(8,128)(2,1)S(1)}, bf16[1024,128]{1,0:T(8,128)(2,1)S(1)}, u32[]{:S(2)}, u32[]{:S(2)}) collective-permute-start(bf16[1024,128]{1,0:T(8,128)(2,1)S(1)} %get-tuple-element.22), channel_id=1, source_target_pairs={{0,4},{4,0},{8,12},{12,8},{16,20},{20,16},{24,28},{28,24},{1,5},{5... | collective-permute-start | bytes 786440 | tf_op jit(solution)/shard_map/ppermute | solution.py:578
  4.4 1.3 %collective-permute-start.3 = (bf16[2,1024,128]{2,1,0:T(8,128)(2,1)S(1)}, bf16[2,1024,128]{2,1,0:T(8,128)(2,1)S(1)}, u32[]{:S(2)}, u32[]{:S(2)}) collective-permute-start(bf16[2,1024,128]{2,1,0:T(8,128)(2,1)S(1)} %get-tuple-element.21.refs_1_.refs_2_), channel_id=1, source_target_pairs={{0,8},{4,12},{1,9},{5,13},{2,10},{6,14},{3,11},{7,15}} | collective-permute-start | bytes 1572872 | tf_op jit(solution)/shard_map/ppermute | solution.py:578
  6.0 1.3 %collective-permute-start.18 = (bf16[1024,128]{1,0:T(8,128)(2,1)S(1)}, bf16[1024,128]{1,0:T(8,128)(2,1)S(1)}, u32[]{:S(2)}, u32[]{:S(2)}) collective-permute-start(bf16[1024,128]{1,0:T(8,128)(2,1)S(1)} %get-tuple-element.20.refs_0_), channel_id=1, source_target_pairs={{16,8},{20,12},{17,9},{21,13},{18,10},{22,14},{19,11},{23,15}} | collective-permute-start | bytes 786440 | tf_op jit(solution)/shard_map/ppermute | solution.py:578
  7.3 1.3 %collective-permute-start.19 = (bf16[1024,128]{1,0:T(8,128)(2,1)S(1)}, bf16[1024,128]{1,0:T(8,128)(2,1)S(1)}, u32[]{:S(2)}, u32[]{:S(2)}) collective-permute-start(bf16[1024,128]{1,0:T(8,128)(2,1)S(1)} %get-tuple-element.20.refs_0_), channel_id=1, source_target_pairs={{24,8},{28,12},{25,9},{29,13},{26,10},{30,14},{27,11},{31,15}} | collective-permute-start | bytes 786440 | tf_op jit(solution)/shard_map/ppermute | solution.py:578
  8.6 1.8 %collective-permute-done.refs_2_.refs_3_ = bf16[1024,128]{1,0:T(8,128)(2,1)S(1)} collective-permute-done((bf16[1024,128]{1,0:T(8,128)(2,1)S(1)}, bf16[1024,128]{1,0:T(8,128)(2,1)S(1)}, u32[]{:S(2)}, u32[]{:S(2)}) %collective-permute-start) | collective-permute-done | bytes 262176 | tf_op jit(solution)/shard_map/ppermute | solution.py:578
  11.6 4.4 %collective-permute-done.1.refs_3_.refs_4_ = bf16[1024,128]{1,0:T(8,128)(2,1)S(1)} collective-permute-done((bf16[1024,128]{1,0:T(8,128)(2,1)S(1)}, bf16[1024,128]{1,0:T(8,128)(2,1)S(1)}, u32[]{:S(2)}, u32[]{:S(2)}) %collective-permute-start.1) | collective-permute-done | bytes 262176 | tf_op jit(solution)/shard_map/ppermute | solution.py:578
  16.0 1.3 %collective-permute-start.4 = (bf16[1024,128]{1,0:T(8,128)(2,1)S(1)}, bf16[1024,128]{1,0:T(8,128)(2,1)S(1)}, u32[]{:S(2)}, u32[]{:S(2)}) collective-permute-start(bf16[1024,128]{1,0:T(8,128)(2,1)S(1)} %collective-permute-done.refs_2_.refs_3_), channel_id=1, source_target_pairs={{0,8},{4,12},{1,9},{5,13},{2,10},{6,14},{3,11},{7,15}} | collective-permute-start | bytes 786440 | tf_op jit(solution)/shard_map/ppermute | solution.py:578
  17.3 2.8 %collective-permute-done.18.refs_0_ = bf16[1024,128]{1,0:T(8,128)(2,1)S(1)} collective-permute-done((bf16[1024,128]{1,0:T(8,128)(2,1)S(1)}, bf16[1024,128]{1,0:T(8,128)(2,1)S(1)}, u32[]{:S(2)}, u32[]{:S(2)}) %collective-permute-start.18) | collective-permute-done | bytes 262176 | tf_op jit(solution)/shard_map/ppermute | solution.py:578
  20.1 1.3 %collective-permute-start.5 = (bf16[1024,128]{1,0:T(8,128)(2,1)S(1)}, bf16[1024,128]{1,0:T(8,128)(2,1)S(1)}, u32[]{:S(2)}, u32[]{:S(2)}) collective-permute-start(bf16[1024,128]{1,0:T(8,128)(2,1)S(1)} %collective-permute-done.1.refs_3_.refs_4_), channel_id=1, source_target_pairs={{0,8},{4,12},{1,9},{5,13},{2,10},{6,14},{3,11},{7,15}} | collective-permute-start | bytes 786440 | tf_op jit(solution)/shard_map/ppermute | solution.py:578
  22.9 5.3 %shard_map.40 = (bf16[1056,128]{1,0:T(8,128)(2,1)S(1)}, bf16[1056,128]{1,0:T(8,128)(2,1)S(1)}) custom-call(s32[24,128]{1,0:T(8,128)S(1)} %block_tables.1.tab, bf16[1024,128]{1,0:T(8,128)(2,1)S(1)} %collective-permute-done.18.refs_0_, bf16[1024,128]{1,0:T(8,128)(2,1)S(1)} %collective-permute-done.19.refs_1_, ...), custom_call_target="tpu_custom_call" | custom-call | tf_op jit(solution)/shard_map/pallas_call | solution.py:465
  28.2 2.2 %collective-permute-done.5.refs_7_.refs_8_.refs_3_ = bf16[1024,128]{1,0:T(8,128)(2,1)S(1)} collective-permute-done((bf16[1024,128]{1,0:T(8,128)(2,1)S(1)}, bf16[1024,128]{1,0:T(8,128)(2,1)S(1)}, u32[]{:S(2)}, u32[]{:S(2)}) %collective-permute-start.5) | collective-permute-done | bytes 262176 | tf_op jit(solution)/shard_map/ppermute | solution.py:578
  30.3 3.6 %shard_map.41 = (bf16[1056,128]{1,0:T(8,128)(2,1)S(1)}, bf16[1056,128]{1,0:T(8,128)(2,1)S(1)}) custom-call(s32[24,128]{1,0:T(8,128)S(1)} %block_tables.1.tab, bf16[1024,128]{1,0:T(8,128)(2,1)S(1)} %collective-permute-done.18.refs_0_, bf16[1024,128]{1,0:T(8,128)(2,1)S(1)} %collective-permute-done.19.refs_1_, ...), custom_call_target="tpu_custom_call" | custom-call | tf_op jit(solution)/shard_map/pallas_call | solution.py:465
  34.0 1.3 %collective-permute-start.20 = (bf16[1056,128]{1,0:T(8,128)(2,1)S(1)}, bf16[1056,128]{1,0:T(8,128)(2,1)S(1)}, u32[]{:S(2)}, u32[]{:S(2)}) collective-permute-start(bf16[1056,128]{1,0:T(8,128)(2,1)S(1)} %get-tuple-element.33), channel_id=1, source_target_pairs={{8,16},{12,20},{9,17},{13,21},{10,18},{14,22},{11,19},{15,23}} | collective-permute-start | bytes 811016 | tf_op jit(solution)/shard_map/ppermute | solution.py:578
  35.3 1.3 %collective-permute-start.21 = (bf16[1056,128]{1,0:T(8,128)(2,1)S(1)}, bf16[1056,128]{1,0:T(8,128)(2,1)S(1)}, u32[]{:S(2)}, u32[]{:S(2)}) collective-permute-start(bf16[1056,128]{1,0:T(8,128)(2,1)S(1)} %get-tuple-element.34), channel_id=1, source_target_pairs={{8,24},{12,28},{9,25},{13,29},{10,26},{14,30},{11,27},{15,31}} | collective-permute-start | bytes 811016 | tf_op jit(solution)/shard_map/ppermute | solution.py:578
  37.3 1.3 %collective-permute-start.10 = (bf16[1024,128]{1,0:T(8,128)(2,1)S(1)}, bf16[1024,128]{1,0:T(8,128)(2,1)S(1)}, u32[]{:S(2)}, u32[]{:S(2)}) collective-permute-start(bf16[1024,128]{1,0:T(8,128)(2,1)S(1)} %collective-permute-done.refs_2_.refs_3_), channel_id=1, source_target_pairs={{16,8},{20,12},{17,9},{21,13},{18,10},{22,14},{19,11},{23,15}} | collective-permute-start | bytes 786440 | tf_op jit(solution)/shard_map/ppermute | solution.py:578
  38.6 1.3 %collective-permute-start.11 = (bf16[1024,128]{1,0:T(8,128)(2,1)S(1)}, bf16[1024,128]{1,0:T(8,128)(2,1)S(1)}, u32[]{:S(2)}, u32[]{:S(2)}) collective-permute-start(bf16[1024,128]{1,0:T(8,128)(2,1)S(1)} %collective-permute-done.refs_2_.refs_3_), channel_id=1, source_target_pairs={{24,8},{28,12},{25,9},{29,13},{26,10},{30,14},{27,11},{31,15}} | collective-permute-start | bytes 786440 | tf_op jit(solution)/shard_map/ppermute | solution.py:578
  41.3 9.5 %collective-permute-done.10.refs_0_ = bf16[1024,128]{1,0:T(8,128)(2,1)S(1)} collective-permute-done((bf16[1024,128]{1,0:T(8,128)(2,1)S(1)}, bf16[1024,128]{1,0:T(8,128)(2,1)S(1)}, u32[]{:S(2)}, u32[]{:S(2)}) %collective-permute-start.10) | collective-permute-done | bytes 262176 | tf_op jit(solution)/shard_map/ppermute | solution.py:578
  50.8 5.9 %shard_map.39 = (bf16[1056,128]{1,0:T(8,128)(2,1)S(1)}, bf16[1056,128]{1,0:T(8,128)(2,1)S(1)}) custom-call(s32[24,128]{1,0:T(8,128)S(1)} %block_tables.1.tab, bf16[1024,128]{1,0:T(8,128)(2,1)S(1)} %collective-permute-done.10.refs_0_, bf16[1024,128]{1,0:T(8,128)(2,1)S(1)} %collective-permute-done.11.refs_1_, ...), custom_call_target="tpu_custom_call" | custom-call | tf_op jit(solution)/shard_map/pallas_call | solution.py:465
  56.8 1.3 %collective-permute-start.12 = (bf16[1056,128]{1,0:T(8,128)(2,1)S(1)}, bf16[1056,128]{1,0:T(8,128)(2,1)S(1)}, u32[]{:S(2)}, u32[]{:S(2)}) collective-permute-start(bf16[1056,128]{1,0:T(8,128)(2,1)S(1)} %get-tuple-element.27), channel_id=1, source_target_pairs={{8,20},{12,16},{9,21},{13,17},{10,22},{14,18},{11,23},{15,19}} | collective-permute-start | bytes 811016 | tf_op jit(solution)/shard_map/ppermute | solution.py:578
  58.1 1.4 %collective-permute-start.13 = (bf16[1056,128]{1,0:T(8,128)(2,1)S(1)}, bf16[1056,128]{1,0:T(8,128)(2,1)S(1)}, u32[]{:S(2)}, u32[]{:S(2)}) collective-permute-start(bf16[1056,128]{1,0:T(8,128)(2,1)S(1)} %get-tuple-element.28), channel_id=1, source_target_pairs={{8,28},{12,24},{9,29},{13,25},{10,30},{14,26},{11,31},{15,27}} | collective-permute-start | bytes 811016 | tf_op jit(solution)/shard_map/ppermute | solution.py:578
  59.5 6.1 %shard_map.37 = (bf16[1056,128]{1,0:T(8,128)(2,1)S(1)}, bf16[1056,128]{1,0:T(8,128)(2,1)S(1)}) custom-call(s32[24,128]{1,0:T(8,128)S(1)} %block_tables.1.tab, bf16[1024,128]{1,0:T(8,128)(2,1)S(1)} %get-tuple-element.20.refs_0_, bf16[2,1024,128]{2,1,0:T(8,128)(2,1)S(1)} %get-tuple-element.21.refs_1_.refs_2_, ...), custom_call_target="tpu_custom_call" | custom-call | tf_op jit(solution)/shard_map/pallas_call | solution.py:465
  66.4 1.3 %collective-permute-start.6 = (bf16[1056,128]{1,0:T(8,128)(2,1)S(1)}, bf16[1056,128]{1,0:T(8,128)(2,1)S(1)}, u32[]{:S(2)}, u32[]{:S(2)}) collective-permute-start(bf16[1056,128]{1,0:T(8,128)(2,1)S(1)} %get-tuple-element.25), channel_id=1, source_target_pairs={{0,4},{4,0},{8,12},{12,8},{16,20},{20,16},{24,28},{28,24},{1,5},{5... | collective-permute-start | bytes 811016 | tf_op jit(solution)/shard_map/ppermute | solution.py:578
  68.7 3.0 %collective-permute-done.6.own = bf16[1056,128]{1,0:T(8,128)(2,1)S(1)} collective-permute-done((bf16[1056,128]{1,0:T(8,128)(2,1)S(1)}, bf16[1056,128]{1,0:T(8,128)(2,1)S(1)}, u32[]{:S(2)}, u32[]{:S(2)}) %collective-permute-start.6) | collective-permute-done | bytes 270368 | tf_op jit(solution)/shard_map/ppermute | solution.py:578
  72.5 1.8 %collective-permute-start.14 = (bf16[128,1024]{1,0:T(8,128)(2,1)S(1)}, bf16[128,1024]{1,0:T(8,128)(2,1)S(1)}, u32[]{:S(2)}, u32[]{:S(2)}) collective-permute-start(bf16[128,1024]{1,0:T(8,128)(2,1)S(1)} %combine.2.refs_0_), channel_id=1, source_target_pairs={{0,2},{1,3},{2,0},{3,1},{4,6},{5,7},{6,4},{7,5},{8,10},{9,11},{10,... | collective-permute-start | bytes 786440 | tf_op jit(solution)/shard_map/ppermute | solution.py:581
  74.3 3.1 %collective-permute-start.22 = (bf16[128,1024]{1,0:T(8,128)(2,1)S(1)}, bf16[128,1024]{1,0:T(8,128)(2,1)S(1)}, u32[]{:S(2)}, u32[]{:S(2)}) collective-permute-start(bf16[128,1024]{1,0:T(8,128)(2,1)S(1)} %combine.3.refs_0_), channel_id=1, source_target_pairs={{0,1},{1,0},{2,3},{3,2},{4,5},{5,4},{6,7},{7,6},{8,9},{9,8},{10,11... | collective-permute-start | bytes 786440 | tf_op jit(solution)/shard_map/ppermute | solution.py:581
  77.3 4.2 %collective-permute-start.24 = (bf16[128,1024]{1,0:T(8,128)(2,1)S(1)}, bf16[128,1024]{1,0:T(8,128)(2,1)S(1)}, u32[]{:S(2)}, u32[]{:S(2)}) collective-permute-start(bf16[128,1024]{1,0:T(8,128)(2,1)S(1)} %collective-permute-done.23.refs_2_), channel_id=1, source_target_pairs={{0,1},{1,0},{2,3},{3,2},{4,5},{5,4},{6,7},{7,6},{8,9},{9,8},{10,11... | collective-permute-start | bytes 786440 | tf_op jit(solution)/shard_map/ppermute | solution.py:581
  81.6 2.8 %collective-permute-start.15 = (bf16[128,1024]{1,0:T(8,128)(2,1)S(1)}, bf16[128,1024]{1,0:T(8,128)(2,1)S(1)}, u32[]{:S(2)}, u32[]{:S(2)}) collective-permute-start(bf16[128,1024]{1,0:T(8,128)(2,1)S(1)} %collective-permute-done.14.refs_0_), channel_id=1, source_target_pairs={{0,1},{1,0},{2,3},{3,2},{4,5},{5,4},{6,7},{7,6},{8,9},{9,8},{10,11... | collective-permute-start | bytes 786440 | tf_op jit(solution)/shard_map/ppermute | solution.py:581
  84.4 2.5 %project.3.refs_2_ = f32[1024,1024]{1,0:T(8,128)S(1)} custom-call(s32[1,3]{1,0:T(1,128)S(1)} %add_bitcast_fusion.ids_ref, bf16[1024,1024]{1,0:T(8,128)(2,1)S(1)} %copy-done, bf16[128,1024]{1,0:T(8,128)(2,1)S(1)} %combine.3.refs_0_, bf16[128,1024]{1,0:T(8,128)(2,1)S(1)} %collective-permute-done.22.refs_1_, ...), custom_call_target="tpu_custom_call" | custom-call | tf_op jit(solution)/shard_map/project/pallas_call | solution.py:551
  86.9 1.9 %project.4.refs_2_ = f32[1024,1024]{1,0:T(8,128)S(1)} custom-call(s32[1,3]{1,0:T(1,128)S(1)} %add_bitcast_fusion.ids_ref, bf16[1024,1024]{1,0:T(8,128)(2,1)S(1)} %copy-done, bf16[128,1024]{1,0:T(8,128)(2,1)S(1)} %combine.2.refs_0_, bf16[128,1024]{1,0:T(8,128)(2,1)S(1)} %collective-permute-done.16.refs_1_, f32[1024,1024]{1,0:T(8,128)S(1)} %project.3.refs_2_), custom_call_target="tpu_custom_call" | custom-call | tf_op jit(solution)/shard_map/project/pallas_call | solution.py:551
  88.8 3.2 %project.5 = bf16[1024,1024]{1,0:T(8,128)(2,1)} custom-call(s32[1,3]{1,0:T(1,128)S(1)} %add_bitcast_fusion.ids_ref, bf16[1024,1024]{1,0:T(8,128)(2,1)S(1)} %copy-done, bf16[128,1024]{1,0:T(8,128)(2,1)S(1)} %collective-permute-done.14.refs_0_, bf16[128,1024]{1,0:T(8,128)(2,1)S(1)} %collective-permute-done.15.refs_1_, f32[1024,1024]{1,0:T(8,128)S(1)} %project.4.refs_2_), custom_call_target="tpu_custom_call" | custom-call | tf_op jit(solution)/shard_map/project/pallas_call | solution.py:551
  (36 shorter events, 7.6 us)
Async XLA Ops:
  0.0 22.1 %copy-start.1 = (s32[2,64]{1,0:T(2,128)S(1)}, s32[2,64]{1,0:T(2,128)}, u32[]{:S(2)}) copy-start(s32[2,64]{1,0:T(2,128)} %table_ref.1) | copy-start | bytes 1540
  3.1 7.3 %collective-permute-start = (bf16[1024,128]{1,0:T(8,128)(2,1)S(1)}, bf16[1024,128]{1,0:T(8,128)(2,1)S(1)}, u32[]{:S(2)}, u32[]{:S(2)}) collective-permute-start(bf16[1024,128]{1,0:T(8,128)(2,1)S(1)} %get-tuple-element.22), channel_id=1, source_target_pairs={{0,4},{4,0},{8,12},{12,8},{16,20},{20,16},{24,28},{28,24},{1,5},{5... | collective-permute-start | bytes 786440 | tf_op jit(solution)/shard_map/ppermute | solution.py:578
  4.4 18.5 %collective-permute-start.3 = (bf16[2,1024,128]{2,1,0:T(8,128)(2,1)S(1)}, bf16[2,1024,128]{2,1,0:T(8,128)(2,1)S(1)}, u32[]{:S(2)}, u32[]{:S(2)}) collective-permute-start(bf16[2,1024,128]{2,1,0:T(8,128)(2,1)S(1)} %get-tuple-element.21.refs_1_.refs_2_), channel_id=1, source_target_pairs={{0,8},{4,12},{1,9},{5,13},{2,10},{6,14},{3,11},{7,15}} | collective-permute-start | bytes 1572872 | tf_op jit(solution)/shard_map/ppermute | solution.py:578
  5.7 10.3 %collective-permute-start.1 = (bf16[1024,128]{1,0:T(8,128)(2,1)S(1)}, bf16[1024,128]{1,0:T(8,128)(2,1)S(1)}, u32[]{:S(2)}, u32[]{:S(2)}) collective-permute-start(bf16[1024,128]{1,0:T(8,128)(2,1)S(1)} %get-tuple-element.23), channel_id=1, source_target_pairs={{0,4},{4,0},{8,12},{12,8},{16,20},{20,16},{24,28},{28,24},{1,5},{5... | collective-permute-start | bytes 786440 | tf_op jit(solution)/shard_map/ppermute | solution.py:578
  6.0 14.1 %collective-permute-start.18 = (bf16[1024,128]{1,0:T(8,128)(2,1)S(1)}, bf16[1024,128]{1,0:T(8,128)(2,1)S(1)}, u32[]{:S(2)}, u32[]{:S(2)}) collective-permute-start(bf16[1024,128]{1,0:T(8,128)(2,1)S(1)} %get-tuple-element.20.refs_0_), channel_id=1, source_target_pairs={{16,8},{20,12},{17,9},{21,13},{18,10},{22,14},{19,11},{23,15}} | collective-permute-start | bytes 786440 | tf_op jit(solution)/shard_map/ppermute | solution.py:578
  7.3 14.1 %collective-permute-start.19 = (bf16[1024,128]{1,0:T(8,128)(2,1)S(1)}, bf16[1024,128]{1,0:T(8,128)(2,1)S(1)}, u32[]{:S(2)}, u32[]{:S(2)}) collective-permute-start(bf16[1024,128]{1,0:T(8,128)(2,1)S(1)} %get-tuple-element.20.refs_0_), channel_id=1, source_target_pairs={{24,8},{28,12},{25,9},{29,13},{26,10},{30,14},{27,11},{31,15}} | collective-permute-start | bytes 786440 | tf_op jit(solution)/shard_map/ppermute | solution.py:578
  10.4 12.5 %collective-permute-start.2 = (bf16[1024,128]{1,0:T(8,128)(2,1)S(1)}, bf16[1024,128]{1,0:T(8,128)(2,1)S(1)}, u32[]{:S(2)}, u32[]{:S(2)}) collective-permute-start(bf16[1024,128]{1,0:T(8,128)(2,1)S(1)} %get-tuple-element.24), channel_id=1, source_target_pairs={{0,4},{4,0},{8,12},{12,8},{16,20},{20,16},{24,28},{28,24},{1,5},{5... | collective-permute-start | bytes 786440 | tf_op jit(solution)/shard_map/ppermute | solution.py:578
  16.0 12.2 %collective-permute-start.4 = (bf16[1024,128]{1,0:T(8,128)(2,1)S(1)}, bf16[1024,128]{1,0:T(8,128)(2,1)S(1)}, u32[]{:S(2)}, u32[]{:S(2)}) collective-permute-start(bf16[1024,128]{1,0:T(8,128)(2,1)S(1)} %collective-permute-done.refs_2_.refs_3_), channel_id=1, source_target_pairs={{0,8},{4,12},{1,9},{5,13},{2,10},{6,14},{3,11},{7,15}} | collective-permute-start | bytes 786440 | tf_op jit(solution)/shard_map/ppermute | solution.py:578
  20.1 10.2 %collective-permute-start.5 = (bf16[1024,128]{1,0:T(8,128)(2,1)S(1)}, bf16[1024,128]{1,0:T(8,128)(2,1)S(1)}, u32[]{:S(2)}, u32[]{:S(2)}) collective-permute-start(bf16[1024,128]{1,0:T(8,128)(2,1)S(1)} %collective-permute-done.1.refs_3_.refs_4_), channel_id=1, source_target_pairs={{0,8},{4,12},{1,9},{5,13},{2,10},{6,14},{3,11},{7,15}} | collective-permute-start | bytes 786440 | tf_op jit(solution)/shard_map/ppermute | solution.py:578
  21.4 17.2 %collective-permute-start.7 = (bf16[1024,128]{1,0:T(8,128)(2,1)S(1)}, bf16[1024,128]{1,0:T(8,128)(2,1)S(1)}, u32[]{:S(2)}, u32[]{:S(2)}) collective-permute-start(bf16[1024,128]{1,0:T(8,128)(2,1)S(1)} %get-tuple-element.20.refs_0_), channel_id=1, source_target_pairs={{24,16},{28,20},{25,17},{29,21},{26,18},{30,22},{27,19},{31,23}} | collective-permute-start | bytes 786440 | tf_op jit(solution)/shard_map/ppermute | solution.py:578
  34.0 31.7 %collective-permute-start.20 = (bf16[1056,128]{1,0:T(8,128)(2,1)S(1)}, bf16[1056,128]{1,0:T(8,128)(2,1)S(1)}, u32[]{:S(2)}, u32[]{:S(2)}) collective-permute-start(bf16[1056,128]{1,0:T(8,128)(2,1)S(1)} %get-tuple-element.33), channel_id=1, source_target_pairs={{8,16},{12,20},{9,17},{13,21},{10,18},{14,22},{11,19},{15,23}} | collective-permute-start | bytes 811016 | tf_op jit(solution)/shard_map/ppermute | solution.py:578
  35.3 31.1 %collective-permute-start.21 = (bf16[1056,128]{1,0:T(8,128)(2,1)S(1)}, bf16[1056,128]{1,0:T(8,128)(2,1)S(1)}, u32[]{:S(2)}, u32[]{:S(2)}) collective-permute-start(bf16[1056,128]{1,0:T(8,128)(2,1)S(1)} %get-tuple-element.34), channel_id=1, source_target_pairs={{8,24},{12,28},{9,25},{13,29},{10,26},{14,30},{11,27},{15,31}} | collective-permute-start | bytes 811016 | tf_op jit(solution)/shard_map/ppermute | solution.py:578
  36.6 3.3 %collective-permute-start.8 = (bf16[1024,128]{1,0:T(8,128)(2,1)S(1)}, bf16[1024,128]{1,0:T(8,128)(2,1)S(1)}, u32[]{:S(2)}, u32[]{:S(2)}) collective-permute-start(bf16[1024,128]{1,0:T(8,128)(2,1)S(1)} %collective-permute-done.refs_2_.refs_3_), channel_id=1, source_target_pairs={{24,16},{28,20},{25,17},{29,21},{26,18},{30,22},{27,19},{31,23}} | collective-permute-start | bytes 786440 | tf_op jit(solution)/shard_map/ppermute | solution.py:578
  37.3 13.5 %collective-permute-start.10 = (bf16[1024,128]{1,0:T(8,128)(2,1)S(1)}, bf16[1024,128]{1,0:T(8,128)(2,1)S(1)}, u32[]{:S(2)}, u32[]{:S(2)}) collective-permute-start(bf16[1024,128]{1,0:T(8,128)(2,1)S(1)} %collective-permute-done.refs_2_.refs_3_), channel_id=1, source_target_pairs={{16,8},{20,12},{17,9},{21,13},{18,10},{22,14},{19,11},{23,15}} | collective-permute-start | bytes 786440 | tf_op jit(solution)/shard_map/ppermute | solution.py:578
  38.6 12.2 %collective-permute-start.11 = (bf16[1024,128]{1,0:T(8,128)(2,1)S(1)}, bf16[1024,128]{1,0:T(8,128)(2,1)S(1)}, u32[]{:S(2)}, u32[]{:S(2)}) collective-permute-start(bf16[1024,128]{1,0:T(8,128)(2,1)S(1)} %collective-permute-done.refs_2_.refs_3_), channel_id=1, source_target_pairs={{24,8},{28,12},{25,9},{29,13},{26,10},{30,14},{27,11},{31,15}} | collective-permute-start | bytes 786440 | tf_op jit(solution)/shard_map/ppermute | solution.py:578
  40.7 27.0 %collective-permute-start.17 = (bf16[1056,128]{1,0:T(8,128)(2,1)S(1)}, bf16[1056,128]{1,0:T(8,128)(2,1)S(1)}, u32[]{:S(2)}, u32[]{:S(2)}) collective-permute-start(bf16[1056,128]{1,0:T(8,128)(2,1)S(1)} %get-tuple-element.30), channel_id=1, source_target_pairs={{16,24},{20,28},{17,25},{21,29},{18,26},{22,30},{19,27},{23,31}} | collective-permute-start | bytes 811016 | tf_op jit(solution)/shard_map/ppermute | solution.py:578
  56.8 12.0 %collective-permute-start.12 = (bf16[1056,128]{1,0:T(8,128)(2,1)S(1)}, bf16[1056,128]{1,0:T(8,128)(2,1)S(1)}, u32[]{:S(2)}, u32[]{:S(2)}) collective-permute-start(bf16[1056,128]{1,0:T(8,128)(2,1)S(1)} %get-tuple-element.27), channel_id=1, source_target_pairs={{8,20},{12,16},{9,21},{13,17},{10,22},{14,18},{11,23},{15,19}} | collective-permute-start | bytes 811016 | tf_op jit(solution)/shard_map/ppermute | solution.py:578
  58.1 26.3 %copy-start = (bf16[1024,1024]{1,0:T(8,128)(2,1)S(1)}, bf16[1024,1024]{1,0:T(8,128)(2,1)}, u32[]{:S(2)}) copy-start(bf16[1024,1024]{1,0:T(8,128)(2,1)} %weight_ref.5) | copy-start | bytes 6291460
  58.1 10.6 %collective-permute-start.13 = (bf16[1056,128]{1,0:T(8,128)(2,1)S(1)}, bf16[1056,128]{1,0:T(8,128)(2,1)S(1)}, u32[]{:S(2)}, u32[]{:S(2)}) collective-permute-start(bf16[1056,128]{1,0:T(8,128)(2,1)S(1)} %get-tuple-element.28), channel_id=1, source_target_pairs={{8,28},{12,24},{9,29},{13,25},{10,30},{14,26},{11,31},{15,27}} | collective-permute-start | bytes 811016 | tf_op jit(solution)/shard_map/ppermute | solution.py:578
  65.7 3.1 %collective-permute-start.9 = (bf16[1056,128]{1,0:T(8,128)(2,1)S(1)}, bf16[1056,128]{1,0:T(8,128)(2,1)S(1)}, u32[]{:S(2)}, u32[]{:S(2)}) collective-permute-start(bf16[1056,128]{1,0:T(8,128)(2,1)S(1)} %get-tuple-element.26), channel_id=1, source_target_pairs={{16,28},{20,24},{17,29},{21,25},{18,30},{22,26},{19,31},{23,27}} | collective-permute-start | bytes 811016 | tf_op jit(solution)/shard_map/ppermute | solution.py:578
  66.4 5.4 %collective-permute-start.6 = (bf16[1056,128]{1,0:T(8,128)(2,1)S(1)}, bf16[1056,128]{1,0:T(8,128)(2,1)S(1)}, u32[]{:S(2)}, u32[]{:S(2)}) collective-permute-start(bf16[1056,128]{1,0:T(8,128)(2,1)S(1)} %get-tuple-element.25), channel_id=1, source_target_pairs={{0,4},{4,0},{8,12},{12,8},{16,20},{20,16},{24,28},{28,24},{1,5},{5... | collective-permute-start | bytes 811016 | tf_op jit(solution)/shard_map/ppermute | solution.py:578
  68.4 8.9 %collective-permute-start.23 = (bf16[128,1024]{1,0:T(8,128)(2,1)S(1)}, bf16[128,1024]{1,0:T(8,128)(2,1)S(1)}, u32[]{:S(2)}, u32[]{:S(2)}) collective-permute-start(bf16[128,1024]{1,0:T(8,128)(2,1)S(1)} %combine.3.refs_0_), channel_id=1, source_target_pairs={{0,2},{1,3},{2,0},{3,1},{4,6},{5,7},{6,4},{7,5},{8,10},{9,11},{10,... | collective-permute-start | bytes 786440 | tf_op jit(solution)/shard_map/ppermute | solution.py:581
  72.5 9.1 %collective-permute-start.14 = (bf16[128,1024]{1,0:T(8,128)(2,1)S(1)}, bf16[128,1024]{1,0:T(8,128)(2,1)S(1)}, u32[]{:S(2)}, u32[]{:S(2)}) collective-permute-start(bf16[128,1024]{1,0:T(8,128)(2,1)S(1)} %combine.2.refs_0_), channel_id=1, source_target_pairs={{0,2},{1,3},{2,0},{3,1},{4,6},{5,7},{6,4},{7,5},{8,10},{9,11},{10,... | collective-permute-start | bytes 786440 | tf_op jit(solution)/shard_map/ppermute | solution.py:581
  74.3 10.1 %collective-permute-start.22 = (bf16[128,1024]{1,0:T(8,128)(2,1)S(1)}, bf16[128,1024]{1,0:T(8,128)(2,1)S(1)}, u32[]{:S(2)}, u32[]{:S(2)}) collective-permute-start(bf16[128,1024]{1,0:T(8,128)(2,1)S(1)} %combine.3.refs_0_), channel_id=1, source_target_pairs={{0,1},{1,0},{2,3},{3,2},{4,5},{5,4},{6,7},{7,6},{8,9},{9,8},{10,11... | collective-permute-start | bytes 786440 | tf_op jit(solution)/shard_map/ppermute | solution.py:581
  77.3 7.0 %collective-permute-start.24 = (bf16[128,1024]{1,0:T(8,128)(2,1)S(1)}, bf16[128,1024]{1,0:T(8,128)(2,1)S(1)}, u32[]{:S(2)}, u32[]{:S(2)}) collective-permute-start(bf16[128,1024]{1,0:T(8,128)(2,1)S(1)} %collective-permute-done.23.refs_2_), channel_id=1, source_target_pairs={{0,1},{1,0},{2,3},{3,2},{4,5},{5,4},{6,7},{7,6},{8,9},{9,8},{10,11... | collective-permute-start | bytes 786440 | tf_op jit(solution)/shard_map/ppermute | solution.py:581
  81.6 5.3 %collective-permute-start.16 = (bf16[128,1024]{1,0:T(8,128)(2,1)S(1)}, bf16[128,1024]{1,0:T(8,128)(2,1)S(1)}, u32[]{:S(2)}, u32[]{:S(2)}) collective-permute-start(bf16[128,1024]{1,0:T(8,128)(2,1)S(1)} %combine.2.refs_0_), channel_id=1, source_target_pairs={{0,1},{1,0},{2,3},{3,2},{4,5},{5,4},{6,7},{7,6},{8,9},{9,8},{10,11... | collective-permute-start | bytes 786440 | tf_op jit(solution)/shard_map/ppermute | solution.py:581
  81.6 7.3 %collective-permute-start.15 = (bf16[128,1024]{1,0:T(8,128)(2,1)S(1)}, bf16[128,1024]{1,0:T(8,128)(2,1)S(1)}, u32[]{:S(2)}, u32[]{:S(2)}) collective-permute-start(bf16[128,1024]{1,0:T(8,128)(2,1)S(1)} %collective-permute-done.14.refs_0_), channel_id=1, source_target_pairs={{0,1},{1,0},{2,3},{3,2},{4,5},{5,4},{6,7},{7,6},{8,9},{9,8},{10,11... | collective-permute-start | bytes 786440 | tf_op jit(solution)/shard_map/ppermute | solution.py:581

commit v5 on v4

--- a/solution.py
+++ b/solution.py
@@ -481,7 +481,7 @@
 
 def combine_kernel(ids_ref, own, near, second, third, out_ref):
     plane = ids_ref[0, 1]
-    width, rows = out_ref.shape
+    rows, width = out_ref.shape
     own_log = log_of(own, rows)
     near_log = jnp.where(plane == 3, log_of(near, rows), NEG)
     far_log = jnp.where(plane == 3, log_of(third, rows), log_of(second, rows))
@@ -500,7 +500,7 @@
             + near[lines, :].astype(jnp.float32) * near_part[b : b + 1]
             + far.astype(jnp.float32) * far_part[b : b + 1]
         )
-        out_ref[:, lines] = mixed.astype(jnp.bfloat16)
+        out_ref[lines, :] = mixed.T.astype(jnp.bfloat16)
 
 
 def combine(ids, values):
@@ -511,7 +511,7 @@
         combine_kernel,
         in_specs=[pl.BlockSpec(memory_space=pltpu.SMEM)] + [vmem] * len(values),
         out_specs=vmem,
-        out_shape=jax.ShapeDtypeStruct((width, rows), jnp.bfloat16),
+        out_shape=jax.ShapeDtypeStruct((rows, width), jnp.bfloat16),
         compiler_params=pltpu.CompilerParams(vmem_limit_bytes=VMEM_BYTES),
         name="combine",
     )(ids, *values)
@@ -524,36 +524,33 @@
     out_ref = refs[-1]
     features = refs[: len(which)]
     given = refs[len(which)] if len(refs) > len(which) + 1 else None
-    depth = features[0].shape[0]
-    rows = out_ref.shape[0]
-    first = pl.program_id(0) * rows
+    depth = features[0].shape[1]
+    cols = out_ref.shape[1]
+    here = pl.ds(pl.multiple_of(pl.program_id(0) * cols, cols), cols)
     lines = [pl.ds(pl.multiple_of(((group ^ j) * 2 + head) * depth, depth), depth) for j in which]
-    here = pl.ds(pl.multiple_of(first, rows), rows)
-    left = jnp.concatenate([f[:, here] for f in features], axis=0)
+    right = jnp.concatenate([weight_ref[at, here] for at in lines], axis=0)
     chunk = 512
-    for col in range(0, out_ref.shape[1], chunk):
-        cols = slice(col, col + chunk)
-        right = jnp.concatenate([weight_ref[at, cols] for at in lines], axis=0)
-        acc = lax.dot_general(
-            left, right, (((0,), (0,)), ((), ())), preferred_element_type=jnp.float32
-        )
+    for start in range(0, out_ref.shape[0], chunk):
+        rows = slice(start, start + chunk)
+        left = jnp.concatenate([f[rows, :] for f in features], axis=1)
+        acc = jnp.dot(left, right, preferred_element_type=jnp.float32)
         if given is not None:
-            acc = acc + given[here, cols]
-        out_ref[:, cols] = acc.astype(out_ref.dtype)
+            acc = acc + given[rows, here]
+        out_ref[rows, :] = acc.astype(out_ref.dtype)
 
 
 def project(other, final, which, ids, weight, features, given):
-    rows = features[0].shape[1]
-    step = rows // 4
+    rows = features[0].shape[0]
     vmem = pl.BlockSpec(memory_space=pltpu.VMEM)
     given = [] if given is None else [given]
     width = weight.shape[1]
+    step = width // 4
     return pl.pallas_call(
         functools.partial(project_kernel, other, which),
-        grid=(rows // step,),
+        grid=(width // step,),
         in_specs=[pl.BlockSpec(memory_space=pltpu.SMEM)]
         + [vmem] * (1 + len(features) + len(given)),
-        out_specs=pl.BlockSpec((step, width), lambda i: (i, 0)),
+        out_specs=pl.BlockSpec((rows, step), lambda i: (0, i)),
         out_shape=jax.ShapeDtypeStruct((rows, width), jnp.bfloat16 if final else jnp.float32),
         compiler_params=pltpu.CompilerParams(vmem_limit_bytes=VMEM_BYTES),
         name="project",
@@ -611,11 +608,11 @@
     back3_keep = send(back3_keep, hop((1, 3)))
     back2_keep = send(back2_keep, hop((1, 2)))
     both_kv = plane_kv + (low_keep, low_first, low_second)
+    down_keep, down_swap = meet("near", (near_keep, near_swap), plane_kv)
+    down_keep = send(down_keep, hop((2, 3)))
     back2_swap, back3_swap = meet("far_both", (far2_swap, far3_swap), both_kv)
     back3_other = send(back3_swap, hop((1, 3), cross=1))
     back2_other = send(back2_swap, hop((1, 2), cross=1))
-    down_keep, down_swap = meet("near", (near_keep, near_swap), plane_kv)
-    down_keep = send(down_keep, hop((2, 3)))
     down_other = send(down_swap, hop((2, 3), cross=1))
     own_keep, own_swap = meet("own", (q_keep,), both_kv)
     own_other = send(own_swap, swap)

time: 92.4 us -> 92.7 us (level)
  no operation moved by 1% of the time
where the time goes in v5:
time: 92.7 us; the launch traced here: 92.4 us
  Pallas kernels  33.4 us (36%)
  starting transfers between devices  33.4 us (36%)
  waiting for transfers between devices  23.7 us (26%)
  local copies, waits for them, and re-layouts  1.63 us (2%)
    ppermute x19, waiting for transfers between devices, send(): return lax.ppermute(value, 'seq', pairs)  23.6 us
    pallas_call x5, Pallas kernels, attend(): pl.pallas_call(functools.partial(attend_kernel, kind, per_shard, cluster_...  21.7 us
    ppermute x19, starting transfers between devices, send(): return lax.ppermute(value, 'seq', pairs)  21.2 us
    ppermute x6, starting transfers between devices, across(): lax.ppermute(value, 'head', [(g, g ^ flip) for g in range(head_count)])  12.2 us
    pallas_call x3, Pallas kernels, project(): pl.pallas_call(functools.partial(project_kernel, other, which), grid=(wid...  7.94 us
  transfers between devices with their start and end apart: 25, of which 6 were waited for; matrix products, arithmetic and copies ran while one was open for 0% of the time, Pallas kernels for 31%

profile of v5, /device:TPU:13, one launch (start us, length us, event | category | flops | bytes accessed | tf_op | source)
XLA Modules:
  0.0 92.4 jit_solution(10584266761302286408)
XLA Ops:
  0.0 1.6 %copy.6 = bf16[1024,2,384]{2,0,1:T(8,128)(2,1)S(1)} copy(bf16[1024,2,384]{2,1,0:T(2,128)(2,1)} %param.3) | data formatting | bytes 3145728 | tf_op args[0]
  1.7 1.4 %split_heads.1 = (bf16[1024,128]{1,0:T(8,128)(2,1)S(1)}, bf16[2,1024,128]{2,1,0:T(8,128)(2,1)S(1)}, bf16[1024,128]{1,0:T(8,128)(2,1)S(1)}, bf16[1024,128]{1,0:T(8,128)(2,1)S(1)}, bf16[1024,128]{1,0:T(8,128)(2,1)S(1)}) custom-call(s32[1,3]{1,0:T(1,128)S(1)} %add_bitcast_fusion.ids_ref, bf16[2,1024,384]{2,1,0:T(8,128)(2,1)S(1)} %bitcast.8), custom_call_target="tpu_custom_call" | custom-call | tf_op jit(solution)/shard_map/split_heads/pallas_call | solution.py:180
  3.1 1.3 %collective-permute-start = (bf16[1024,128]{1,0:T(8,128)(2,1)S(1)}, bf16[1024,128]{1,0:T(8,128)(2,1)S(1)}, u32[]{:S(2)}, u32[]{:S(2)}) collective-permute-start(bf16[1024,128]{1,0:T(8,128)(2,1)S(1)} %get-tuple-element.22), channel_id=1, source_target_pairs={{0,4},{4,0},{8,12},{12,8},{16,20},{20,16},{24,28},{28,24},{1,5},{5... | collective-permute-start | bytes 786440 | tf_op jit(solution)/shard_map/ppermute | solution.py:575
  4.4 1.3 %collective-permute-start.3 = (bf16[2,1024,128]{2,1,0:T(8,128)(2,1)S(1)}, bf16[2,1024,128]{2,1,0:T(8,128)(2,1)S(1)}, u32[]{:S(2)}, u32[]{:S(2)}) collective-permute-start(bf16[2,1024,128]{2,1,0:T(8,128)(2,1)S(1)} %get-tuple-element.21.refs_1_.refs_2_), channel_id=1, source_target_pairs={{0,8},{4,12},{1,9},{5,13},{2,10},{6,14},{3,11},{7,15}} | collective-permute-start | bytes 1572872 | tf_op jit(solution)/shard_map/ppermute | solution.py:575
  6.0 1.3 %collective-permute-start.18 = (bf16[1024,128]{1,0:T(8,128)(2,1)S(1)}, bf16[1024,128]{1,0:T(8,128)(2,1)S(1)}, u32[]{:S(2)}, u32[]{:S(2)}) collective-permute-start(bf16[1024,128]{1,0:T(8,128)(2,1)S(1)} %get-tuple-element.20.refs_0_), channel_id=1, source_target_pairs={{16,8},{20,12},{17,9},{21,13},{18,10},{22,14},{19,11},{23,15}} | collective-permute-start | bytes 786440 | tf_op jit(solution)/shard_map/ppermute | solution.py:575
  7.3 1.3 %collective-permute-start.19 = (bf16[1024,128]{1,0:T(8,128)(2,1)S(1)}, bf16[1024,128]{1,0:T(8,128)(2,1)S(1)}, u32[]{:S(2)}, u32[]{:S(2)}) collective-permute-start(bf16[1024,128]{1,0:T(8,128)(2,1)S(1)} %get-tuple-element.20.refs_0_), channel_id=1, source_target_pairs={{24,8},{28,12},{25,9},{29,13},{26,10},{30,14},{27,11},{31,15}} | collective-permute-start | bytes 786440 | tf_op jit(solution)/shard_map/ppermute | solution.py:575
  8.6 1.8 %collective-permute-done.refs_2_.refs_3_ = bf16[1024,128]{1,0:T(8,128)(2,1)S(1)} collective-permute-done((bf16[1024,128]{1,0:T(8,128)(2,1)S(1)}, bf16[1024,128]{1,0:T(8,128)(2,1)S(1)}, u32[]{:S(2)}, u32[]{:S(2)}) %collective-permute-start) | collective-permute-done | bytes 262176 | tf_op jit(solution)/shard_map/ppermute | solution.py:575
  11.6 4.4 %collective-permute-done.1.refs_3_.refs_4_ = bf16[1024,128]{1,0:T(8,128)(2,1)S(1)} collective-permute-done((bf16[1024,128]{1,0:T(8,128)(2,1)S(1)}, bf16[1024,128]{1,0:T(8,128)(2,1)S(1)}, u32[]{:S(2)}, u32[]{:S(2)}) %collective-permute-start.1) | collective-permute-done | bytes 262176 | tf_op jit(solution)/shard_map/ppermute | solution.py:575
  16.0 1.3 %collective-permute-start.4 = (bf16[1024,128]{1,0:T(8,128)(2,1)S(1)}, bf16[1024,128]{1,0:T(8,128)(2,1)S(1)}, u32[]{:S(2)}, u32[]{:S(2)}) collective-permute-start(bf16[1024,128]{1,0:T(8,128)(2,1)S(1)} %collective-permute-done.refs_2_.refs_3_), channel_id=1, source_target_pairs={{0,8},{4,12},{1,9},{5,13},{2,10},{6,14},{3,11},{7,15}} | collective-permute-start | bytes 786440 | tf_op jit(solution)/shard_map/ppermute | solution.py:575
  17.3 2.8 %collective-permute-done.18.refs_0_ = bf16[1024,128]{1,0:T(8,128)(2,1)S(1)} collective-permute-done((bf16[1024,128]{1,0:T(8,128)(2,1)S(1)}, bf16[1024,128]{1,0:T(8,128)(2,1)S(1)}, u32[]{:S(2)}, u32[]{:S(2)}) %collective-permute-start.18) | collective-permute-done | bytes 262176 | tf_op jit(solution)/shard_map/ppermute | solution.py:575
  20.1 1.3 %collective-permute-start.5 = (bf16[1024,128]{1,0:T(8,128)(2,1)S(1)}, bf16[1024,128]{1,0:T(8,128)(2,1)S(1)}, u32[]{:S(2)}, u32[]{:S(2)}) collective-permute-start(bf16[1024,128]{1,0:T(8,128)(2,1)S(1)} %collective-permute-done.1.refs_3_.refs_4_), channel_id=1, source_target_pairs={{0,8},{4,12},{1,9},{5,13},{2,10},{6,14},{3,11},{7,15}} | collective-permute-start | bytes 786440 | tf_op jit(solution)/shard_map/ppermute | solution.py:575
  22.9 5.3 %shard_map.40 = (bf16[1056,128]{1,0:T(8,128)(2,1)S(1)}, bf16[1056,128]{1,0:T(8,128)(2,1)S(1)}) custom-call(s32[24,128]{1,0:T(8,128)S(1)} %block_tables.1.tab, bf16[1024,128]{1,0:T(8,128)(2,1)S(1)} %collective-permute-done.18.refs_0_, bf16[1024,128]{1,0:T(8,128)(2,1)S(1)} %collective-permute-done.19.refs_1_, ...), custom_call_target="tpu_custom_call" | custom-call | tf_op jit(solution)/shard_map/pallas_call | solution.py:465
  28.2 2.2 %collective-permute-done.5.refs_7_.refs_8_.refs_3_ = bf16[1024,128]{1,0:T(8,128)(2,1)S(1)} collective-permute-done((bf16[1024,128]{1,0:T(8,128)(2,1)S(1)}, bf16[1024,128]{1,0:T(8,128)(2,1)S(1)}, u32[]{:S(2)}, u32[]{:S(2)}) %collective-permute-start.5) | collective-permute-done | bytes 262176 | tf_op jit(solution)/shard_map/ppermute | solution.py:575
  30.3 3.6 %shard_map.41 = (bf16[1056,128]{1,0:T(8,128)(2,1)S(1)}, bf16[1056,128]{1,0:T(8,128)(2,1)S(1)}) custom-call(s32[24,128]{1,0:T(8,128)S(1)} %block_tables.1.tab, bf16[1024,128]{1,0:T(8,128)(2,1)S(1)} %collective-permute-done.18.refs_0_, bf16[1024,128]{1,0:T(8,128)(2,1)S(1)} %collective-permute-done.19.refs_1_, ...), custom_call_target="tpu_custom_call" | custom-call | tf_op jit(solution)/shard_map/pallas_call | solution.py:465
  34.0 1.3 %collective-permute-start.20 = (bf16[1056,128]{1,0:T(8,128)(2,1)S(1)}, bf16[1056,128]{1,0:T(8,128)(2,1)S(1)}, u32[]{:S(2)}, u32[]{:S(2)}) collective-permute-start(bf16[1056,128]{1,0:T(8,128)(2,1)S(1)} %get-tuple-element.33), channel_id=1, source_target_pairs={{8,16},{12,20},{9,17},{13,21},{10,18},{14,22},{11,19},{15,23}} | collective-permute-start | bytes 811016 | tf_op jit(solution)/shard_map/ppermute | solution.py:575
  35.3 1.3 %collective-permute-start.21 = (bf16[1056,128]{1,0:T(8,128)(2,1)S(1)}, bf16[1056,128]{1,0:T(8,128)(2,1)S(1)}, u32[]{:S(2)}, u32[]{:S(2)}) collective-permute-start(bf16[1056,128]{1,0:T(8,128)(2,1)S(1)} %get-tuple-element.34), channel_id=1, source_target_pairs={{8,24},{12,28},{9,25},{13,29},{10,26},{14,30},{11,27},{15,31}} | collective-permute-start | bytes 811016 | tf_op jit(solution)/shard_map/ppermute | solution.py:575
  37.3 1.3 %collective-permute-start.10 = (bf16[1024,128]{1,0:T(8,128)(2,1)S(1)}, bf16[1024,128]{1,0:T(8,128)(2,1)S(1)}, u32[]{:S(2)}, u32[]{:S(2)}) collective-permute-start(bf16[1024,128]{1,0:T(8,128)(2,1)S(1)} %collective-permute-done.refs_2_.refs_3_), channel_id=1, source_target_pairs={{16,8},{20,12},{17,9},{21,13},{18,10},{22,14},{19,11},{23,15}} | collective-permute-start | bytes 786440 | tf_op jit(solution)/shard_map/ppermute | solution.py:575
  38.6 1.3 %collective-permute-start.11 = (bf16[1024,128]{1,0:T(8,128)(2,1)S(1)}, bf16[1024,128]{1,0:T(8,128)(2,1)S(1)}, u32[]{:S(2)}, u32[]{:S(2)}) collective-permute-start(bf16[1024,128]{1,0:T(8,128)(2,1)S(1)} %collective-permute-done.refs_2_.refs_3_), channel_id=1, source_target_pairs={{24,8},{28,12},{25,9},{29,13},{26,10},{30,14},{27,11},{31,15}} | collective-permute-start | bytes 786440 | tf_op jit(solution)/shard_map/ppermute | solution.py:575
  41.3 9.5 %collective-permute-done.10.refs_0_ = bf16[1024,128]{1,0:T(8,128)(2,1)S(1)} collective-permute-done((bf16[1024,128]{1,0:T(8,128)(2,1)S(1)}, bf16[1024,128]{1,0:T(8,128)(2,1)S(1)}, u32[]{:S(2)}, u32[]{:S(2)}) %collective-permute-start.10) | collective-permute-done | bytes 262176 | tf_op jit(solution)/shard_map/ppermute | solution.py:575
  50.8 5.9 %shard_map.39 = (bf16[1056,128]{1,0:T(8,128)(2,1)S(1)}, bf16[1056,128]{1,0:T(8,128)(2,1)S(1)}) custom-call(s32[24,128]{1,0:T(8,128)S(1)} %block_tables.1.tab, bf16[1024,128]{1,0:T(8,128)(2,1)S(1)} %collective-permute-done.10.refs_0_, bf16[1024,128]{1,0:T(8,128)(2,1)S(1)} %collective-permute-done.11.refs_1_, ...), custom_call_target="tpu_custom_call" | custom-call | tf_op jit(solution)/shard_map/pallas_call | solution.py:465
  56.8 1.3 %collective-permute-start.12 = (bf16[1056,128]{1,0:T(8,128)(2,1)S(1)}, bf16[1056,128]{1,0:T(8,128)(2,1)S(1)}, u32[]{:S(2)}, u32[]{:S(2)}) collective-permute-start(bf16[1056,128]{1,0:T(8,128)(2,1)S(1)} %get-tuple-element.27), channel_id=1, source_target_pairs={{8,20},{12,16},{9,21},{13,17},{10,22},{14,18},{11,23},{15,19}} | collective-permute-start | bytes 811016 | tf_op jit(solution)/shard_map/ppermute | solution.py:575
  58.1 1.4 %collective-permute-start.13 = (bf16[1056,128]{1,0:T(8,128)(2,1)S(1)}, bf16[1056,128]{1,0:T(8,128)(2,1)S(1)}, u32[]{:S(2)}, u32[]{:S(2)}) collective-permute-start(bf16[1056,128]{1,0:T(8,128)(2,1)S(1)} %get-tuple-element.28), channel_id=1, source_target_pairs={{8,28},{12,24},{9,29},{13,25},{10,30},{14,26},{11,31},{15,27}} | collective-permute-start | bytes 811016 | tf_op jit(solution)/shard_map/ppermute | solution.py:575
  59.5 6.1 %shard_map.37 = (bf16[1056,128]{1,0:T(8,128)(2,1)S(1)}, bf16[1056,128]{1,0:T(8,128)(2,1)S(1)}) custom-call(s32[24,128]{1,0:T(8,128)S(1)} %block_tables.1.tab, bf16[1024,128]{1,0:T(8,128)(2,1)S(1)} %get-tuple-element.20.refs_0_, bf16[2,1024,128]{2,1,0:T(8,128)(2,1)S(1)} %get-tuple-element.21.refs_1_.refs_2_, ...), custom_call_target="tpu_custom_call" | custom-call | tf_op jit(solution)/shard_map/pallas_call | solution.py:465
  66.4 1.3 %collective-permute-start.6 = (bf16[1056,128]{1,0:T(8,128)(2,1)S(1)}, bf16[1056,128]{1,0:T(8,128)(2,1)S(1)}, u32[]{:S(2)}, u32[]{:S(2)}) collective-permute-start(bf16[1056,128]{1,0:T(8,128)(2,1)S(1)} %get-tuple-element.25), channel_id=1, source_target_pairs={{0,4},{4,0},{8,12},{12,8},{16,20},{20,16},{24,28},{28,24},{1,5},{5... | collective-permute-start | bytes 811016 | tf_op jit(solution)/shard_map/ppermute | solution.py:575
  68.8 2.9 %collective-permute-done.6.own = bf16[1056,128]{1,0:T(8,128)(2,1)S(1)} collective-permute-done((bf16[1056,128]{1,0:T(8,128)(2,1)S(1)}, bf16[1056,128]{1,0:T(8,128)(2,1)S(1)}, u32[]{:S(2)}, u32[]{:S(2)}) %collective-permute-start.6) | collective-permute-done | bytes 270368 | tf_op jit(solution)/shard_map/ppermute | solution.py:575
  72.5 1.8 %collective-permute-start.14 = (bf16[1024,128]{1,0:T(8,128)(2,1)S(1)}, bf16[1024,128]{1,0:T(8,128)(2,1)S(1)}, u32[]{:S(2)}, u32[]{:S(2)}) collective-permute-start(bf16[1024,128]{1,0:T(8,128)(2,1)S(1)} %combine.2.refs_0_), channel_id=1, source_target_pairs={{0,2},{1,3},{2,0},{3,1},{4,6},{5,7},{6,4},{7,5},{8,10},{9,11},{10,... | collective-permute-start | bytes 786440 | tf_op jit(solution)/shard_map/ppermute | solution.py:578
  74.4 3.1 %collective-permute-start.22 = (bf16[1024,128]{1,0:T(8,128)(2,1)S(1)}, bf16[1024,128]{1,0:T(8,128)(2,1)S(1)}, u32[]{:S(2)}, u32[]{:S(2)}) collective-permute-start(bf16[1024,128]{1,0:T(8,128)(2,1)S(1)} %combine.3.refs_0_), channel_id=1, source_target_pairs={{0,1},{1,0},{2,3},{3,2},{4,5},{5,4},{6,7},{7,6},{8,9},{9,8},{10,11... | collective-permute-start | bytes 786440 | tf_op jit(solution)/shard_map/ppermute | solution.py:578
  77.4 4.2 %collective-permute-start.24 = (bf16[1024,128]{1,0:T(8,128)(2,1)S(1)}, bf16[1024,128]{1,0:T(8,128)(2,1)S(1)}, u32[]{:S(2)}, u32[]{:S(2)}) collective-permute-start(bf16[1024,128]{1,0:T(8,128)(2,1)S(1)} %collective-permute-done.23.refs_2_), channel_id=1, source_target_pairs={{0,1},{1,0},{2,3},{3,2},{4,5},{5,4},{6,7},{7,6},{8,9},{9,8},{10,11... | collective-permute-start | bytes 786440 | tf_op jit(solution)/shard_map/ppermute | solution.py:578
  81.6 2.8 %collective-permute-start.15 = (bf16[1024,128]{1,0:T(8,128)(2,1)S(1)}, bf16[1024,128]{1,0:T(8,128)(2,1)S(1)}, u32[]{:S(2)}, u32[]{:S(2)}) collective-permute-start(bf16[1024,128]{1,0:T(8,128)(2,1)S(1)} %collective-permute-done.14.refs_0_), channel_id=1, source_target_pairs={{0,1},{1,0},{2,3},{3,2},{4,5},{5,4},{6,7},{7,6},{8,9},{9,8},{10,11... | collective-permute-start | bytes 786440 | tf_op jit(solution)/shard_map/ppermute | solution.py:578
  84.4 2.7 %project.3.refs_2_ = f32[1024,1024]{1,0:T(8,128)S(1)} custom-call(s32[1,3]{1,0:T(1,128)S(1)} %add_bitcast_fusion.ids_ref, bf16[1024,1024]{1,0:T(8,128)(2,1)S(1)} %copy-done, bf16[1024,128]{1,0:T(8,128)(2,1)S(1)} %combine.3.refs_0_, bf16[1024,128]{1,0:T(8,128)(2,1)S(1)} %collective-permute-done.22.refs_1_, ...), custom_call_target="tpu_custom_call" | custom-call | tf_op jit(solution)/shard_map/project/pallas_call | solution.py:548
  87.1 2.2 %project.4.refs_2_ = f32[1024,1024]{1,0:T(8,128)S(1)} custom-call(s32[1,3]{1,0:T(1,128)S(1)} %add_bitcast_fusion.ids_ref, bf16[1024,1024]{1,0:T(8,128)(2,1)S(1)} %copy-done, bf16[1024,128]{1,0:T(8,128)(2,1)S(1)} %combine.2.refs_0_, bf16[1024,128]{1,0:T(8,128)(2,1)S(1)} %collective-permute-done.16.refs_1_, f32[1024,1024]{1,0:T(8,128)S(1)} %project.3.refs_2_), custom_call_target="tpu_custom_call" | custom-call | tf_op jit(solution)/shard_map/project/pallas_call | solution.py:548
  89.3 3.1 %project.5 = bf16[1024,1024]{1,0:T(8,128)(2,1)} custom-call(s32[1,3]{1,0:T(1,128)S(1)} %add_bitcast_fusion.ids_ref, bf16[1024,1024]{1,0:T(8,128)(2,1)S(1)} %copy-done, bf16[1024,128]{1,0:T(8,128)(2,1)S(1)} %collective-permute-done.14.refs_0_, bf16[1024,128]{1,0:T(8,128)(2,1)S(1)} %collective-permute-done.15.refs_1_, f32[1024,1024]{1,0:T(8,128)S(1)} %project.4.refs_2_), custom_call_target="tpu_custom_call" | custom-call | tf_op jit(solution)/shard_map/project/pallas_call | solution.py:548
  (36 shorter events, 7.7 us)
Async XLA Ops:
  0.0 22.1 %copy-start.1 = (s32[2,64]{1,0:T(2,128)S(1)}, s32[2,64]{1,0:T(2,128)}, u32[]{:S(2)}) copy-start(s32[2,64]{1,0:T(2,128)} %table_ref.1) | copy-start | bytes 1540
  3.1 7.3 %collective-permute-start = (bf16[1024,128]{1,0:T(8,128)(2,1)S(1)}, bf16[1024,128]{1,0:T(8,128)(2,1)S(1)}, u32[]{:S(2)}, u32[]{:S(2)}) collective-permute-start(bf16[1024,128]{1,0:T(8,128)(2,1)S(1)} %get-tuple-element.22), channel_id=1, source_target_pairs={{0,4},{4,0},{8,12},{12,8},{16,20},{20,16},{24,28},{28,24},{1,5},{5... | collective-permute-start | bytes 786440 | tf_op jit(solution)/shard_map/ppermute | solution.py:575
  4.4 18.5 %collective-permute-start.3 = (bf16[2,1024,128]{2,1,0:T(8,128)(2,1)S(1)}, bf16[2,1024,128]{2,1,0:T(8,128)(2,1)S(1)}, u32[]{:S(2)}, u32[]{:S(2)}) collective-permute-start(bf16[2,1024,128]{2,1,0:T(8,128)(2,1)S(1)} %get-tuple-element.21.refs_1_.refs_2_), channel_id=1, source_target_pairs={{0,8},{4,12},{1,9},{5,13},{2,10},{6,14},{3,11},{7,15}} | collective-permute-start | bytes 1572872 | tf_op jit(solution)/shard_map/ppermute | solution.py:575
  5.7 10.3 %collective-permute-start.1 = (bf16[1024,128]{1,0:T(8,128)(2,1)S(1)}, bf16[1024,128]{1,0:T(8,128)(2,1)S(1)}, u32[]{:S(2)}, u32[]{:S(2)}) collective-permute-start(bf16[1024,128]{1,0:T(8,128)(2,1)S(1)} %get-tuple-element.23), channel_id=1, source_target_pairs={{0,4},{4,0},{8,12},{12,8},{16,20},{20,16},{24,28},{28,24},{1,5},{5... | collective-permute-start | bytes 786440 | tf_op jit(solution)/shard_map/ppermute | solution.py:575
  6.0 14.1 %collective-permute-start.18 = (bf16[1024,128]{1,0:T(8,128)(2,1)S(1)}, bf16[1024,128]{1,0:T(8,128)(2,1)S(1)}, u32[]{:S(2)}, u32[]{:S(2)}) collective-permute-start(bf16[1024,128]{1,0:T(8,128)(2,1)S(1)} %get-tuple-element.20.refs_0_), channel_id=1, source_target_pairs={{16,8},{20,12},{17,9},{21,13},{18,10},{22,14},{19,11},{23,15}} | collective-permute-start | bytes 786440 | tf_op jit(solution)/shard_map/ppermute | solution.py:575
  7.3 14.1 %collective-permute-start.19 = (bf16[1024,128]{1,0:T(8,128)(2,1)S(1)}, bf16[1024,128]{1,0:T(8,128)(2,1)S(1)}, u32[]{:S(2)}, u32[]{:S(2)}) collective-permute-start(bf16[1024,128]{1,0:T(8,128)(2,1)S(1)} %get-tuple-element.20.refs_0_), channel_id=1, source_target_pairs={{24,8},{28,12},{25,9},{29,13},{26,10},{30,14},{27,11},{31,15}} | collective-permute-start | bytes 786440 | tf_op jit(solution)/shard_map/ppermute | solution.py:575
  10.4 12.5 %collective-permute-start.2 = (bf16[1024,128]{1,0:T(8,128)(2,1)S(1)}, bf16[1024,128]{1,0:T(8,128)(2,1)S(1)}, u32[]{:S(2)}, u32[]{:S(2)}) collective-permute-start(bf16[1024,128]{1,0:T(8,128)(2,1)S(1)} %get-tuple-element.24), channel_id=1, source_target_pairs={{0,4},{4,0},{8,12},{12,8},{16,20},{20,16},{24,28},{28,24},{1,5},{5... | collective-permute-start | bytes 786440 | tf_op jit(solution)/shard_map/ppermute | solution.py:575
  16.0 12.2 %collective-permute-start.4 = (bf16[1024,128]{1,0:T(8,128)(2,1)S(1)}, bf16[1024,128]{1,0:T(8,128)(2,1)S(1)}, u32[]{:S(2)}, u32[]{:S(2)}) collective-permute-start(bf16[1024,128]{1,0:T(8,128)(2,1)S(1)} %collective-permute-done.refs_2_.refs_3_), channel_id=1, source_target_pairs={{0,8},{4,12},{1,9},{5,13},{2,10},{6,14},{3,11},{7,15}} | collective-permute-start | bytes 786440 | tf_op jit(solution)/shard_map/ppermute | solution.py:575
  20.1 10.2 %collective-permute-start.5 = (bf16[1024,128]{1,0:T(8,128)(2,1)S(1)}, bf16[1024,128]{1,0:T(8,128)(2,1)S(1)}, u32[]{:S(2)}, u32[]{:S(2)}) collective-permute-start(bf16[1024,128]{1,0:T(8,128)(2,1)S(1)} %collective-permute-done.1.refs_3_.refs_4_), channel_id=1, source_target_pairs={{0,8},{4,12},{1,9},{5,13},{2,10},{6,14},{3,11},{7,15}} | collective-permute-start | bytes 786440 | tf_op jit(solution)/shard_map/ppermute | solution.py:575
  21.4 17.2 %collective-permute-start.7 = (bf16[1024,128]{1,0:T(8,128)(2,1)S(1)}, bf16[1024,128]{1,0:T(8,128)(2,1)S(1)}, u32[]{:S(2)}, u32[]{:S(2)}) collective-permute-start(bf16[1024,128]{1,0:T(8,128)(2,1)S(1)} %get-tuple-element.20.refs_0_), channel_id=1, source_target_pairs={{24,16},{28,20},{25,17},{29,21},{26,18},{30,22},{27,19},{31,23}} | collective-permute-start | bytes 786440 | tf_op jit(solution)/shard_map/ppermute | solution.py:575
  34.0 31.7 %collective-permute-start.20 = (bf16[1056,128]{1,0:T(8,128)(2,1)S(1)}, bf16[1056,128]{1,0:T(8,128)(2,1)S(1)}, u32[]{:S(2)}, u32[]{:S(2)}) collective-permute-start(bf16[1056,128]{1,0:T(8,128)(2,1)S(1)} %get-tuple-element.33), channel_id=1, source_target_pairs={{8,16},{12,20},{9,17},{13,21},{10,18},{14,22},{11,19},{15,23}} | collective-permute-start | bytes 811016 | tf_op jit(solution)/shard_map/ppermute | solution.py:575
  35.3 31.1 %collective-permute-start.21 = (bf16[1056,128]{1,0:T(8,128)(2,1)S(1)}, bf16[1056,128]{1,0:T(8,128)(2,1)S(1)}, u32[]{:S(2)}, u32[]{:S(2)}) collective-permute-start(bf16[1056,128]{1,0:T(8,128)(2,1)S(1)} %get-tuple-element.34), channel_id=1, source_target_pairs={{8,24},{12,28},{9,25},{13,29},{10,26},{14,30},{11,27},{15,31}} | collective-permute-start | bytes 811016 | tf_op jit(solution)/shard_map/ppermute | solution.py:575
  36.6 3.3 %collective-permute-start.8 = (bf16[1024,128]{1,0:T(8,128)(2,1)S(1)}, bf16[1024,128]{1,0:T(8,128)(2,1)S(1)}, u32[]{:S(2)}, u32[]{:S(2)}) collective-permute-start(bf16[1024,128]{1,0:T(8,128)(2,1)S(1)} %collective-permute-done.refs_2_.refs_3_), channel_id=1, source_target_pairs={{24,16},{28,20},{25,17},{29,21},{26,18},{30,22},{27,19},{31,23}} | collective-permute-start | bytes 786440 | tf_op jit(solution)/shard_map/ppermute | solution.py:575
  37.3 13.5 %collective-permute-start.10 = (bf16[1024,128]{1,0:T(8,128)(2,1)S(1)}, bf16[1024,128]{1,0:T(8,128)(2,1)S(1)}, u32[]{:S(2)}, u32[]{:S(2)}) collective-permute-start(bf16[1024,128]{1,0:T(8,128)(2,1)S(1)} %collective-permute-done.refs_2_.refs_3_), channel_id=1, source_target_pairs={{16,8},{20,12},{17,9},{21,13},{18,10},{22,14},{19,11},{23,15}} | collective-permute-start | bytes 786440 | tf_op jit(solution)/shard_map/ppermute | solution.py:575
  38.6 12.2 %collective-permute-start.11 = (bf16[1024,128]{1,0:T(8,128)(2,1)S(1)}, bf16[1024,128]{1,0:T(8,128)(2,1)S(1)}, u32[]{:S(2)}, u32[]{:S(2)}) collective-permute-start(bf16[1024,128]{1,0:T(8,128)(2,1)S(1)} %collective-permute-done.refs_2_.refs_3_), channel_id=1, source_target_pairs={{24,8},{28,12},{25,9},{29,13},{26,10},{30,14},{27,11},{31,15}} | collective-permute-start | bytes 786440 | tf_op jit(solution)/shard_map/ppermute | solution.py:575
  40.7 27.0 %collective-permute-start.17 = (bf16[1056,128]{1,0:T(8,128)(2,1)S(1)}, bf16[1056,128]{1,0:T(8,128)(2,1)S(1)}, u32[]{:S(2)}, u32[]{:S(2)}) collective-permute-start(bf16[1056,128]{1,0:T(8,128)(2,1)S(1)} %get-tuple-element.30), channel_id=1, source_target_pairs={{16,24},{20,28},{17,25},{21,29},{18,26},{22,30},{19,27},{23,31}} | collective-permute-start | bytes 811016 | tf_op jit(solution)/shard_map/ppermute | solution.py:575
  56.8 12.0 %collective-permute-start.12 = (bf16[1056,128]{1,0:T(8,128)(2,1)S(1)}, bf16[1056,128]{1,0:T(8,128)(2,1)S(1)}, u32[]{:S(2)}, u32[]{:S(2)}) collective-permute-start(bf16[1056,128]{1,0:T(8,128)(2,1)S(1)} %get-tuple-element.27), channel_id=1, source_target_pairs={{8,20},{12,16},{9,21},{13,17},{10,22},{14,18},{11,23},{15,19}} | collective-permute-start | bytes 811016 | tf_op jit(solution)/shard_map/ppermute | solution.py:575
  58.1 26.4 %copy-start = (bf16[1024,1024]{1,0:T(8,128)(2,1)S(1)}, bf16[1024,1024]{1,0:T(8,128)(2,1)}, u32[]{:S(2)}) copy-start(bf16[1024,1024]{1,0:T(8,128)(2,1)} %weight_ref.5) | copy-start | bytes 6291460
  58.1 10.7 %collective-permute-start.13 = (bf16[1056,128]{1,0:T(8,128)(2,1)S(1)}, bf16[1056,128]{1,0:T(8,128)(2,1)S(1)}, u32[]{:S(2)}, u32[]{:S(2)}) collective-permute-start(bf16[1056,128]{1,0:T(8,128)(2,1)S(1)} %get-tuple-element.28), channel_id=1, source_target_pairs={{8,28},{12,24},{9,29},{13,25},{10,30},{14,26},{11,31},{15,27}} | collective-permute-start | bytes 811016 | tf_op jit(solution)/shard_map/ppermute | solution.py:575
  65.7 3.1 %collective-permute-start.9 = (bf16[1056,128]{1,0:T(8,128)(2,1)S(1)}, bf16[1056,128]{1,0:T(8,128)(2,1)S(1)}, u32[]{:S(2)}, u32[]{:S(2)}) collective-permute-start(bf16[1056,128]{1,0:T(8,128)(2,1)S(1)} %get-tuple-element.26), channel_id=1, source_target_pairs={{16,28},{20,24},{17,29},{21,25},{18,30},{22,26},{19,31},{23,27}} | collective-permute-start | bytes 811016 | tf_op jit(solution)/shard_map/ppermute | solution.py:575
  66.4 5.4 %collective-permute-start.6 = (bf16[1056,128]{1,0:T(8,128)(2,1)S(1)}, bf16[1056,128]{1,0:T(8,128)(2,1)S(1)}, u32[]{:S(2)}, u32[]{:S(2)}) collective-permute-start(bf16[1056,128]{1,0:T(8,128)(2,1)S(1)} %get-tuple-element.25), channel_id=1, source_target_pairs={{0,4},{4,0},{8,12},{12,8},{16,20},{20,16},{24,28},{28,24},{1,5},{5... | collective-permute-start | bytes 811016 | tf_op jit(solution)/shard_map/ppermute | solution.py:575
  68.5 8.9 %collective-permute-start.23 = (bf16[1024,128]{1,0:T(8,128)(2,1)S(1)}, bf16[1024,128]{1,0:T(8,128)(2,1)S(1)}, u32[]{:S(2)}, u32[]{:S(2)}) collective-permute-start(bf16[1024,128]{1,0:T(8,128)(2,1)S(1)} %combine.3.refs_0_), channel_id=1, source_target_pairs={{0,2},{1,3},{2,0},{3,1},{4,6},{5,7},{6,4},{7,5},{8,10},{9,11},{10,... | collective-permute-start | bytes 786440 | tf_op jit(solution)/shard_map/ppermute | solution.py:578
  72.5 9.1 %collective-permute-start.14 = (bf16[1024,128]{1,0:T(8,128)(2,1)S(1)}, bf16[1024,128]{1,0:T(8,128)(2,1)S(1)}, u32[]{:S(2)}, u32[]{:S(2)}) collective-permute-start(bf16[1024,128]{1,0:T(8,128)(2,1)S(1)} %combine.2.refs_0_), channel_id=1, source_target_pairs={{0,2},{1,3},{2,0},{3,1},{4,6},{5,7},{6,4},{7,5},{8,10},{9,11},{10,... | collective-permute-start | bytes 786440 | tf_op jit(solution)/shard_map/ppermute | solution.py:578
  74.4 10.1 %collective-permute-start.22 = (bf16[1024,128]{1,0:T(8,128)(2,1)S(1)}, bf16[1024,128]{1,0:T(8,128)(2,1)S(1)}, u32[]{:S(2)}, u32[]{:S(2)}) collective-permute-start(bf16[1024,128]{1,0:T(8,128)(2,1)S(1)} %combine.3.refs_0_), channel_id=1, source_target_pairs={{0,1},{1,0},{2,3},{3,2},{4,5},{5,4},{6,7},{7,6},{8,9},{9,8},{10,11... | collective-permute-start | bytes 786440 | tf_op jit(solution)/shard_map/ppermute | solution.py:578
  77.4 7.0 %collective-permute-start.24 = (bf16[1024,128]{1,0:T(8,128)(2,1)S(1)}, bf16[1024,128]{1,0:T(8,128)(2,1)S(1)}, u32[]{:S(2)}, u32[]{:S(2)}) collective-permute-start(bf16[1024,128]{1,0:T(8,128)(2,1)S(1)} %collective-permute-done.23.refs_2_), channel_id=1, source_target_pairs={{0,1},{1,0},{2,3},{3,2},{4,5},{5,4},{6,7},{7,6},{8,9},{9,8},{10,11... | collective-permute-start | bytes 786440 | tf_op jit(solution)/shard_map/ppermute | solution.py:578
  81.6 5.5 %collective-permute-start.16 = (bf16[1024,128]{1,0:T(8,128)(2,1)S(1)}, bf16[1024,128]{1,0:T(8,128)(2,1)S(1)}, u32[]{:S(2)}, u32[]{:S(2)}) collective-permute-start(bf16[1024,128]{1,0:T(8,128)(2,1)S(1)} %combine.2.refs_0_), channel_id=1, source_target_pairs={{0,1},{1,0},{2,3},{3,2},{4,5},{5,4},{6,7},{7,6},{8,9},{9,8},{10,11... | collective-permute-start | bytes 786440 | tf_op jit(solution)/shard_map/ppermute | solution.py:578
  81.6 7.7 %collective-permute-start.15 = (bf16[1024,128]{1,0:T(8,128)(2,1)S(1)}, bf16[1024,128]{1,0:T(8,128)(2,1)S(1)}, u32[]{:S(2)}, u32[]{:S(2)}) collective-permute-start(bf16[1024,128]{1,0:T(8,128)(2,1)S(1)} %collective-permute-done.14.refs_0_), channel_id=1, source_target_pairs={{0,1},{1,0},{2,3},{3,2},{4,5},{5,4},{6,7},{7,6},{8,9},{9,8},{10,11... | collective-permute-start | bytes 786440 | tf_op jit(solution)/shard_map/ppermute | solution.py:578

commit v6 on v5

--- a/solution.py
+++ b/solution.py
@@ -517,17 +517,20 @@
     )(ids, *values)
 
 
-def project_kernel(other, which, ids_ref, weight_ref, *refs):
+def project_kernel(which, ids_ref, weight_ref, *refs):
     group = ids_ref[0, 2]
     column = ids_ref[0, 0]
-    head = 1 - column if other else column
+    heads = (column, 1 - column)
     out_ref = refs[-1]
     features = refs[: len(which)]
     given = refs[len(which)] if len(refs) > len(which) + 1 else None
     depth = features[0].shape[1]
     cols = out_ref.shape[1]
     here = pl.ds(pl.multiple_of(pl.program_id(0) * cols, cols), cols)
-    lines = [pl.ds(pl.multiple_of(((group ^ j) * 2 + head) * depth, depth), depth) for j in which]
+    lines = [
+        pl.ds(pl.multiple_of(((group ^ j) * 2 + heads[part]) * depth, depth), depth)
+        for part, j in which
+    ]
     right = jnp.concatenate([weight_ref[at, here] for at in lines], axis=0)
     chunk = 512
     for start in range(0, out_ref.shape[0], chunk):
@@ -539,14 +542,14 @@
         out_ref[rows, :] = acc.astype(out_ref.dtype)
 
 
-def project(other, final, which, ids, weight, features, given):
+def project(final, which, ids, weight, features, given):
     rows = features[0].shape[0]
     vmem = pl.BlockSpec(memory_space=pltpu.VMEM)
     given = [] if given is None else [given]
     width = weight.shape[1]
     step = width // 4
     return pl.pallas_call(
-        functools.partial(project_kernel, other, which),
+        functools.partial(project_kernel, which),
         grid=(width // step,),
         in_specs=[pl.BlockSpec(memory_space=pltpu.SMEM)]
         + [vmem] * (1 + len(features) + len(given)),
@@ -618,6 +621,7 @@
     own_other = send(own_swap, swap)
     half = head_count // 2
     out = None
+    pieces = []
     for part, values in enumerate(
         (
             (own_keep, down_keep, back2_keep, back3_keep),
@@ -628,14 +632,10 @@
         over = across(local, half)
         beside = across(local, 1)
         over_beside = across(over, 1)
-        if part == 0:
-            out = project(
-                False, False, (0, 1, 2, 3), ids, out_weight,
-                (local, beside, over, over_beside), None,
-            )
-        else:
-            out = project(True, False, (0, 1), ids, out_weight, (local, beside), out)
-            out = project(True, True, (2, 3), ids, out_weight, (over, over_beside), out)
+        pieces += [((part, 0), local), ((part, 1), beside), ((part, 2), over), ((part, 3), over_beside)]
+    for step, chosen in enumerate((pieces[:2], pieces[2:6], pieces[6:])):
+        which, features = zip(*chosen)
+        out = project(step == 2, which, ids, out_weight, features, out)
     return out
 
 

time: 92.7 us -> 92.7 us (level)
  no operation moved by 1% of the time
where the time goes in v6:
time: 92.7 us; the launch traced here: 92.4 us
  starting transfers between devices  33.4 us (36%)
  Pallas kernels  33.3 us (36%)
  waiting for transfers between devices  23.7 us (26%)
  local copies, waits for them, and re-layouts  1.63 us (2%)
    ppermute x19, waiting for transfers between devices, send(): return lax.ppermute(value, 'seq', pairs)  23.6 us
    pallas_call x5, Pallas kernels, attend(): pl.pallas_call(functools.partial(attend_kernel, kind, per_shard, cluster_...  21.7 us
    ppermute x19, starting transfers between devices, send(): return lax.ppermute(value, 'seq', pairs)  21.2 us
    ppermute x6, starting transfers between devices, across(): lax.ppermute(value, 'head', [(g, g ^ flip) for g in range(head_count)])  12.2 us
    pallas_call x3, Pallas kernels, project(): pl.pallas_call(functools.partial(project_kernel, which), grid=(width // s...  7.89 us
  transfers between devices with their start and end apart: 25, of which 6 were waited for; matrix products, arithmetic and copies ran while one was open for 0% of the time, Pallas kernels for 31%

profile of v6, /device:TPU:13, one launch (start us, length us, event | category | flops | bytes accessed | tf_op | source)
XLA Modules:
  0.0 92.4 jit_solution(9848678325359013551)
XLA Ops:
  0.0 1.6 %copy.6 = bf16[1024,2,384]{2,0,1:T(8,128)(2,1)S(1)} copy(bf16[1024,2,384]{2,1,0:T(2,128)(2,1)} %param.3) | data formatting | bytes 3145728 | tf_op args[0]
  1.7 1.4 %split_heads.1 = (bf16[1024,128]{1,0:T(8,128)(2,1)S(1)}, bf16[2,1024,128]{2,1,0:T(8,128)(2,1)S(1)}, bf16[1024,128]{1,0:T(8,128)(2,1)S(1)}, bf16[1024,128]{1,0:T(8,128)(2,1)S(1)}, bf16[1024,128]{1,0:T(8,128)(2,1)S(1)}) custom-call(s32[1,3]{1,0:T(1,128)S(1)} %add_bitcast_fusion.ids_ref, bf16[2,1024,384]{2,1,0:T(8,128)(2,1)S(1)} %bitcast.8), custom_call_target="tpu_custom_call" | custom-call | tf_op jit(solution)/shard_map/split_heads/pallas_call | solution.py:180
  3.1 1.3 %collective-permute-start = (bf16[1024,128]{1,0:T(8,128)(2,1)S(1)}, bf16[1024,128]{1,0:T(8,128)(2,1)S(1)}, u32[]{:S(2)}, u32[]{:S(2)}) collective-permute-start(bf16[1024,128]{1,0:T(8,128)(2,1)S(1)} %get-tuple-element.22), channel_id=1, source_target_pairs={{0,4},{4,0},{8,12},{12,8},{16,20},{20,16},{24,28},{28,24},{1,5},{5... | collective-permute-start | bytes 786440 | tf_op jit(solution)/shard_map/ppermute | solution.py:578
  4.4 1.3 %collective-permute-start.3 = (bf16[2,1024,128]{2,1,0:T(8,128)(2,1)S(1)}, bf16[2,1024,128]{2,1,0:T(8,128)(2,1)S(1)}, u32[]{:S(2)}, u32[]{:S(2)}) collective-permute-start(bf16[2,1024,128]{2,1,0:T(8,128)(2,1)S(1)} %get-tuple-element.21.refs_1_.refs_2_), channel_id=1, source_target_pairs={{0,8},{4,12},{1,9},{5,13},{2,10},{6,14},{3,11},{7,15}} | collective-permute-start | bytes 1572872 | tf_op jit(solution)/shard_map/ppermute | solution.py:578
  6.0 1.3 %collective-permute-start.17 = (bf16[1024,128]{1,0:T(8,128)(2,1)S(1)}, bf16[1024,128]{1,0:T(8,128)(2,1)S(1)}, u32[]{:S(2)}, u32[]{:S(2)}) collective-permute-start(bf16[1024,128]{1,0:T(8,128)(2,1)S(1)} %get-tuple-element.20.refs_0_), channel_id=1, source_target_pairs={{16,8},{20,12},{17,9},{21,13},{18,10},{22,14},{19,11},{23,15}} | collective-permute-start | bytes 786440 | tf_op jit(solution)/shard_map/ppermute | solution.py:578
  7.3 1.3 %collective-permute-start.18 = (bf16[1024,128]{1,0:T(8,128)(2,1)S(1)}, bf16[1024,128]{1,0:T(8,128)(2,1)S(1)}, u32[]{:S(2)}, u32[]{:S(2)}) collective-permute-start(bf16[1024,128]{1,0:T(8,128)(2,1)S(1)} %get-tuple-element.20.refs_0_), channel_id=1, source_target_pairs={{24,8},{28,12},{25,9},{29,13},{26,10},{30,14},{27,11},{31,15}} | collective-permute-start | bytes 786440 | tf_op jit(solution)/shard_map/ppermute | solution.py:578
  8.6 1.8 %collective-permute-done.refs_2_.refs_3_ = bf16[1024,128]{1,0:T(8,128)(2,1)S(1)} collective-permute-done((bf16[1024,128]{1,0:T(8,128)(2,1)S(1)}, bf16[1024,128]{1,0:T(8,128)(2,1)S(1)}, u32[]{:S(2)}, u32[]{:S(2)}) %collective-permute-start) | collective-permute-done | bytes 262176 | tf_op jit(solution)/shard_map/ppermute | solution.py:578
  11.6 4.4 %collective-permute-done.1.refs_3_.refs_4_ = bf16[1024,128]{1,0:T(8,128)(2,1)S(1)} collective-permute-done((bf16[1024,128]{1,0:T(8,128)(2,1)S(1)}, bf16[1024,128]{1,0:T(8,128)(2,1)S(1)}, u32[]{:S(2)}, u32[]{:S(2)}) %collective-permute-start.1) | collective-permute-done | bytes 262176 | tf_op jit(solution)/shard_map/ppermute | solution.py:578
  16.0 1.3 %collective-permute-start.4 = (bf16[1024,128]{1,0:T(8,128)(2,1)S(1)}, bf16[1024,128]{1,0:T(8,128)(2,1)S(1)}, u32[]{:S(2)}, u32[]{:S(2)}) collective-permute-start(bf16[1024,128]{1,0:T(8,128)(2,1)S(1)} %collective-permute-done.refs_2_.refs_3_), channel_id=1, source_target_pairs={{0,8},{4,12},{1,9},{5,13},{2,10},{6,14},{3,11},{7,15}} | collective-permute-start | bytes 786440 | tf_op jit(solution)/shard_map/ppermute | solution.py:578
  17.3 2.8 %collective-permute-done.17.refs_0_ = bf16[1024,128]{1,0:T(8,128)(2,1)S(1)} collective-permute-done((bf16[1024,128]{1,0:T(8,128)(2,1)S(1)}, bf16[1024,128]{1,0:T(8,128)(2,1)S(1)}, u32[]{:S(2)}, u32[]{:S(2)}) %collective-permute-start.17) | collective-permute-done | bytes 262176 | tf_op jit(solution)/shard_map/ppermute | solution.py:578
  20.1 1.3 %collective-permute-start.5 = (bf16[1024,128]{1,0:T(8,128)(2,1)S(1)}, bf16[1024,128]{1,0:T(8,128)(2,1)S(1)}, u32[]{:S(2)}, u32[]{:S(2)}) collective-permute-start(bf16[1024,128]{1,0:T(8,128)(2,1)S(1)} %collective-permute-done.1.refs_3_.refs_4_), channel_id=1, source_target_pairs={{0,8},{4,12},{1,9},{5,13},{2,10},{6,14},{3,11},{7,15}} | collective-permute-start | bytes 786440 | tf_op jit(solution)/shard_map/ppermute | solution.py:578
  22.9 5.3 %shard_map.40 = (bf16[1056,128]{1,0:T(8,128)(2,1)S(1)}, bf16[1056,128]{1,0:T(8,128)(2,1)S(1)}) custom-call(s32[24,128]{1,0:T(8,128)S(1)} %block_tables.1.tab, bf16[1024,128]{1,0:T(8,128)(2,1)S(1)} %collective-permute-done.17.refs_0_, bf16[1024,128]{1,0:T(8,128)(2,1)S(1)} %collective-permute-done.18.refs_1_, ...), custom_call_target="tpu_custom_call" | custom-call | tf_op jit(solution)/shard_map/pallas_call | solution.py:465
  28.2 2.2 %collective-permute-done.5.refs_7_.refs_8_.refs_3_ = bf16[1024,128]{1,0:T(8,128)(2,1)S(1)} collective-permute-done((bf16[1024,128]{1,0:T(8,128)(2,1)S(1)}, bf16[1024,128]{1,0:T(8,128)(2,1)S(1)}, u32[]{:S(2)}, u32[]{:S(2)}) %collective-permute-start.5) | collective-permute-done | bytes 262176 | tf_op jit(solution)/shard_map/ppermute | solution.py:578
  30.3 3.6 %shard_map.41 = (bf16[1056,128]{1,0:T(8,128)(2,1)S(1)}, bf16[1056,128]{1,0:T(8,128)(2,1)S(1)}) custom-call(s32[24,128]{1,0:T(8,128)S(1)} %block_tables.1.tab, bf16[1024,128]{1,0:T(8,128)(2,1)S(1)} %collective-permute-done.17.refs_0_, bf16[1024,128]{1,0:T(8,128)(2,1)S(1)} %collective-permute-done.18.refs_1_, ...), custom_call_target="tpu_custom_call" | custom-call | tf_op jit(solution)/shard_map/pallas_call | solution.py:465
  34.0 1.3 %collective-permute-start.19 = (bf16[1056,128]{1,0:T(8,128)(2,1)S(1)}, bf16[1056,128]{1,0:T(8,128)(2,1)S(1)}, u32[]{:S(2)}, u32[]{:S(2)}) collective-permute-start(bf16[1056,128]{1,0:T(8,128)(2,1)S(1)} %get-tuple-element.33), channel_id=1, source_target_pairs={{8,16},{12,20},{9,17},{13,21},{10,18},{14,22},{11,19},{15,23}} | collective-permute-start | bytes 811016 | tf_op jit(solution)/shard_map/ppermute | solution.py:578
  35.3 1.3 %collective-permute-start.20 = (bf16[1056,128]{1,0:T(8,128)(2,1)S(1)}, bf16[1056,128]{1,0:T(8,128)(2,1)S(1)}, u32[]{:S(2)}, u32[]{:S(2)}) collective-permute-start(bf16[1056,128]{1,0:T(8,128)(2,1)S(1)} %get-tuple-element.34), channel_id=1, source_target_pairs={{8,24},{12,28},{9,25},{13,29},{10,26},{14,30},{11,27},{15,31}} | collective-permute-start | bytes 811016 | tf_op jit(solution)/shard_map/ppermute | solution.py:578
  37.3 1.3 %collective-permute-start.10 = (bf16[1024,128]{1,0:T(8,128)(2,1)S(1)}, bf16[1024,128]{1,0:T(8,128)(2,1)S(1)}, u32[]{:S(2)}, u32[]{:S(2)}) collective-permute-start(bf16[1024,128]{1,0:T(8,128)(2,1)S(1)} %collective-permute-done.refs_2_.refs_3_), channel_id=1, source_target_pairs={{16,8},{20,12},{17,9},{21,13},{18,10},{22,14},{19,11},{23,15}} | collective-permute-start | bytes 786440 | tf_op jit(solution)/shard_map/ppermute | solution.py:578
  38.6 1.3 %collective-permute-start.11 = (bf16[1024,128]{1,0:T(8,128)(2,1)S(1)}, bf16[1024,128]{1,0:T(8,128)(2,1)S(1)}, u32[]{:S(2)}, u32[]{:S(2)}) collective-permute-start(bf16[1024,128]{1,0:T(8,128)(2,1)S(1)} %collective-permute-done.refs_2_.refs_3_), channel_id=1, source_target_pairs={{24,8},{28,12},{25,9},{29,13},{26,10},{30,14},{27,11},{31,15}} | collective-permute-start | bytes 786440 | tf_op jit(solution)/shard_map/ppermute | solution.py:578
  41.3 9.5 %collective-permute-done.10.refs_0_ = bf16[1024,128]{1,0:T(8,128)(2,1)S(1)} collective-permute-done((bf16[1024,128]{1,0:T(8,128)(2,1)S(1)}, bf16[1024,128]{1,0:T(8,128)(2,1)S(1)}, u32[]{:S(2)}, u32[]{:S(2)}) %collective-permute-start.10) | collective-permute-done | bytes 262176 | tf_op jit(solution)/shard_map/ppermute | solution.py:578
  50.8 5.9 %shard_map.39 = (bf16[1056,128]{1,0:T(8,128)(2,1)S(1)}, bf16[1056,128]{1,0:T(8,128)(2,1)S(1)}) custom-call(s32[24,128]{1,0:T(8,128)S(1)} %block_tables.1.tab, bf16[1024,128]{1,0:T(8,128)(2,1)S(1)} %collective-permute-done.10.refs_0_, bf16[1024,128]{1,0:T(8,128)(2,1)S(1)} %collective-permute-done.11.refs_1_, ...), custom_call_target="tpu_custom_call" | custom-call | tf_op jit(solution)/shard_map/pallas_call | solution.py:465
  56.8 1.3 %collective-permute-start.12 = (bf16[1056,128]{1,0:T(8,128)(2,1)S(1)}, bf16[1056,128]{1,0:T(8,128)(2,1)S(1)}, u32[]{:S(2)}, u32[]{:S(2)}) collective-permute-start(bf16[1056,128]{1,0:T(8,128)(2,1)S(1)} %get-tuple-element.27), channel_id=1, source_target_pairs={{8,20},{12,16},{9,21},{13,17},{10,22},{14,18},{11,23},{15,19}} | collective-permute-start | bytes 811016 | tf_op jit(solution)/shard_map/ppermute | solution.py:578
  58.1 1.4 %collective-permute-start.13 = (bf16[1056,128]{1,0:T(8,128)(2,1)S(1)}, bf16[1056,128]{1,0:T(8,128)(2,1)S(1)}, u32[]{:S(2)}, u32[]{:S(2)}) collective-permute-start(bf16[1056,128]{1,0:T(8,128)(2,1)S(1)} %get-tuple-element.28), channel_id=1, source_target_pairs={{8,28},{12,24},{9,29},{13,25},{10,30},{14,26},{11,31},{15,27}} | collective-permute-start | bytes 811016 | tf_op jit(solution)/shard_map/ppermute | solution.py:578
  59.5 6.1 %shard_map.37 = (bf16[1056,128]{1,0:T(8,128)(2,1)S(1)}, bf16[1056,128]{1,0:T(8,128)(2,1)S(1)}) custom-call(s32[24,128]{1,0:T(8,128)S(1)} %block_tables.1.tab, bf16[1024,128]{1,0:T(8,128)(2,1)S(1)} %get-tuple-element.20.refs_0_, bf16[2,1024,128]{2,1,0:T(8,128)(2,1)S(1)} %get-tuple-element.21.refs_1_.refs_2_, ...), custom_call_target="tpu_custom_call" | custom-call | tf_op jit(solution)/shard_map/pallas_call | solution.py:465
  66.4 1.3 %collective-permute-start.6 = (bf16[1056,128]{1,0:T(8,128)(2,1)S(1)}, bf16[1056,128]{1,0:T(8,128)(2,1)S(1)}, u32[]{:S(2)}, u32[]{:S(2)}) collective-permute-start(bf16[1056,128]{1,0:T(8,128)(2,1)S(1)} %get-tuple-element.25), channel_id=1, source_target_pairs={{0,4},{4,0},{8,12},{12,8},{16,20},{20,16},{24,28},{28,24},{1,5},{5... | collective-permute-start | bytes 811016 | tf_op jit(solution)/shard_map/ppermute | solution.py:578
  68.8 2.9 %collective-permute-done.6.own = bf16[1056,128]{1,0:T(8,128)(2,1)S(1)} collective-permute-done((bf16[1056,128]{1,0:T(8,128)(2,1)S(1)}, bf16[1056,128]{1,0:T(8,128)(2,1)S(1)}, u32[]{:S(2)}, u32[]{:S(2)}) %collective-permute-start.6) | collective-permute-done | bytes 270368 | tf_op jit(solution)/shard_map/ppermute | solution.py:578
  72.5 1.8 %collective-permute-start.14 = (bf16[1024,128]{1,0:T(8,128)(2,1)S(1)}, bf16[1024,128]{1,0:T(8,128)(2,1)S(1)}, u32[]{:S(2)}, u32[]{:S(2)}) collective-permute-start(bf16[1024,128]{1,0:T(8,128)(2,1)S(1)} %combine.2.refs_2_), channel_id=1, source_target_pairs={{0,2},{1,3},{2,0},{3,1},{4,6},{5,7},{6,4},{7,5},{8,10},{9,11},{10,... | collective-permute-start | bytes 786440 | tf_op jit(solution)/shard_map/ppermute | solution.py:581
  74.4 3.1 %collective-permute-start.24 = (bf16[1024,128]{1,0:T(8,128)(2,1)S(1)}, bf16[1024,128]{1,0:T(8,128)(2,1)S(1)}, u32[]{:S(2)}, u32[]{:S(2)}) collective-permute-start(bf16[1024,128]{1,0:T(8,128)(2,1)S(1)} %combine.3.refs_0_), channel_id=1, source_target_pairs={{0,1},{1,0},{2,3},{3,2},{4,5},{5,4},{6,7},{7,6},{8,9},{9,8},{10,11... | collective-permute-start | bytes 786440 | tf_op jit(solution)/shard_map/ppermute | solution.py:581
  77.4 4.2 %collective-permute-start.22 = (bf16[1024,128]{1,0:T(8,128)(2,1)S(1)}, bf16[1024,128]{1,0:T(8,128)(2,1)S(1)}, u32[]{:S(2)}, u32[]{:S(2)}) collective-permute-start(bf16[1024,128]{1,0:T(8,128)(2,1)S(1)} %collective-permute-done.21.refs_0_), channel_id=1, source_target_pairs={{0,1},{1,0},{2,3},{3,2},{4,5},{5,4},{6,7},{7,6},{8,9},{9,8},{10,11... | collective-permute-start | bytes 786440 | tf_op jit(solution)/shard_map/ppermute | solution.py:581
  81.6 2.8 %collective-permute-start.15 = (bf16[1024,128]{1,0:T(8,128)(2,1)S(1)}, bf16[1024,128]{1,0:T(8,128)(2,1)S(1)}, u32[]{:S(2)}, u32[]{:S(2)}) collective-permute-start(bf16[1024,128]{1,0:T(8,128)(2,1)S(1)} %collective-permute-done.14.refs_0_), channel_id=1, source_target_pairs={{0,1},{1,0},{2,3},{3,2},{4,5},{5,4},{6,7},{7,6},{8,9},{9,8},{10,11... | collective-permute-start | bytes 786440 | tf_op jit(solution)/shard_map/ppermute | solution.py:581
  84.4 2.1 %project.3.refs_4_ = f32[1024,1024]{1,0:T(8,128)S(1)} custom-call(s32[1,3]{1,0:T(1,128)S(1)} %add_bitcast_fusion.ids_ref, bf16[1024,1024]{1,0:T(8,128)(2,1)S(1)} %copy-done, bf16[1024,128]{1,0:T(8,128)(2,1)S(1)} %combine.3.refs_0_, bf16[1024,128]{1,0:T(8,128)(2,1)S(1)} %collective-permute-done.24.refs_1_), custom_call_target="tpu_custom_call" | custom-call | tf_op jit(solution)/shard_map/project/pallas_call | solution.py:551
  86.5 2.7 %project.4.refs_2_ = f32[1024,1024]{1,0:T(8,128)S(1)} custom-call(s32[1,3]{1,0:T(1,128)S(1)} %add_bitcast_fusion.ids_ref, bf16[1024,1024]{1,0:T(8,128)(2,1)S(1)} %copy-done, bf16[1024,128]{1,0:T(8,128)(2,1)S(1)} %collective-permute-done.21.refs_0_, bf16[1024,128]{1,0:T(8,128)(2,1)S(1)} %collective-permute-done.22.refs_1_, ...), custom_call_target="tpu_custom_call" | custom-call | tf_op jit(solution)/shard_map/project/pallas_call | solution.py:551
  89.3 3.1 %project.5 = bf16[1024,1024]{1,0:T(8,128)(2,1)} custom-call(s32[1,3]{1,0:T(1,128)S(1)} %add_bitcast_fusion.ids_ref, bf16[1024,1024]{1,0:T(8,128)(2,1)S(1)} %copy-done, bf16[1024,128]{1,0:T(8,128)(2,1)S(1)} %collective-permute-done.14.refs_0_, bf16[1024,128]{1,0:T(8,128)(2,1)S(1)} %collective-permute-done.15.refs_1_, f32[1024,1024]{1,0:T(8,128)S(1)} %project.4.refs_2_), custom_call_target="tpu_custom_call" | custom-call | tf_op jit(solution)/shard_map/project/pallas_call | solution.py:551
  (36 shorter events, 7.7 us)
Async XLA Ops:
  0.0 22.1 %copy-start.1 = (s32[2,64]{1,0:T(2,128)S(1)}, s32[2,64]{1,0:T(2,128)}, u32[]{:S(2)}) copy-start(s32[2,64]{1,0:T(2,128)} %table_ref.1) | copy-start | bytes 1540
  3.1 7.3 %collective-permute-start = (bf16[1024,128]{1,0:T(8,128)(2,1)S(1)}, bf16[1024,128]{1,0:T(8,128)(2,1)S(1)}, u32[]{:S(2)}, u32[]{:S(2)}) collective-permute-start(bf16[1024,128]{1,0:T(8,128)(2,1)S(1)} %get-tuple-element.22), channel_id=1, source_target_pairs={{0,4},{4,0},{8,12},{12,8},{16,20},{20,16},{24,28},{28,24},{1,5},{5... | collective-permute-start | bytes 786440 | tf_op jit(solution)/shard_map/ppermute | solution.py:578
  4.4 18.5 %collective-permute-start.3 = (bf16[2,1024,128]{2,1,0:T(8,128)(2,1)S(1)}, bf16[2,1024,128]{2,1,0:T(8,128)(2,1)S(1)}, u32[]{:S(2)}, u32[]{:S(2)}) collective-permute-start(bf16[2,1024,128]{2,1,0:T(8,128)(2,1)S(1)} %get-tuple-element.21.refs_1_.refs_2_), channel_id=1, source_target_pairs={{0,8},{4,12},{1,9},{5,13},{2,10},{6,14},{3,11},{7,15}} | collective-permute-start | bytes 1572872 | tf_op jit(solution)/shard_map/ppermute | solution.py:578
  5.7 10.3 %collective-permute-start.1 = (bf16[1024,128]{1,0:T(8,128)(2,1)S(1)}, bf16[1024,128]{1,0:T(8,128)(2,1)S(1)}, u32[]{:S(2)}, u32[]{:S(2)}) collective-permute-start(bf16[1024,128]{1,0:T(8,128)(2,1)S(1)} %get-tuple-element.23), channel_id=1, source_target_pairs={{0,4},{4,0},{8,12},{12,8},{16,20},{20,16},{24,28},{28,24},{1,5},{5... | collective-permute-start | bytes 786440 | tf_op jit(solution)/shard_map/ppermute | solution.py:578
  6.0 14.1 %collective-permute-start.17 = (bf16[1024,128]{1,0:T(8,128)(2,1)S(1)}, bf16[1024,128]{1,0:T(8,128)(2,1)S(1)}, u32[]{:S(2)}, u32[]{:S(2)}) collective-permute-start(bf16[1024,128]{1,0:T(8,128)(2,1)S(1)} %get-tuple-element.20.refs_0_), channel_id=1, source_target_pairs={{16,8},{20,12},{17,9},{21,13},{18,10},{22,14},{19,11},{23,15}} | collective-permute-start | bytes 786440 | tf_op jit(solution)/shard_map/ppermute | solution.py:578
  7.3 14.1 %collective-permute-start.18 = (bf16[1024,128]{1,0:T(8,128)(2,1)S(1)}, bf16[1024,128]{1,0:T(8,128)(2,1)S(1)}, u32[]{:S(2)}, u32[]{:S(2)}) collective-permute-start(bf16[1024,128]{1,0:T(8,128)(2,1)S(1)} %get-tuple-element.20.refs_0_), channel_id=1, source_target_pairs={{24,8},{28,12},{25,9},{29,13},{26,10},{30,14},{27,11},{31,15}} | collective-permute-start | bytes 786440 | tf_op jit(solution)/shard_map/ppermute | solution.py:578
  10.4 12.5 %collective-permute-start.2 = (bf16[1024,128]{1,0:T(8,128)(2,1)S(1)}, bf16[1024,128]{1,0:T(8,128)(2,1)S(1)}, u32[]{:S(2)}, u32[]{:S(2)}) collective-permute-start(bf16[1024,128]{1,0:T(8,128)(2,1)S(1)} %get-tuple-element.24), channel_id=1, source_target_pairs={{0,4},{4,0},{8,12},{12,8},{16,20},{20,16},{24,28},{28,24},{1,5},{5... | collective-permute-start | bytes 786440 | tf_op jit(solution)/shard_map/ppermute | solution.py:578
  16.0 12.2 %collective-permute-start.4 = (bf16[1024,128]{1,0:T(8,128)(2,1)S(1)}, bf16[1024,128]{1,0:T(8,128)(2,1)S(1)}, u32[]{:S(2)}, u32[]{:S(2)}) collective-permute-start(bf16[1024,128]{1,0:T(8,128)(2,1)S(1)} %collective-permute-done.refs_2_.refs_3_), channel_id=1, source_target_pairs={{0,8},{4,12},{1,9},{5,13},{2,10},{6,14},{3,11},{7,15}} | collective-permute-start | bytes 786440 | tf_op jit(solution)/shard_map/ppermute | solution.py:578
  20.1 10.2 %collective-permute-start.5 = (bf16[1024,128]{1,0:T(8,128)(2,1)S(1)}, bf16[1024,128]{1,0:T(8,128)(2,1)S(1)}, u32[]{:S(2)}, u32[]{:S(2)}) collective-permute-start(bf16[1024,128]{1,0:T(8,128)(2,1)S(1)} %collective-permute-done.1.refs_3_.refs_4_), channel_id=1, source_target_pairs={{0,8},{4,12},{1,9},{5,13},{2,10},{6,14},{3,11},{7,15}} | collective-permute-start | bytes 786440 | tf_op jit(solution)/shard_map/ppermute | solution.py:578
  21.4 17.2 %collective-permute-start.7 = (bf16[1024,128]{1,0:T(8,128)(2,1)S(1)}, bf16[1024,128]{1,0:T(8,128)(2,1)S(1)}, u32[]{:S(2)}, u32[]{:S(2)}) collective-permute-start(bf16[1024,128]{1,0:T(8,128)(2,1)S(1)} %get-tuple-element.20.refs_0_), channel_id=1, source_target_pairs={{24,16},{28,20},{25,17},{29,21},{26,18},{30,22},{27,19},{31,23}} | collective-permute-start | bytes 786440 | tf_op jit(solution)/shard_map/ppermute | solution.py:578
  34.0 31.7 %collective-permute-start.19 = (bf16[1056,128]{1,0:T(8,128)(2,1)S(1)}, bf16[1056,128]{1,0:T(8,128)(2,1)S(1)}, u32[]{:S(2)}, u32[]{:S(2)}) collective-permute-start(bf16[1056,128]{1,0:T(8,128)(2,1)S(1)} %get-tuple-element.33), channel_id=1, source_target_pairs={{8,16},{12,20},{9,17},{13,21},{10,18},{14,22},{11,19},{15,23}} | collective-permute-start | bytes 811016 | tf_op jit(solution)/shard_map/ppermute | solution.py:578
  35.3 31.1 %collective-permute-start.20 = (bf16[1056,128]{1,0:T(8,128)(2,1)S(1)}, bf16[1056,128]{1,0:T(8,128)(2,1)S(1)}, u32[]{:S(2)}, u32[]{:S(2)}) collective-permute-start(bf16[1056,128]{1,0:T(8,128)(2,1)S(1)} %get-tuple-element.34), channel_id=1, source_target_pairs={{8,24},{12,28},{9,25},{13,29},{10,26},{14,30},{11,27},{15,31}} | collective-permute-start | bytes 811016 | tf_op jit(solution)/shard_map/ppermute | solution.py:578
  36.6 3.3 %collective-permute-start.8 = (bf16[1024,128]{1,0:T(8,128)(2,1)S(1)}, bf16[1024,128]{1,0:T(8,128)(2,1)S(1)}, u32[]{:S(2)}, u32[]{:S(2)}) collective-permute-start(bf16[1024,128]{1,0:T(8,128)(2,1)S(1)} %collective-permute-done.refs_2_.refs_3_), channel_id=1, source_target_pairs={{24,16},{28,20},{25,17},{29,21},{26,18},{30,22},{27,19},{31,23}} | collective-permute-start | bytes 786440 | tf_op jit(solution)/shard_map/ppermute | solution.py:578
  37.3 13.5 %collective-permute-start.10 = (bf16[1024,128]{1,0:T(8,128)(2,1)S(1)}, bf16[1024,128]{1,0:T(8,128)(2,1)S(1)}, u32[]{:S(2)}, u32[]{:S(2)}) collective-permute-start(bf16[1024,128]{1,0:T(8,128)(2,1)S(1)} %collective-permute-done.refs_2_.refs_3_), channel_id=1, source_target_pairs={{16,8},{20,12},{17,9},{21,13},{18,10},{22,14},{19,11},{23,15}} | collective-permute-start | bytes 786440 | tf_op jit(solution)/shard_map/ppermute | solution.py:578
  38.6 12.2 %collective-permute-start.11 = (bf16[1024,128]{1,0:T(8,128)(2,1)S(1)}, bf16[1024,128]{1,0:T(8,128)(2,1)S(1)}, u32[]{:S(2)}, u32[]{:S(2)}) collective-permute-start(bf16[1024,128]{1,0:T(8,128)(2,1)S(1)} %collective-permute-done.refs_2_.refs_3_), channel_id=1, source_target_pairs={{24,8},{28,12},{25,9},{29,13},{26,10},{30,14},{27,11},{31,15}} | collective-permute-start | bytes 786440 | tf_op jit(solution)/shard_map/ppermute | solution.py:578
  40.7 27.0 %collective-permute-start.16 = (bf16[1056,128]{1,0:T(8,128)(2,1)S(1)}, bf16[1056,128]{1,0:T(8,128)(2,1)S(1)}, u32[]{:S(2)}, u32[]{:S(2)}) collective-permute-start(bf16[1056,128]{1,0:T(8,128)(2,1)S(1)} %get-tuple-element.30), channel_id=1, source_target_pairs={{16,24},{20,28},{17,25},{21,29},{18,26},{22,30},{19,27},{23,31}} | collective-permute-start | bytes 811016 | tf_op jit(solution)/shard_map/ppermute | solution.py:578
  56.8 12.0 %collective-permute-start.12 = (bf16[1056,128]{1,0:T(8,128)(2,1)S(1)}, bf16[1056,128]{1,0:T(8,128)(2,1)S(1)}, u32[]{:S(2)}, u32[]{:S(2)}) collective-permute-start(bf16[1056,128]{1,0:T(8,128)(2,1)S(1)} %get-tuple-element.27), channel_id=1, source_target_pairs={{8,20},{12,16},{9,21},{13,17},{10,22},{14,18},{11,23},{15,19}} | collective-permute-start | bytes 811016 | tf_op jit(solution)/shard_map/ppermute | solution.py:578
  58.1 26.4 %copy-start = (bf16[1024,1024]{1,0:T(8,128)(2,1)S(1)}, bf16[1024,1024]{1,0:T(8,128)(2,1)}, u32[]{:S(2)}) copy-start(bf16[1024,1024]{1,0:T(8,128)(2,1)} %weight_ref.5) | copy-start | bytes 6291460
  58.1 10.7 %collective-permute-start.13 = (bf16[1056,128]{1,0:T(8,128)(2,1)S(1)}, bf16[1056,128]{1,0:T(8,128)(2,1)S(1)}, u32[]{:S(2)}, u32[]{:S(2)}) collective-permute-start(bf16[1056,128]{1,0:T(8,128)(2,1)S(1)} %get-tuple-element.28), channel_id=1, source_target_pairs={{8,28},{12,24},{9,29},{13,25},{10,30},{14,26},{11,31},{15,27}} | collective-permute-start | bytes 811016 | tf_op jit(solution)/shard_map/ppermute | solution.py:578
  65.7 3.1 %collective-permute-start.9 = (bf16[1056,128]{1,0:T(8,128)(2,1)S(1)}, bf16[1056,128]{1,0:T(8,128)(2,1)S(1)}, u32[]{:S(2)}, u32[]{:S(2)}) collective-permute-start(bf16[1056,128]{1,0:T(8,128)(2,1)S(1)} %get-tuple-element.26), channel_id=1, source_target_pairs={{16,28},{20,24},{17,29},{21,25},{18,30},{22,26},{19,31},{23,27}} | collective-permute-start | bytes 811016 | tf_op jit(solution)/shard_map/ppermute | solution.py:578
  66.4 5.4 %collective-permute-start.6 = (bf16[1056,128]{1,0:T(8,128)(2,1)S(1)}, bf16[1056,128]{1,0:T(8,128)(2,1)S(1)}, u32[]{:S(2)}, u32[]{:S(2)}) collective-permute-start(bf16[1056,128]{1,0:T(8,128)(2,1)S(1)} %get-tuple-element.25), channel_id=1, source_target_pairs={{0,4},{4,0},{8,12},{12,8},{16,20},{20,16},{24,28},{28,24},{1,5},{5... | collective-permute-start | bytes 811016 | tf_op jit(solution)/shard_map/ppermute | solution.py:578
  68.5 8.9 %collective-permute-start.21 = (bf16[1024,128]{1,0:T(8,128)(2,1)S(1)}, bf16[1024,128]{1,0:T(8,128)(2,1)S(1)}, u32[]{:S(2)}, u32[]{:S(2)}) collective-permute-start(bf16[1024,128]{1,0:T(8,128)(2,1)S(1)} %combine.3.refs_0_), channel_id=1, source_target_pairs={{0,2},{1,3},{2,0},{3,1},{4,6},{5,7},{6,4},{7,5},{8,10},{9,11},{10,... | collective-permute-start | bytes 786440 | tf_op jit(solution)/shard_map/ppermute | solution.py:581
  72.5 9.1 %collective-permute-start.14 = (bf16[1024,128]{1,0:T(8,128)(2,1)S(1)}, bf16[1024,128]{1,0:T(8,128)(2,1)S(1)}, u32[]{:S(2)}, u32[]{:S(2)}) collective-permute-start(bf16[1024,128]{1,0:T(8,128)(2,1)S(1)} %combine.2.refs_2_), channel_id=1, source_target_pairs={{0,2},{1,3},{2,0},{3,1},{4,6},{5,7},{6,4},{7,5},{8,10},{9,11},{10,... | collective-permute-start | bytes 786440 | tf_op jit(solution)/shard_map/ppermute | solution.py:581
  74.4 10.1 %collective-permute-start.24 = (bf16[1024,128]{1,0:T(8,128)(2,1)S(1)}, bf16[1024,128]{1,0:T(8,128)(2,1)S(1)}, u32[]{:S(2)}, u32[]{:S(2)}) collective-permute-start(bf16[1024,128]{1,0:T(8,128)(2,1)S(1)} %combine.3.refs_0_), channel_id=1, source_target_pairs={{0,1},{1,0},{2,3},{3,2},{4,5},{5,4},{6,7},{7,6},{8,9},{9,8},{10,11... | collective-permute-start | bytes 786440 | tf_op jit(solution)/shard_map/ppermute | solution.py:581
  77.4 9.1 %collective-permute-start.23 = (bf16[1024,128]{1,0:T(8,128)(2,1)S(1)}, bf16[1024,128]{1,0:T(8,128)(2,1)S(1)}, u32[]{:S(2)}, u32[]{:S(2)}) collective-permute-start(bf16[1024,128]{1,0:T(8,128)(2,1)S(1)} %combine.2.refs_2_), channel_id=1, source_target_pairs={{0,1},{1,0},{2,3},{3,2},{4,5},{5,4},{6,7},{7,6},{8,9},{9,8},{10,11... | collective-permute-start | bytes 786440 | tf_op jit(solution)/shard_map/ppermute | solution.py:581
  77.4 9.1 %collective-permute-start.22 = (bf16[1024,128]{1,0:T(8,128)(2,1)S(1)}, bf16[1024,128]{1,0:T(8,128)(2,1)S(1)}, u32[]{:S(2)}, u32[]{:S(2)}) collective-permute-start(bf16[1024,128]{1,0:T(8,128)(2,1)S(1)} %collective-permute-done.21.refs_0_), channel_id=1, source_target_pairs={{0,1},{1,0},{2,3},{3,2},{4,5},{5,4},{6,7},{7,6},{8,9},{9,8},{10,11... | collective-permute-start | bytes 786440 | tf_op jit(solution)/shard_map/ppermute | solution.py:581
  81.6 7.6 %collective-permute-start.15 = (bf16[1024,128]{1,0:T(8,128)(2,1)S(1)}, bf16[1024,128]{1,0:T(8,128)(2,1)S(1)}, u32[]{:S(2)}, u32[]{:S(2)}) collective-permute-start(bf16[1024,128]{1,0:T(8,128)(2,1)S(1)} %collective-permute-done.14.refs_0_), channel_id=1, source_target_pairs={{0,1},{1,0},{2,3},{3,2},{4,5},{5,4},{6,7},{7,6},{8,9},{9,8},{10,11... | collective-permute-start | bytes 786440 | tf_op jit(solution)/shard_map/ppermute | solution.py:581

commit v7 on v6

--- a/solution.py
+++ b/solution.py
@@ -446,25 +446,46 @@
             body()
 
 
+def low_near_kernel(per_shard, cluster_count, sizes, tab, *refs):
+    low, near, shared = refs[:6], refs[6:12], refs[12:]
+    attend_kernel("far_low", per_shard, cluster_count, sizes[0], tab, *low, *shared)
+    attend_kernel("near", per_shard, cluster_count, sizes[1], tab, *near, *shared)
+
+
+def both_kernel(per_shard, cluster_count, sizes, tab, *refs):
+    passed, refs = refs[9], refs[:9] + refs[10:]
+    attend_kernel("far_both", per_shard, cluster_count, sizes, tab, *refs)
+
+    @pl.when(tab[WHERE, 1] == 2)
+    def _():
+        refs[9][...] = passed[...]
+
+
 def log_of(ref, rows):
     tail = ref[rows:, :].astype(jnp.float32)
     step = tail.shape[0] // 4
     return tail[:step] + tail[step : 2 * step] + tail[2 * step : 3 * step]
 
 
-def attend(kind, cluster_count, tables, queries, key_values, earlier=()):
-    rows, width = queries[0].shape
+def attend(kind, cluster_count, tables, operands):
+    rows, width = operands[0].shape
     per_shard = rows // width
-    shards, quarters = KINDS[kind][2:]
-    sizes = tuple(q * per_shard // 4 for q in quarters)
-    held = shards * per_shard + sizes[-1]
+    kinds = ("far_low", "near") if kind == "low_near" else (kind,)
+    sizes = tuple(tuple(q * per_shard // 4 for q in KINDS[k][3]) for k in kinds)
+    held = max(KINDS[k][2] * per_shard + size[-1] for k, size in zip(kinds, sizes))
+    if kind == "low_near":
+        kernel = functools.partial(low_near_kernel, per_shard, cluster_count, sizes)
+    elif kind == "far_both":
+        kernel = functools.partial(both_kernel, per_shard, cluster_count, sizes[0])
+    else:
+        kernel = functools.partial(attend_kernel, kind, per_shard, cluster_count, sizes[0])
     smem = pl.BlockSpec(memory_space=pltpu.SMEM)
     vmem = pl.BlockSpec(memory_space=pltpu.VMEM)
     out = jax.ShapeDtypeStruct((per_shard * (width + 4), width), jnp.bfloat16)
     tile = (width, width)
     return pl.pallas_call(
-        functools.partial(attend_kernel, kind, per_shard, cluster_count, sizes),
-        in_specs=[smem] + [vmem] * (len(queries) + len(key_values) + len(earlier)),
+        kernel,
+        in_specs=[smem] + [vmem] * len(operands),
         out_specs=[vmem] * 2,
         out_shape=[out] * 2,
         scratch_shapes=[
@@ -476,29 +497,27 @@
             pltpu.VMEM((per_shard, width), jnp.float32),
         ],
         compiler_params=pltpu.CompilerParams(vmem_limit_bytes=VMEM_BYTES),
-    )(tables, *queries, *key_values, *earlier)
-
-
-def combine_kernel(ids_ref, own, near, second, third, out_ref):
+    )(tables, *operands)
+
+
+def combine_kernel(ids_ref, own, up, third, out_ref):
     plane = ids_ref[0, 1]
     rows, width = out_ref.shape
     own_log = log_of(own, rows)
-    near_log = jnp.where(plane == 3, log_of(near, rows), NEG)
-    far_log = jnp.where(plane == 3, log_of(third, rows), log_of(second, rows))
-    far_log = jnp.where(plane > 1, far_log, NEG)
-    top = jnp.maximum(jnp.maximum(own_log, near_log), far_log)
+    up_log = jnp.where(plane > 1, log_of(up, rows), NEG)
+    far_log = jnp.where(plane == 3, log_of(third, rows), NEG)
+    top = jnp.maximum(jnp.maximum(own_log, up_log), far_log)
     own_part = jnp.exp(own_log - top)
-    near_part = jnp.exp(near_log - top)
+    up_part = jnp.exp(up_log - top)
     far_part = jnp.exp(far_log - top)
-    share = 1.0 / (own_part + near_part + far_part)
-    own_part, near_part, far_part = own_part * share, near_part * share, far_part * share
+    share = 1.0 / (own_part + up_part + far_part)
+    own_part, up_part, far_part = own_part * share, up_part * share, far_part * share
     for b in range(rows // width):
         lines = slice(b * width, (b + 1) * width)
-        far = jnp.where(plane == 3, third[lines, :], second[lines, :])
         mixed = (
             own[lines, :].astype(jnp.float32) * own_part[b : b + 1]
-            + near[lines, :].astype(jnp.float32) * near_part[b : b + 1]
-            + far.astype(jnp.float32) * far_part[b : b + 1]
+            + up[lines, :].astype(jnp.float32) * up_part[b : b + 1]
+            + third[lines, :].astype(jnp.float32) * far_part[b : b + 1]
         )
         out_ref[lines, :] = mixed.T.astype(jnp.bfloat16)
 
@@ -547,7 +566,7 @@
     vmem = pl.BlockSpec(memory_space=pltpu.VMEM)
     given = [] if given is None else [given]
     width = weight.shape[1]
-    step = width // 4
+    step = width // 2 if final else width
     return pl.pallas_call(
         functools.partial(project_kernel, which),
         grid=(width // step,),
@@ -600,32 +619,30 @@
     cluster_count = clusters.shape[1] // per_shard
     tables = block_tables(ids, clusters, per_shard)
 
-    def meet(kind, queries, key_values, earlier=()):
-        return attend(kind, cluster_count, tables, queries, key_values, earlier)
+    def meet(kind, *operands):
+        return attend(kind, cluster_count, tables, operands)
 
     plane_kv = (kv_keep, first, second, third)
-    started = meet("far_high", (far2_keep, far3_keep), plane_kv + (low_keep,))
-    back2_keep, back3_keep = meet(
-        "far_low", (far2_keep, far3_keep), (low_first, low_second), started
+    both_kv = plane_kv + (low_keep, low_first, low_second)
+    started = meet("far_high", far2_keep, far3_keep, *plane_kv, low_keep)
+    one, two = meet(
+        "low_near", far2_keep, far3_keep, low_first, low_second, *started,
+        near_keep, near_swap, *plane_kv,
     )
-    back3_keep = send(back3_keep, hop((1, 3)))
-    back2_keep = send(back2_keep, hop((1, 2)))
-    both_kv = plane_kv + (low_keep, low_first, low_second)
-    down_keep, down_swap = meet("near", (near_keep, near_swap), plane_kv)
-    down_keep = send(down_keep, hop((2, 3)))
-    back2_swap, back3_swap = meet("far_both", (far2_swap, far3_swap), both_kv)
-    back3_other = send(back3_swap, hop((1, 3), cross=1))
-    back2_other = send(back2_swap, hop((1, 2), cross=1))
-    down_other = send(down_swap, hop((2, 3), cross=1))
-    own_keep, own_swap = meet("own", (q_keep,), both_kv)
+    far_kept = send(two, hop((1, 3)))
+    one_up = send(one, hop((1, 2), (2, 3)))
+    back2_swap, back3_swap = meet("far_both", far2_swap, far3_swap, *both_kv, two)
+    far_other = send(back3_swap, hop((1, 3), cross=1))
+    one_up_other = send(back2_swap, hop((1, 2), (2, 3), cross=1))
+    own_keep, own_swap = meet("own", q_keep, *both_kv)
     own_other = send(own_swap, swap)
     half = head_count // 2
     out = None
     pieces = []
     for part, values in enumerate(
         (
-            (own_keep, down_keep, back2_keep, back3_keep),
-            (own_other, down_other, back2_other, back3_other),
+            (own_keep, one_up, far_kept),
+            (own_other, one_up_other, far_other),
         )
     ):
         local = combine(ids, values)

time: 92.7 us -> 79.9 us (0.86)
  waiting for transfers between devices: 23.7 us -> 16.7 us
  Pallas kernels: 33.3 us -> 30.2 us
  starting transfers between devices: 33.4 us -> 30.7 us
    ppermute x19 -> x17, waiting for transfers between devices: 23.6 us -> 16 us  [send(): return lax.ppermute(value, 'seq', pairs)]
    pallas_call x3, Pallas kernels: 7.89 us -> 5.55 us  [project(): pl.pallas_call(functools.partial(project_kernel, which), grid=(width // s...]
    ppermute x19 -> x17, starting transfers between devices: 21.2 us -> 19.8 us  [send(): return lax.ppermute(value, 'seq', pairs)]
    ppermute x6, starting transfers between devices: 12.2 us -> 10.9 us  [across(): lax.ppermute(value, 'head', [(g, g ^ flip) for g in range(head_count)])]
    pallas_call x5 -> x4, Pallas kernels: 21.7 us -> 21 us  [attend(): pl.pallas_call(kernel, in_specs=[smem] + [vmem] * len(operands), out_spec...]
  transfers between devices with their start and end apart: 25 -> 23, of which waited for: 6 -> 7; matrix products, arithmetic and copies ran while one was open for 0% -> 0% of each run, Pallas kernels for 31% -> 33%
where the time goes in v7:
time: 79.9 us; the launch traced here: 79.6 us
  starting transfers between devices  30.7 us (38%)
  Pallas kernels  30.2 us (38%)
  waiting for transfers between devices  16.7 us (21%)
  local copies, waits for them, and re-layouts  1.63 us (2%)
    pallas_call x4, Pallas kernels, attend(): pl.pallas_call(kernel, in_specs=[smem] + [vmem] * len(operands), out_spec...  21 us
    ppermute x17, starting transfers between devices, send(): return lax.ppermute(value, 'seq', pairs)  19.8 us
    ppermute x17, waiting for transfers between devices, send(): return lax.ppermute(value, 'seq', pairs)  16 us
    ppermute x6, starting transfers between devices, across(): lax.ppermute(value, 'head', [(g, g ^ flip) for g in range(head_count)])  10.9 us
    pallas_call x3, Pallas kernels, project(): pl.pallas_call(functools.partial(project_kernel, which), grid=(width // s...  5.55 us
    unnamed x5, local copies, waits for them, and re-layouts  1.63 us
  transfers between devices with their start and end apart: 23, of which 7 were waited for; matrix products, arithmetic and copies ran while one was open for 0% of the time, Pallas kernels for 33%

profile of v7, /device:TPU:13, one launch (start us, length us, event | category | flops | bytes accessed | tf_op | source)
XLA Modules:
  0.0 79.6 jit_solution(4367065607389222902)
XLA Ops:
  0.0 1.6 %copy.6 = bf16[1024,2,384]{2,0,1:T(8,128)(2,1)S(1)} copy(bf16[1024,2,384]{2,1,0:T(2,128)(2,1)} %param.3) | data formatting | bytes 3145728 | tf_op args[0]
  1.7 1.4 %split_heads.1 = (bf16[1024,128]{1,0:T(8,128)(2,1)S(1)}, bf16[2,1024,128]{2,1,0:T(8,128)(2,1)S(1)}, bf16[1024,128]{1,0:T(8,128)(2,1)S(1)}, bf16[1024,128]{1,0:T(8,128)(2,1)S(1)}, bf16[1024,128]{1,0:T(8,128)(2,1)S(1)}) custom-call(s32[1,3]{1,0:T(1,128)S(1)} %add_bitcast_fusion.ids_ref, bf16[2,1024,384]{2,1,0:T(8,128)(2,1)S(1)} %bitcast.8), custom_call_target="tpu_custom_call" | custom-call | tf_op jit(solution)/shard_map/split_heads/pallas_call | solution.py:180
  3.1 1.3 %collective-permute-start = (bf16[1024,128]{1,0:T(8,128)(2,1)S(1)}, bf16[1024,128]{1,0:T(8,128)(2,1)S(1)}, u32[]{:S(2)}, u32[]{:S(2)}) collective-permute-start(bf16[1024,128]{1,0:T(8,128)(2,1)S(1)} %get-tuple-element.20), channel_id=1, source_target_pairs={{0,4},{4,0},{8,12},{12,8},{16,20},{20,16},{24,28},{28,24},{1,5},{5... | collective-permute-start | bytes 786440 | tf_op jit(solution)/shard_map/ppermute | solution.py:597
  4.6 1.3 %collective-permute-start.3 = (bf16[2,1024,128]{2,1,0:T(8,128)(2,1)S(1)}, bf16[2,1024,128]{2,1,0:T(8,128)(2,1)S(1)}, u32[]{:S(2)}, u32[]{:S(2)}) collective-permute-start(bf16[2,1024,128]{2,1,0:T(8,128)(2,1)S(1)} %get-tuple-element.19.refs_1_.refs_2_.refs_8_), channel_id=1, source_target_pairs={{0,8},{4,12},{1,9},{5,13},{2,10},{6,14},{3,11},{7,15}} | collective-permute-start | bytes 1572872 | tf_op jit(solution)/shard_map/ppermute | solution.py:597
  5.9 1.3 %collective-permute-start.10 = (bf16[1024,128]{1,0:T(8,128)(2,1)S(1)}, bf16[1024,128]{1,0:T(8,128)(2,1)S(1)}, u32[]{:S(2)}, u32[]{:S(2)}) collective-permute-start(bf16[1024,128]{1,0:T(8,128)(2,1)S(1)} %get-tuple-element.18.refs_0_), channel_id=1, source_target_pairs={{24,8},{28,12},{25,9},{29,13},{26,10},{30,14},{27,11},{31,15}} | collective-permute-start | bytes 786440 | tf_op jit(solution)/shard_map/ppermute | solution.py:597
  7.2 1.3 %collective-permute-start.2 = (bf16[1024,128]{1,0:T(8,128)(2,1)S(1)}, bf16[1024,128]{1,0:T(8,128)(2,1)S(1)}, u32[]{:S(2)}, u32[]{:S(2)}) collective-permute-start(bf16[1024,128]{1,0:T(8,128)(2,1)S(1)} %get-tuple-element.22), channel_id=1, source_target_pairs={{0,4},{4,0},{8,12},{12,8},{16,20},{20,16},{24,28},{28,24},{1,5},{5... | collective-permute-start | bytes 786440 | tf_op jit(solution)/shard_map/ppermute | solution.py:597
  8.5 1.9 %collective-permute-done.refs_2_.refs_3_.refs_9_ = bf16[1024,128]{1,0:T(8,128)(2,1)S(1)} collective-permute-done((bf16[1024,128]{1,0:T(8,128)(2,1)S(1)}, bf16[1024,128]{1,0:T(8,128)(2,1)S(1)}, u32[]{:S(2)}, u32[]{:S(2)}) %collective-permute-start) | collective-permute-done | bytes 262176 | tf_op jit(solution)/shard_map/ppermute | solution.py:597
  10.4 1.3 %collective-permute-start.9 = (bf16[1024,128]{1,0:T(8,128)(2,1)S(1)}, bf16[1024,128]{1,0:T(8,128)(2,1)S(1)}, u32[]{:S(2)}, u32[]{:S(2)}) collective-permute-start(bf16[1024,128]{1,0:T(8,128)(2,1)S(1)} %get-tuple-element.18.refs_0_), channel_id=1, source_target_pairs={{16,8},{20,12},{17,9},{21,13},{18,10},{22,14},{19,11},{23,15}} | collective-permute-start | bytes 786440 | tf_op jit(solution)/shard_map/ppermute | solution.py:597
  11.7 4.3 %collective-permute-done.1.refs_3_.refs_4_.refs_10_ = bf16[1024,128]{1,0:T(8,128)(2,1)S(1)} collective-permute-done((bf16[1024,128]{1,0:T(8,128)(2,1)S(1)}, bf16[1024,128]{1,0:T(8,128)(2,1)S(1)}, u32[]{:S(2)}, u32[]{:S(2)}) %collective-permute-start.1) | collective-permute-done | bytes 262176 | tf_op jit(solution)/shard_map/ppermute | solution.py:597
  17.4 4.2 %collective-permute-done.2.refs_4_.refs_5_.refs_11_ = bf16[1024,128]{1,0:T(8,128)(2,1)S(1)} collective-permute-done((bf16[1024,128]{1,0:T(8,128)(2,1)S(1)}, bf16[1024,128]{1,0:T(8,128)(2,1)S(1)}, u32[]{:S(2)}, u32[]{:S(2)}) %collective-permute-start.2) | collective-permute-done | bytes 262176 | tf_op jit(solution)/shard_map/ppermute | solution.py:597
  21.6 1.3 %collective-permute-start.4 = (bf16[1024,128]{1,0:T(8,128)(2,1)S(1)}, bf16[1024,128]{1,0:T(8,128)(2,1)S(1)}, u32[]{:S(2)}, u32[]{:S(2)}) collective-permute-start(bf16[1024,128]{1,0:T(8,128)(2,1)S(1)} %collective-permute-done.refs_2_.refs_3_.refs_9_), channel_id=1, source_target_pairs={{0,8},{4,12},{1,9},{5,13},{2,10},{6,14},{3,11},{7,15}} | collective-permute-start | bytes 786440 | tf_op jit(solution)/shard_map/ppermute | solution.py:597
  22.9 1.3 %collective-permute-start.5 = (bf16[1024,128]{1,0:T(8,128)(2,1)S(1)}, bf16[1024,128]{1,0:T(8,128)(2,1)S(1)}, u32[]{:S(2)}, u32[]{:S(2)}) collective-permute-start(bf16[1024,128]{1,0:T(8,128)(2,1)S(1)} %collective-permute-done.1.refs_3_.refs_4_.refs_10_), channel_id=1, source_target_pairs={{0,8},{4,12},{1,9},{5,13},{2,10},{6,14},{3,11},{7,15}} | collective-permute-start | bytes 786440 | tf_op jit(solution)/shard_map/ppermute | solution.py:597
  24.2 1.3 %collective-permute-start.7 = (bf16[1024,128]{1,0:T(8,128)(2,1)S(1)}, bf16[1024,128]{1,0:T(8,128)(2,1)S(1)}, u32[]{:S(2)}, u32[]{:S(2)}) collective-permute-start(bf16[1024,128]{1,0:T(8,128)(2,1)S(1)} %collective-permute-done.refs_2_.refs_3_.refs_9_), channel_id=1, source_target_pairs={{16,8},{20,12},{17,9},{21,13},{18,10},{22,14},{19,11},{23,15}} | collective-permute-start | bytes 786440 | tf_op jit(solution)/shard_map/ppermute | solution.py:597
  25.5 1.3 %collective-permute-start.8 = (bf16[1024,128]{1,0:T(8,128)(2,1)S(1)}, bf16[1024,128]{1,0:T(8,128)(2,1)S(1)}, u32[]{:S(2)}, u32[]{:S(2)}) collective-permute-start(bf16[1024,128]{1,0:T(8,128)(2,1)S(1)} %collective-permute-done.refs_2_.refs_3_.refs_9_), channel_id=1, source_target_pairs={{24,8},{28,12},{25,9},{29,13},{26,10},{30,14},{27,11},{31,15}} | collective-permute-start | bytes 786440 | tf_op jit(solution)/shard_map/ppermute | solution.py:597
  27.6 5.3 %shard_map.38 = (bf16[1056,128]{1,0:T(8,128)(2,1)S(1)}, bf16[1056,128]{1,0:T(8,128)(2,1)S(1)}) custom-call(s32[24,128]{1,0:T(8,128)S(1)} %block_tables.1.tab, bf16[1024,128]{1,0:T(8,128)(2,1)S(1)} %collective-permute-done.9.refs_0_, bf16[1024,128]{1,0:T(8,128)(2,1)S(1)} %collective-permute-done.10.refs_1_, ...), custom_call_target="tpu_custom_call" | custom-call | tf_op jit(solution)/shard_map/pallas_call | solution.py:486
  32.9 2.6 %collective-permute-done.5.refs_7_.refs_3_.refs_8_ = bf16[1024,128]{1,0:T(8,128)(2,1)S(1)} collective-permute-done((bf16[1024,128]{1,0:T(8,128)(2,1)S(1)}, bf16[1024,128]{1,0:T(8,128)(2,1)S(1)}, u32[]{:S(2)}, u32[]{:S(2)}) %collective-permute-start.5) | collective-permute-done | bytes 262176 | tf_op jit(solution)/shard_map/ppermute | solution.py:597
  35.4 3.6 %shard_map.39 = (bf16[1056,128]{1,0:T(8,128)(2,1)S(1)}, bf16[1056,128]{1,0:T(8,128)(2,1)S(1)}) custom-call(s32[24,128]{1,0:T(8,128)S(1)} %block_tables.1.tab, bf16[1024,128]{1,0:T(8,128)(2,1)S(1)} %collective-permute-done.9.refs_0_, bf16[1024,128]{1,0:T(8,128)(2,1)S(1)} %collective-permute-done.10.refs_1_, ...), custom_call_target="tpu_custom_call" | custom-call | tf_op jit(solution)/shard_map/pallas_call | solution.py:486
  39.1 1.3 %collective-permute-start.17 = (bf16[1056,128]{1,0:T(8,128)(2,1)S(1)}, bf16[1056,128]{1,0:T(8,128)(2,1)S(1)}, u32[]{:S(2)}, u32[]{:S(2)}) collective-permute-start(bf16[1056,128]{1,0:T(8,128)(2,1)S(1)} %get-tuple-element.30), channel_id=1, source_target_pairs={{8,16},{12,20},{16,24},{20,28},{9,17},{13,21},{17,25},{21,29},{10,... | collective-permute-start | bytes 811016 | tf_op jit(solution)/shard_map/ppermute | solution.py:597
  40.4 1.3 %collective-permute-start.18 = (bf16[1056,128]{1,0:T(8,128)(2,1)S(1)}, bf16[1056,128]{1,0:T(8,128)(2,1)S(1)}, u32[]{:S(2)}, u32[]{:S(2)}) collective-permute-start(bf16[1056,128]{1,0:T(8,128)(2,1)S(1)} %get-tuple-element.26.refs_9_), channel_id=1, source_target_pairs={{8,24},{12,28},{9,25},{13,29},{10,26},{14,30},{11,27},{15,31}} | collective-permute-start | bytes 811016 | tf_op jit(solution)/shard_map/ppermute | solution.py:597
  41.7 6.0 %shard_map.40 = (bf16[1056,128]{1,0:T(8,128)(2,1)S(1)}, bf16[1056,128]{1,0:T(8,128)(2,1)S(1)}) custom-call(s32[24,128]{1,0:T(8,128)S(1)} %block_tables.1.tab, bf16[1024,128]{1,0:T(8,128)(2,1)S(1)} %collective-permute-done.7.refs_0_, bf16[1024,128]{1,0:T(8,128)(2,1)S(1)} %collective-permute-done.8.refs_1_, ...), custom_call_target="tpu_custom_call" | custom-call | tf_op jit(solution)/shard_map/pallas_call | solution.py:486
  47.7 1.3 %collective-permute-start.13 = (bf16[1056,128]{1,0:T(8,128)(2,1)S(1)}, bf16[1056,128]{1,0:T(8,128)(2,1)S(1)}, u32[]{:S(2)}, u32[]{:S(2)}) collective-permute-start(bf16[1056,128]{1,0:T(8,128)(2,1)S(1)} %get-tuple-element.27), channel_id=1, source_target_pairs={{8,20},{12,16},{16,28},{20,24},{9,21},{13,17},{17,29},{21,25},{10,... | collective-permute-start | bytes 811016 | tf_op jit(solution)/shard_map/ppermute | solution.py:597
  49.0 1.4 %collective-permute-start.14 = (bf16[1056,128]{1,0:T(8,128)(2,1)S(1)}, bf16[1056,128]{1,0:T(8,128)(2,1)S(1)}, u32[]{:S(2)}, u32[]{:S(2)}) collective-permute-start(bf16[1056,128]{1,0:T(8,128)(2,1)S(1)} %get-tuple-element.28), channel_id=1, source_target_pairs={{8,28},{12,24},{9,29},{13,25},{10,30},{14,26},{11,31},{15,27}} | collective-permute-start | bytes 811016 | tf_op jit(solution)/shard_map/ppermute | solution.py:597
  50.5 6.1 %shard_map.37 = (bf16[1056,128]{1,0:T(8,128)(2,1)S(1)}, bf16[1056,128]{1,0:T(8,128)(2,1)S(1)}) custom-call(s32[24,128]{1,0:T(8,128)S(1)} %block_tables.1.tab, bf16[1024,128]{1,0:T(8,128)(2,1)S(1)} %get-tuple-element.18.refs_0_, bf16[2,1024,128]{2,1,0:T(8,128)(2,1)S(1)} %get-tuple-element.19.refs_1_.refs_2_.refs_8_, ...), custom_call_target="tpu_custom_call" | custom-call | tf_op jit(solution)/shard_map/pallas_call | solution.py:486
  56.6 1.3 %collective-permute-start.6 = (bf16[1056,128]{1,0:T(8,128)(2,1)S(1)}, bf16[1056,128]{1,0:T(8,128)(2,1)S(1)}, u32[]{:S(2)}, u32[]{:S(2)}) collective-permute-start(bf16[1056,128]{1,0:T(8,128)(2,1)S(1)} %get-tuple-element.23), channel_id=1, source_target_pairs={{0,4},{4,0},{8,12},{12,8},{16,20},{20,16},{24,28},{28,24},{1,5},{5... | collective-permute-start | bytes 811016 | tf_op jit(solution)/shard_map/ppermute | solution.py:597
  59.0 2.9 %collective-permute-done.14.third = bf16[1056,128]{1,0:T(8,128)(2,1)S(1)} collective-permute-done((bf16[1056,128]{1,0:T(8,128)(2,1)S(1)}, bf16[1056,128]{1,0:T(8,128)(2,1)S(1)}, u32[]{:S(2)}, u32[]{:S(2)}) %collective-permute-start.14) | collective-permute-done | bytes 270368 | tf_op jit(solution)/shard_map/ppermute | solution.py:597
  62.8 1.8 %collective-permute-start.15 = (bf16[1024,128]{1,0:T(8,128)(2,1)S(1)}, bf16[1024,128]{1,0:T(8,128)(2,1)S(1)}, u32[]{:S(2)}, u32[]{:S(2)}) collective-permute-start(bf16[1024,128]{1,0:T(8,128)(2,1)S(1)} %combine.2.refs_2_), channel_id=1, source_target_pairs={{0,2},{1,3},{2,0},{3,1},{4,6},{5,7},{6,4},{7,5},{8,10},{9,11},{10,... | collective-permute-start | bytes 786440 | tf_op jit(solution)/shard_map/ppermute | solution.py:600
  64.5 3.1 %collective-permute-start.22 = (bf16[1024,128]{1,0:T(8,128)(2,1)S(1)}, bf16[1024,128]{1,0:T(8,128)(2,1)S(1)}, u32[]{:S(2)}, u32[]{:S(2)}) collective-permute-start(bf16[1024,128]{1,0:T(8,128)(2,1)S(1)} %combine.3.refs_0_), channel_id=1, source_target_pairs={{0,1},{1,0},{2,3},{3,2},{4,5},{5,4},{6,7},{7,6},{8,9},{9,8},{10,11... | collective-permute-start | bytes 786440 | tf_op jit(solution)/shard_map/ppermute | solution.py:600
  67.6 3.0 %collective-permute-start.20 = (bf16[1024,128]{1,0:T(8,128)(2,1)S(1)}, bf16[1024,128]{1,0:T(8,128)(2,1)S(1)}, u32[]{:S(2)}, u32[]{:S(2)}) collective-permute-start(bf16[1024,128]{1,0:T(8,128)(2,1)S(1)} %collective-permute-done.19.refs_0_), channel_id=1, source_target_pairs={{0,1},{1,0},{2,3},{3,2},{4,5},{5,4},{6,7},{7,6},{8,9},{9,8},{10,11... | collective-permute-start | bytes 786440 | tf_op jit(solution)/shard_map/ppermute | solution.py:600
  71.4 2.6 %collective-permute-start.16 = (bf16[1024,128]{1,0:T(8,128)(2,1)S(1)}, bf16[1024,128]{1,0:T(8,128)(2,1)S(1)}, u32[]{:S(2)}, u32[]{:S(2)}) collective-permute-start(bf16[1024,128]{1,0:T(8,128)(2,1)S(1)} %collective-permute-done.15.refs_0_), channel_id=1, source_target_pairs={{0,1},{1,0},{2,3},{3,2},{4,5},{5,4},{6,7},{7,6},{8,9},{9,8},{10,11... | collective-permute-start | bytes 786440 | tf_op jit(solution)/shard_map/ppermute | solution.py:600
  74.0 1.3 %project.3.refs_4_ = f32[1024,1024]{1,0:T(8,128)S(1)} custom-call(s32[1,3]{1,0:T(1,128)S(1)} %add_bitcast_fusion.ids_ref, bf16[1024,1024]{1,0:T(8,128)(2,1)S(1)} %copy-done, bf16[1024,128]{1,0:T(8,128)(2,1)S(1)} %combine.3.refs_0_, bf16[1024,128]{1,0:T(8,128)(2,1)S(1)} %collective-permute-done.22.refs_1_), custom_call_target="tpu_custom_call" | custom-call | tf_op jit(solution)/shard_map/project/pallas_call | solution.py:570
  75.3 1.8 %project.4.refs_2_ = f32[1024,1024]{1,0:T(8,128)S(1)} custom-call(s32[1,3]{1,0:T(1,128)S(1)} %add_bitcast_fusion.ids_ref, bf16[1024,1024]{1,0:T(8,128)(2,1)S(1)} %copy-done, bf16[1024,128]{1,0:T(8,128)(2,1)S(1)} %collective-permute-done.19.refs_0_, bf16[1024,128]{1,0:T(8,128)(2,1)S(1)} %collective-permute-done.20.refs_1_, ...), custom_call_target="tpu_custom_call" | custom-call | tf_op jit(solution)/shard_map/project/pallas_call | solution.py:570
  77.2 2.4 %project.5 = bf16[1024,1024]{1,0:T(8,128)(2,1)} custom-call(s32[1,3]{1,0:T(1,128)S(1)} %add_bitcast_fusion.ids_ref, bf16[1024,1024]{1,0:T(8,128)(2,1)S(1)} %copy-done, bf16[1024,128]{1,0:T(8,128)(2,1)S(1)} %collective-permute-done.15.refs_0_, bf16[1024,128]{1,0:T(8,128)(2,1)S(1)} %collective-permute-done.16.refs_1_, f32[1024,1024]{1,0:T(8,128)S(1)} %project.4.refs_2_), custom_call_target="tpu_custom_call" | custom-call | tf_op jit(solution)/shard_map/project/pallas_call | solution.py:570
  (31 shorter events, 5.2 us)
Async XLA Ops:
  0.0 26.8 %copy-start.1 = (s32[2,64]{1,0:T(2,128)S(1)}, s32[2,64]{1,0:T(2,128)}, u32[]{:S(2)}) copy-start(s32[2,64]{1,0:T(2,128)} %table_ref.1) | copy-start | bytes 1540
  3.1 7.3 %collective-permute-start = (bf16[1024,128]{1,0:T(8,128)(2,1)S(1)}, bf16[1024,128]{1,0:T(8,128)(2,1)S(1)}, u32[]{:S(2)}, u32[]{:S(2)}) collective-permute-start(bf16[1024,128]{1,0:T(8,128)(2,1)S(1)} %get-tuple-element.20), channel_id=1, source_target_pairs={{0,4},{4,0},{8,12},{12,8},{16,20},{20,16},{24,28},{28,24},{1,5},{5... | collective-permute-start | bytes 786440 | tf_op jit(solution)/shard_map/ppermute | solution.py:597
  4.4 11.6 %collective-permute-start.1 = (bf16[1024,128]{1,0:T(8,128)(2,1)S(1)}, bf16[1024,128]{1,0:T(8,128)(2,1)S(1)}, u32[]{:S(2)}, u32[]{:S(2)}) collective-permute-start(bf16[1024,128]{1,0:T(8,128)(2,1)S(1)} %get-tuple-element.21), channel_id=1, source_target_pairs={{0,4},{4,0},{8,12},{12,8},{16,20},{20,16},{24,28},{28,24},{1,5},{5... | collective-permute-start | bytes 786440 | tf_op jit(solution)/shard_map/ppermute | solution.py:597
  4.6 20.9 %collective-permute-start.3 = (bf16[2,1024,128]{2,1,0:T(8,128)(2,1)S(1)}, bf16[2,1024,128]{2,1,0:T(8,128)(2,1)S(1)}, u32[]{:S(2)}, u32[]{:S(2)}) collective-permute-start(bf16[2,1024,128]{2,1,0:T(8,128)(2,1)S(1)} %get-tuple-element.19.refs_1_.refs_2_.refs_8_), channel_id=1, source_target_pairs={{0,8},{4,12},{1,9},{5,13},{2,10},{6,14},{3,11},{7,15}} | collective-permute-start | bytes 1572872 | tf_op jit(solution)/shard_map/ppermute | solution.py:597
  5.9 10.7 %collective-permute-start.10 = (bf16[1024,128]{1,0:T(8,128)(2,1)S(1)}, bf16[1024,128]{1,0:T(8,128)(2,1)S(1)}, u32[]{:S(2)}, u32[]{:S(2)}) collective-permute-start(bf16[1024,128]{1,0:T(8,128)(2,1)S(1)} %get-tuple-element.18.refs_0_), channel_id=1, source_target_pairs={{24,8},{28,12},{25,9},{29,13},{26,10},{30,14},{27,11},{31,15}} | collective-permute-start | bytes 786440 | tf_op jit(solution)/shard_map/ppermute | solution.py:597
  7.2 14.4 %collective-permute-start.2 = (bf16[1024,128]{1,0:T(8,128)(2,1)S(1)}, bf16[1024,128]{1,0:T(8,128)(2,1)S(1)}, u32[]{:S(2)}, u32[]{:S(2)}) collective-permute-start(bf16[1024,128]{1,0:T(8,128)(2,1)S(1)} %get-tuple-element.22), channel_id=1, source_target_pairs={{0,4},{4,0},{8,12},{12,8},{16,20},{20,16},{24,28},{28,24},{1,5},{5... | collective-permute-start | bytes 786440 | tf_op jit(solution)/shard_map/ppermute | solution.py:597
  10.4 12.5 %collective-permute-start.9 = (bf16[1024,128]{1,0:T(8,128)(2,1)S(1)}, bf16[1024,128]{1,0:T(8,128)(2,1)S(1)}, u32[]{:S(2)}, u32[]{:S(2)}) collective-permute-start(bf16[1024,128]{1,0:T(8,128)(2,1)S(1)} %get-tuple-element.18.refs_0_), channel_id=1, source_target_pairs={{16,8},{20,12},{17,9},{21,13},{18,10},{22,14},{19,11},{23,15}} | collective-permute-start | bytes 786440 | tf_op jit(solution)/shard_map/ppermute | solution.py:597
  16.0 8.2 %collective-permute-start.11 = (bf16[1024,128]{1,0:T(8,128)(2,1)S(1)}, bf16[1024,128]{1,0:T(8,128)(2,1)S(1)}, u32[]{:S(2)}, u32[]{:S(2)}) collective-permute-start(bf16[1024,128]{1,0:T(8,128)(2,1)S(1)} %get-tuple-element.18.refs_0_), channel_id=1, source_target_pairs={{24,16},{28,20},{25,17},{29,21},{26,18},{30,22},{27,19},{31,23}} | collective-permute-start | bytes 786440 | tf_op jit(solution)/shard_map/ppermute | solution.py:597
  16.7 16.2 %collective-permute-start.12 = (bf16[1024,128]{1,0:T(8,128)(2,1)S(1)}, bf16[1024,128]{1,0:T(8,128)(2,1)S(1)}, u32[]{:S(2)}, u32[]{:S(2)}) collective-permute-start(bf16[1024,128]{1,0:T(8,128)(2,1)S(1)} %collective-permute-done.refs_2_.refs_3_.refs_9_), channel_id=1, source_target_pairs={{24,16},{28,20},{25,17},{29,21},{26,18},{30,22},{27,19},{31,23}} | collective-permute-start | bytes 786440 | tf_op jit(solution)/shard_map/ppermute | solution.py:597
  21.6 11.3 %collective-permute-start.4 = (bf16[1024,128]{1,0:T(8,128)(2,1)S(1)}, bf16[1024,128]{1,0:T(8,128)(2,1)S(1)}, u32[]{:S(2)}, u32[]{:S(2)}) collective-permute-start(bf16[1024,128]{1,0:T(8,128)(2,1)S(1)} %collective-permute-done.refs_2_.refs_3_.refs_9_), channel_id=1, source_target_pairs={{0,8},{4,12},{1,9},{5,13},{2,10},{6,14},{3,11},{7,15}} | collective-permute-start | bytes 786440 | tf_op jit(solution)/shard_map/ppermute | solution.py:597
  22.9 12.5 %collective-permute-start.5 = (bf16[1024,128]{1,0:T(8,128)(2,1)S(1)}, bf16[1024,128]{1,0:T(8,128)(2,1)S(1)}, u32[]{:S(2)}, u32[]{:S(2)}) collective-permute-start(bf16[1024,128]{1,0:T(8,128)(2,1)S(1)} %collective-permute-done.1.refs_3_.refs_4_.refs_10_), channel_id=1, source_target_pairs={{0,8},{4,12},{1,9},{5,13},{2,10},{6,14},{3,11},{7,15}} | collective-permute-start | bytes 786440 | tf_op jit(solution)/shard_map/ppermute | solution.py:597
  24.2 17.5 %collective-permute-start.7 = (bf16[1024,128]{1,0:T(8,128)(2,1)S(1)}, bf16[1024,128]{1,0:T(8,128)(2,1)S(1)}, u32[]{:S(2)}, u32[]{:S(2)}) collective-permute-start(bf16[1024,128]{1,0:T(8,128)(2,1)S(1)} %collective-permute-done.refs_2_.refs_3_.refs_9_), channel_id=1, source_target_pairs={{16,8},{20,12},{17,9},{21,13},{18,10},{22,14},{19,11},{23,15}} | collective-permute-start | bytes 786440 | tf_op jit(solution)/shard_map/ppermute | solution.py:597
  25.5 16.2 %collective-permute-start.8 = (bf16[1024,128]{1,0:T(8,128)(2,1)S(1)}, bf16[1024,128]{1,0:T(8,128)(2,1)S(1)}, u32[]{:S(2)}, u32[]{:S(2)}) collective-permute-start(bf16[1024,128]{1,0:T(8,128)(2,1)S(1)} %collective-permute-done.refs_2_.refs_3_.refs_9_), channel_id=1, source_target_pairs={{24,8},{28,12},{25,9},{29,13},{26,10},{30,14},{27,11},{31,15}} | collective-permute-start | bytes 786440 | tf_op jit(solution)/shard_map/ppermute | solution.py:597
  39.1 18.8 %collective-permute-start.17 = (bf16[1056,128]{1,0:T(8,128)(2,1)S(1)}, bf16[1056,128]{1,0:T(8,128)(2,1)S(1)}, u32[]{:S(2)}, u32[]{:S(2)}) collective-permute-start(bf16[1056,128]{1,0:T(8,128)(2,1)S(1)} %get-tuple-element.30), channel_id=1, source_target_pairs={{8,16},{12,20},{16,24},{20,28},{9,17},{13,21},{17,25},{21,29},{10,... | collective-permute-start | bytes 811016 | tf_op jit(solution)/shard_map/ppermute | solution.py:597
  40.4 17.5 %collective-permute-start.18 = (bf16[1056,128]{1,0:T(8,128)(2,1)S(1)}, bf16[1056,128]{1,0:T(8,128)(2,1)S(1)}, u32[]{:S(2)}, u32[]{:S(2)}) collective-permute-start(bf16[1056,128]{1,0:T(8,128)(2,1)S(1)} %get-tuple-element.26.refs_9_), channel_id=1, source_target_pairs={{8,24},{12,28},{9,25},{13,29},{10,26},{14,30},{11,27},{15,31}} | collective-permute-start | bytes 811016 | tf_op jit(solution)/shard_map/ppermute | solution.py:597
  47.7 11.3 %collective-permute-start.13 = (bf16[1056,128]{1,0:T(8,128)(2,1)S(1)}, bf16[1056,128]{1,0:T(8,128)(2,1)S(1)}, u32[]{:S(2)}, u32[]{:S(2)}) collective-permute-start(bf16[1056,128]{1,0:T(8,128)(2,1)S(1)} %get-tuple-element.27), channel_id=1, source_target_pairs={{8,20},{12,16},{16,28},{20,24},{9,21},{13,17},{17,29},{21,25},{10,... | collective-permute-start | bytes 811016 | tf_op jit(solution)/shard_map/ppermute | solution.py:597
  49.0 25.0 %copy-start = (bf16[1024,1024]{1,0:T(8,128)(2,1)S(1)}, bf16[1024,1024]{1,0:T(8,128)(2,1)}, u32[]{:S(2)}) copy-start(bf16[1024,1024]{1,0:T(8,128)(2,1)} %weight_ref.5) | copy-start | bytes 6291460
  49.0 12.8 %collective-permute-start.14 = (bf16[1056,128]{1,0:T(8,128)(2,1)S(1)}, bf16[1056,128]{1,0:T(8,128)(2,1)S(1)}, u32[]{:S(2)}, u32[]{:S(2)}) collective-permute-start(bf16[1056,128]{1,0:T(8,128)(2,1)S(1)} %get-tuple-element.28), channel_id=1, source_target_pairs={{8,28},{12,24},{9,29},{13,25},{10,30},{14,26},{11,31},{15,27}} | collective-permute-start | bytes 811016 | tf_op jit(solution)/shard_map/ppermute | solution.py:597
  56.6 5.4 %collective-permute-start.6 = (bf16[1056,128]{1,0:T(8,128)(2,1)S(1)}, bf16[1056,128]{1,0:T(8,128)(2,1)S(1)}, u32[]{:S(2)}, u32[]{:S(2)}) collective-permute-start(bf16[1056,128]{1,0:T(8,128)(2,1)S(1)} %get-tuple-element.23), channel_id=1, source_target_pairs={{0,4},{4,0},{8,12},{12,8},{16,20},{20,16},{24,28},{28,24},{1,5},{5... | collective-permute-start | bytes 811016 | tf_op jit(solution)/shard_map/ppermute | solution.py:597
  58.7 9.0 %collective-permute-start.19 = (bf16[1024,128]{1,0:T(8,128)(2,1)S(1)}, bf16[1024,128]{1,0:T(8,128)(2,1)S(1)}, u32[]{:S(2)}, u32[]{:S(2)}) collective-permute-start(bf16[1024,128]{1,0:T(8,128)(2,1)S(1)} %combine.3.refs_0_), channel_id=1, source_target_pairs={{0,2},{1,3},{2,0},{3,1},{4,6},{5,7},{6,4},{7,5},{8,10},{9,11},{10,... | collective-permute-start | bytes 786440 | tf_op jit(solution)/shard_map/ppermute | solution.py:600
  62.8 8.6 %collective-permute-start.15 = (bf16[1024,128]{1,0:T(8,128)(2,1)S(1)}, bf16[1024,128]{1,0:T(8,128)(2,1)S(1)}, u32[]{:S(2)}, u32[]{:S(2)}) collective-permute-start(bf16[1024,128]{1,0:T(8,128)(2,1)S(1)} %combine.2.refs_2_), channel_id=1, source_target_pairs={{0,2},{1,3},{2,0},{3,1},{4,6},{5,7},{6,4},{7,5},{8,10},{9,11},{10,... | collective-permute-start | bytes 786440 | tf_op jit(solution)/shard_map/ppermute | solution.py:600
  64.5 9.5 %collective-permute-start.22 = (bf16[1024,128]{1,0:T(8,128)(2,1)S(1)}, bf16[1024,128]{1,0:T(8,128)(2,1)S(1)}, u32[]{:S(2)}, u32[]{:S(2)}) collective-permute-start(bf16[1024,128]{1,0:T(8,128)(2,1)S(1)} %combine.3.refs_0_), channel_id=1, source_target_pairs={{0,1},{1,0},{2,3},{3,2},{4,5},{5,4},{6,7},{7,6},{8,9},{9,8},{10,11... | collective-permute-start | bytes 786440 | tf_op jit(solution)/shard_map/ppermute | solution.py:600
  67.6 7.7 %collective-permute-start.21 = (bf16[1024,128]{1,0:T(8,128)(2,1)S(1)}, bf16[1024,128]{1,0:T(8,128)(2,1)S(1)}, u32[]{:S(2)}, u32[]{:S(2)}) collective-permute-start(bf16[1024,128]{1,0:T(8,128)(2,1)S(1)} %combine.2.refs_2_), channel_id=1, source_target_pairs={{0,1},{1,0},{2,3},{3,2},{4,5},{5,4},{6,7},{7,6},{8,9},{9,8},{10,11... | collective-permute-start | bytes 786440 | tf_op jit(solution)/shard_map/ppermute | solution.py:600
  67.6 7.7 %collective-permute-start.20 = (bf16[1024,128]{1,0:T(8,128)(2,1)S(1)}, bf16[1024,128]{1,0:T(8,128)(2,1)S(1)}, u32[]{:S(2)}, u32[]{:S(2)}) collective-permute-start(bf16[1024,128]{1,0:T(8,128)(2,1)S(1)} %collective-permute-done.19.refs_0_), channel_id=1, source_target_pairs={{0,1},{1,0},{2,3},{3,2},{4,5},{5,4},{6,7},{7,6},{8,9},{9,8},{10,11... | collective-permute-start | bytes 786440 | tf_op jit(solution)/shard_map/ppermute | solution.py:600
  71.4 5.8 %collective-permute-start.16 = (bf16[1024,128]{1,0:T(8,128)(2,1)S(1)}, bf16[1024,128]{1,0:T(8,128)(2,1)S(1)}, u32[]{:S(2)}, u32[]{:S(2)}) collective-permute-start(bf16[1024,128]{1,0:T(8,128)(2,1)S(1)} %collective-permute-done.15.refs_0_), channel_id=1, source_target_pairs={{0,1},{1,0},{2,3},{3,2},{4,5},{5,4},{6,7},{7,6},{8,9},{9,8},{10,11... | collective-permute-start | bytes 786440 | tf_op jit(solution)/shard_map/ppermute | solution.py:600

commit v8 on v7

--- a/solution.py
+++ b/solution.py
@@ -446,19 +446,10 @@
             body()
 
 
-def low_near_kernel(per_shard, cluster_count, sizes, tab, *refs):
-    low, near, shared = refs[:6], refs[6:12], refs[12:]
-    attend_kernel("far_low", per_shard, cluster_count, sizes[0], tab, *low, *shared)
-    attend_kernel("near", per_shard, cluster_count, sizes[1], tab, *near, *shared)
-
-
-def both_kernel(per_shard, cluster_count, sizes, tab, *refs):
-    passed, refs = refs[9], refs[:9] + refs[10:]
-    attend_kernel("far_both", per_shard, cluster_count, sizes, tab, *refs)
-
-    @pl.when(tab[WHERE, 1] == 2)
-    def _():
-        refs[9][...] = passed[...]
+def both_near_kernel(per_shard, cluster_count, sizes, tab, *refs):
+    both, near, outs, scratch = refs[:9], refs[9:15], refs[15:17], refs[17:]
+    attend_kernel("far_both", per_shard, cluster_count, sizes[0], tab, *both, *outs, *scratch)
+    attend_kernel("near", per_shard, cluster_count, sizes[1], tab, *near, *outs[::-1], *scratch)
 
 
 def log_of(ref, rows):
@@ -470,13 +461,11 @@
 def attend(kind, cluster_count, tables, operands):
     rows, width = operands[0].shape
     per_shard = rows // width
-    kinds = ("far_low", "near") if kind == "low_near" else (kind,)
+    kinds = ("far_both", "near") if kind == "both_near" else (kind,)
     sizes = tuple(tuple(q * per_shard // 4 for q in KINDS[k][3]) for k in kinds)
     held = max(KINDS[k][2] * per_shard + size[-1] for k, size in zip(kinds, sizes))
-    if kind == "low_near":
-        kernel = functools.partial(low_near_kernel, per_shard, cluster_count, sizes)
-    elif kind == "far_both":
-        kernel = functools.partial(both_kernel, per_shard, cluster_count, sizes[0])
+    if kind == "both_near":
+        kernel = functools.partial(both_near_kernel, per_shard, cluster_count, sizes)
     else:
         kernel = functools.partial(attend_kernel, kind, per_shard, cluster_count, sizes[0])
     smem = pl.BlockSpec(memory_space=pltpu.SMEM)
@@ -500,11 +489,12 @@
     )(tables, *operands)
 
 
-def combine_kernel(ids_ref, own, up, third, out_ref):
+def combine_kernel(ids_ref, own, up2, up3, third, out_ref):
     plane = ids_ref[0, 1]
     rows, width = out_ref.shape
     own_log = log_of(own, rows)
-    up_log = jnp.where(plane > 1, log_of(up, rows), NEG)
+    up_log = jnp.where(plane == 3, log_of(up3, rows), log_of(up2, rows))
+    up_log = jnp.where(plane > 1, up_log, NEG)
     far_log = jnp.where(plane == 3, log_of(third, rows), NEG)
     top = jnp.maximum(jnp.maximum(own_log, up_log), far_log)
     own_part = jnp.exp(own_log - top)
@@ -514,9 +504,10 @@
     own_part, up_part, far_part = own_part * share, up_part * share, far_part * share
     for b in range(rows // width):
         lines = slice(b * width, (b + 1) * width)
+        up = jnp.where(plane == 3, up3[lines, :], up2[lines, :])
         mixed = (
             own[lines, :].astype(jnp.float32) * own_part[b : b + 1]
-            + up[lines, :].astype(jnp.float32) * up_part[b : b + 1]
+            + up.astype(jnp.float32) * up_part[b : b + 1]
             + third[lines, :].astype(jnp.float32) * far_part[b : b + 1]
         )
         out_ref[lines, :] = mixed.T.astype(jnp.bfloat16)
@@ -625,15 +616,17 @@
     plane_kv = (kv_keep, first, second, third)
     both_kv = plane_kv + (low_keep, low_first, low_second)
     started = meet("far_high", far2_keep, far3_keep, *plane_kv, low_keep)
+    back2_keep, back3_keep = meet(
+        "far_low", far2_keep, far3_keep, low_first, low_second, *started
+    )
+    far_kept = send(back3_keep, hop((1, 3)))
+    up2_kept = send(back2_keep, hop((1, 2)))
     one, two = meet(
-        "low_near", far2_keep, far3_keep, low_first, low_second, *started,
-        near_keep, near_swap, *plane_kv,
+        "both_near", far2_swap, far3_swap, *both_kv, near_keep, near_swap, *plane_kv
     )
-    far_kept = send(two, hop((1, 3)))
-    one_up = send(one, hop((1, 2), (2, 3)))
-    back2_swap, back3_swap = meet("far_both", far2_swap, far3_swap, *both_kv, two)
-    far_other = send(back3_swap, hop((1, 3), cross=1))
-    one_up_other = send(back2_swap, hop((1, 2), (2, 3), cross=1))
+    far_other = send(two, hop((1, 3), cross=1))
+    up_other = send(one, hop((1, 2), (2, 3), cross=1))
+    up3_kept = send(two, hop((2, 3)))
     own_keep, own_swap = meet("own", q_keep, *both_kv)
     own_other = send(own_swap, swap)
     half = head_count // 2
@@ -641,8 +634,8 @@
     pieces = []
     for part, values in enumerate(
         (
-            (own_keep, one_up, far_kept),
-            (own_other, one_up_other, far_other),
+            (own_keep, up2_kept, up3_kept, far_kept),
+            (own_other, up_other, up_other, far_other),
         )
     ):
         local = combine(ids, values)

time: 79.9 us -> 89.7 us (1.12)
  starting transfers between devices: 30.7 us -> 36.3 us
  waiting for transfers between devices: 16.7 us -> 20.9 us
    ppermute x17 -> x18, waiting for transfers between devices: 16 us -> 20.8 us  [send(): return lax.ppermute(value, 'seq', pairs)]
    ppermute x17 -> x18, starting transfers between devices: 19.8 us -> 24.1 us  [send(): return lax.ppermute(value, 'seq', pairs)]
    ppermute x6, starting transfers between devices: 10.9 us -> 12.2 us  [across(): lax.ppermute(value, 'head', [(g, g ^ flip) for g in range(head_count)])]
  transfers between devices with their start and end apart: 23 -> 24, of which waited for: 7 -> 6; matrix products, arithmetic and copies ran while one was open for 0% -> 0% of each run, Pallas kernels for 33% -> 25%
where the time goes in v8:
time: 89.7 us; the launch traced here: 89.4 us
  starting transfers between devices  36.3 us (40%)
  Pallas kernels  30.2 us (34%)
  waiting for transfers between devices  20.9 us (23%)
  local copies, waits for them, and re-layouts  1.63 us (2%)
    ppermute x18, starting transfers between devices, send(): return lax.ppermute(value, 'seq', pairs)  24.1 us
    pallas_call x4, Pallas kernels, attend(): pl.pallas_call(kernel, in_specs=[smem] + [vmem] * len(operands), out_spec...  21 us
    ppermute x18, waiting for transfers between devices, send(): return lax.ppermute(value, 'seq', pairs)  20.8 us
    ppermute x6, starting transfers between devices, across(): lax.ppermute(value, 'head', [(g, g ^ flip) for g in range(head_count)])  12.2 us
    pallas_call x3, Pallas kernels, project(): pl.pallas_call(functools.partial(project_kernel, which), grid=(width // s...  5.55 us
  transfers between devices with their start and end apart: 24, of which 6 were waited for; matrix products, arithmetic and copies ran while one was open for 0% of the time, Pallas kernels for 25%

profile of v8, /device:TPU:13, one launch (start us, length us, event | category | flops | bytes accessed | tf_op | source)
XLA Modules:
  0.0 89.4 jit_solution(13595030670232969707)
XLA Ops:
  0.0 1.6 %copy.6 = bf16[1024,2,384]{2,0,1:T(8,128)(2,1)S(1)} copy(bf16[1024,2,384]{2,1,0:T(2,128)(2,1)} %param.3) | data formatting | bytes 3145728 | tf_op args[0]
  1.7 1.4 %split_heads.1 = (bf16[1024,128]{1,0:T(8,128)(2,1)S(1)}, bf16[2,1024,128]{2,1,0:T(8,128)(2,1)S(1)}, bf16[1024,128]{1,0:T(8,128)(2,1)S(1)}, bf16[1024,128]{1,0:T(8,128)(2,1)S(1)}, bf16[1024,128]{1,0:T(8,128)(2,1)S(1)}) custom-call(s32[1,3]{1,0:T(1,128)S(1)} %add_bitcast_fusion.ids_ref, bf16[2,1024,384]{2,1,0:T(8,128)(2,1)S(1)} %bitcast.8), custom_call_target="tpu_custom_call" | custom-call | tf_op jit(solution)/shard_map/split_heads/pallas_call | solution.py:180
  3.1 1.3 %collective-permute-start = (bf16[1024,128]{1,0:T(8,128)(2,1)S(1)}, bf16[1024,128]{1,0:T(8,128)(2,1)S(1)}, u32[]{:S(2)}, u32[]{:S(2)}) collective-permute-start(bf16[1024,128]{1,0:T(8,128)(2,1)S(1)} %get-tuple-element.20), channel_id=1, source_target_pairs={{0,4},{4,0},{8,12},{12,8},{16,20},{20,16},{24,28},{28,24},{1,5},{5... | collective-permute-start | bytes 786440 | tf_op jit(solution)/shard_map/ppermute | solution.py:588
  4.4 1.3 %collective-permute-start.3 = (bf16[2,1024,128]{2,1,0:T(8,128)(2,1)S(1)}, bf16[2,1024,128]{2,1,0:T(8,128)(2,1)S(1)}, u32[]{:S(2)}, u32[]{:S(2)}) collective-permute-start(bf16[2,1024,128]{2,1,0:T(8,128)(2,1)S(1)} %get-tuple-element.19.refs_1_.refs_2_.refs_11_), channel_id=1, source_target_pairs={{0,8},{4,12},{1,9},{5,13},{2,10},{6,14},{3,11},{7,15}} | collective-permute-start | bytes 1572872 | tf_op jit(solution)/shard_map/ppermute | solution.py:588
  6.0 1.3 %collective-permute-start.15 = (bf16[1024,128]{1,0:T(8,128)(2,1)S(1)}, bf16[1024,128]{1,0:T(8,128)(2,1)S(1)}, u32[]{:S(2)}, u32[]{:S(2)}) collective-permute-start(bf16[1024,128]{1,0:T(8,128)(2,1)S(1)} %get-tuple-element.18.refs_0_), channel_id=1, source_target_pairs={{16,8},{20,12},{17,9},{21,13},{18,10},{22,14},{19,11},{23,15}} | collective-permute-start | bytes 786440 | tf_op jit(solution)/shard_map/ppermute | solution.py:588
  7.3 1.3 %collective-permute-start.16 = (bf16[1024,128]{1,0:T(8,128)(2,1)S(1)}, bf16[1024,128]{1,0:T(8,128)(2,1)S(1)}, u32[]{:S(2)}, u32[]{:S(2)}) collective-permute-start(bf16[1024,128]{1,0:T(8,128)(2,1)S(1)} %get-tuple-element.18.refs_0_), channel_id=1, source_target_pairs={{24,8},{28,12},{25,9},{29,13},{26,10},{30,14},{27,11},{31,15}} | collective-permute-start | bytes 786440 | tf_op jit(solution)/shard_map/ppermute | solution.py:588
  8.6 1.8 %collective-permute-done.refs_2_.refs_3_.refs_12_ = bf16[1024,128]{1,0:T(8,128)(2,1)S(1)} collective-permute-done((bf16[1024,128]{1,0:T(8,128)(2,1)S(1)}, bf16[1024,128]{1,0:T(8,128)(2,1)S(1)}, u32[]{:S(2)}, u32[]{:S(2)}) %collective-permute-start) | collective-permute-done | bytes 262176 | tf_op jit(solution)/shard_map/ppermute | solution.py:588
  11.6 4.4 %collective-permute-done.1.refs_3_.refs_4_.refs_13_ = bf16[1024,128]{1,0:T(8,128)(2,1)S(1)} collective-permute-done((bf16[1024,128]{1,0:T(8,128)(2,1)S(1)}, bf16[1024,128]{1,0:T(8,128)(2,1)S(1)}, u32[]{:S(2)}, u32[]{:S(2)}) %collective-permute-start.1) | collective-permute-done | bytes 262176 | tf_op jit(solution)/shard_map/ppermute | solution.py:588
  16.0 1.3 %collective-permute-start.4 = (bf16[1024,128]{1,0:T(8,128)(2,1)S(1)}, bf16[1024,128]{1,0:T(8,128)(2,1)S(1)}, u32[]{:S(2)}, u32[]{:S(2)}) collective-permute-start(bf16[1024,128]{1,0:T(8,128)(2,1)S(1)} %collective-permute-done.refs_2_.refs_3_.refs_12_), channel_id=1, source_target_pairs={{0,8},{4,12},{1,9},{5,13},{2,10},{6,14},{3,11},{7,15}} | collective-permute-start | bytes 786440 | tf_op jit(solution)/shard_map/ppermute | solution.py:588
  17.3 2.8 %collective-permute-done.15.refs_0_ = bf16[1024,128]{1,0:T(8,128)(2,1)S(1)} collective-permute-done((bf16[1024,128]{1,0:T(8,128)(2,1)S(1)}, bf16[1024,128]{1,0:T(8,128)(2,1)S(1)}, u32[]{:S(2)}, u32[]{:S(2)}) %collective-permute-start.15) | collective-permute-done | bytes 262176 | tf_op jit(solution)/shard_map/ppermute | solution.py:588
  20.1 1.3 %collective-permute-start.5 = (bf16[1024,128]{1,0:T(8,128)(2,1)S(1)}, bf16[1024,128]{1,0:T(8,128)(2,1)S(1)}, u32[]{:S(2)}, u32[]{:S(2)}) collective-permute-start(bf16[1024,128]{1,0:T(8,128)(2,1)S(1)} %collective-permute-done.1.refs_3_.refs_4_.refs_13_), channel_id=1, source_target_pairs={{0,8},{4,12},{1,9},{5,13},{2,10},{6,14},{3,11},{7,15}} | collective-permute-start | bytes 786440 | tf_op jit(solution)/shard_map/ppermute | solution.py:588
  22.2 5.3 %shard_map.39 = (bf16[1056,128]{1,0:T(8,128)(2,1)S(1)}, bf16[1056,128]{1,0:T(8,128)(2,1)S(1)}) custom-call(s32[24,128]{1,0:T(8,128)S(1)} %block_tables.1.tab, bf16[1024,128]{1,0:T(8,128)(2,1)S(1)} %collective-permute-done.15.refs_0_, bf16[1024,128]{1,0:T(8,128)(2,1)S(1)} %collective-permute-done.16.refs_1_, ...), custom_call_target="tpu_custom_call" | custom-call | tf_op jit(solution)/shard_map/pallas_call | solution.py:475
  27.5 2.9 %collective-permute-done.5.refs_7_.refs_8_.refs_3_ = bf16[1024,128]{1,0:T(8,128)(2,1)S(1)} collective-permute-done((bf16[1024,128]{1,0:T(8,128)(2,1)S(1)}, bf16[1024,128]{1,0:T(8,128)(2,1)S(1)}, u32[]{:S(2)}, u32[]{:S(2)}) %collective-permute-start.5) | collective-permute-done | bytes 262176 | tf_op jit(solution)/shard_map/ppermute | solution.py:588
  30.3 3.6 %shard_map.40 = (bf16[1056,128]{1,0:T(8,128)(2,1)S(1)}, bf16[1056,128]{1,0:T(8,128)(2,1)S(1)}) custom-call(s32[24,128]{1,0:T(8,128)S(1)} %block_tables.1.tab, bf16[1024,128]{1,0:T(8,128)(2,1)S(1)} %collective-permute-done.15.refs_0_, bf16[1024,128]{1,0:T(8,128)(2,1)S(1)} %collective-permute-done.16.refs_1_, ...), custom_call_target="tpu_custom_call" | custom-call | tf_op jit(solution)/shard_map/pallas_call | solution.py:475
  34.0 1.3 %collective-permute-start.17 = (bf16[1056,128]{1,0:T(8,128)(2,1)S(1)}, bf16[1056,128]{1,0:T(8,128)(2,1)S(1)}, u32[]{:S(2)}, u32[]{:S(2)}) collective-permute-start(bf16[1056,128]{1,0:T(8,128)(2,1)S(1)} %get-tuple-element.29), channel_id=1, source_target_pairs={{8,16},{12,20},{9,17},{13,21},{10,18},{14,22},{11,19},{15,23}} | collective-permute-start | bytes 811016 | tf_op jit(solution)/shard_map/ppermute | solution.py:588
  36.7 1.3 %collective-permute-start.7 = (bf16[1024,128]{1,0:T(8,128)(2,1)S(1)}, bf16[1024,128]{1,0:T(8,128)(2,1)S(1)}, u32[]{:S(2)}, u32[]{:S(2)}) collective-permute-start(bf16[1024,128]{1,0:T(8,128)(2,1)S(1)} %collective-permute-done.refs_2_.refs_3_.refs_12_), channel_id=1, source_target_pairs={{16,8},{20,12},{17,9},{21,13},{18,10},{22,14},{19,11},{23,15}} | collective-permute-start | bytes 786440 | tf_op jit(solution)/shard_map/ppermute | solution.py:588
  38.0 1.3 %collective-permute-start.8 = (bf16[1024,128]{1,0:T(8,128)(2,1)S(1)}, bf16[1024,128]{1,0:T(8,128)(2,1)S(1)}, u32[]{:S(2)}, u32[]{:S(2)}) collective-permute-start(bf16[1024,128]{1,0:T(8,128)(2,1)S(1)} %collective-permute-done.refs_2_.refs_3_.refs_12_), channel_id=1, source_target_pairs={{24,8},{28,12},{25,9},{29,13},{26,10},{30,14},{27,11},{31,15}} | collective-permute-start | bytes 786440 | tf_op jit(solution)/shard_map/ppermute | solution.py:588
  39.3 4.9 %collective-permute-start.19 = (bf16[1056,128]{1,0:T(8,128)(2,1)S(1)}, bf16[1056,128]{1,0:T(8,128)(2,1)S(1)}, u32[]{:S(2)}, u32[]{:S(2)}) collective-permute-start(bf16[1056,128]{1,0:T(8,128)(2,1)S(1)} %get-tuple-element.30), channel_id=1, source_target_pairs={{8,24},{12,28},{9,25},{13,29},{10,26},{14,30},{11,27},{15,31}} | collective-permute-start | bytes 811016 | tf_op jit(solution)/shard_map/ppermute | solution.py:588
  44.2 6.0 %collective-permute-done.7.refs_0_ = bf16[1024,128]{1,0:T(8,128)(2,1)S(1)} collective-permute-done((bf16[1024,128]{1,0:T(8,128)(2,1)S(1)}, bf16[1024,128]{1,0:T(8,128)(2,1)S(1)}, u32[]{:S(2)}, u32[]{:S(2)}) %collective-permute-start.7) | collective-permute-done | bytes 262176 | tf_op jit(solution)/shard_map/ppermute | solution.py:588
  50.2 5.9 %shard_map.38 = (bf16[1056,128]{1,0:T(8,128)(2,1)S(1)}, bf16[1056,128]{1,0:T(8,128)(2,1)S(1)}) custom-call(s32[24,128]{1,0:T(8,128)S(1)} %block_tables.1.tab, bf16[1024,128]{1,0:T(8,128)(2,1)S(1)} %collective-permute-done.7.refs_0_, bf16[1024,128]{1,0:T(8,128)(2,1)S(1)} %collective-permute-done.8.refs_1_, ...), custom_call_target="tpu_custom_call" | custom-call | tf_op jit(solution)/shard_map/pallas_call | solution.py:475
  56.8 1.3 %collective-permute-start.12 = (bf16[1056,128]{1,0:T(8,128)(2,1)S(1)}, bf16[1056,128]{1,0:T(8,128)(2,1)S(1)}, u32[]{:S(2)}, u32[]{:S(2)}) collective-permute-start(bf16[1056,128]{1,0:T(8,128)(2,1)S(1)} %get-tuple-element.25), channel_id=1, source_target_pairs={{8,28},{12,24},{9,29},{13,25},{10,30},{14,26},{11,31},{15,27}} | collective-permute-start | bytes 811016 | tf_op jit(solution)/shard_map/ppermute | solution.py:588
  58.2 1.4 %collective-permute-start.11 = (bf16[1056,128]{1,0:T(8,128)(2,1)S(1)}, bf16[1056,128]{1,0:T(8,128)(2,1)S(1)}, u32[]{:S(2)}, u32[]{:S(2)}) collective-permute-start(bf16[1056,128]{1,0:T(8,128)(2,1)S(1)} %get-tuple-element.24), channel_id=1, source_target_pairs={{8,20},{12,16},{16,28},{20,24},{9,21},{13,17},{17,29},{21,25},{10,... | collective-permute-start | bytes 811016 | tf_op jit(solution)/shard_map/ppermute | solution.py:588
  59.6 6.1 %shard_map.37 = (bf16[1056,128]{1,0:T(8,128)(2,1)S(1)}, bf16[1056,128]{1,0:T(8,128)(2,1)S(1)}) custom-call(s32[24,128]{1,0:T(8,128)S(1)} %block_tables.1.tab, bf16[1024,128]{1,0:T(8,128)(2,1)S(1)} %get-tuple-element.18.refs_0_, bf16[2,1024,128]{2,1,0:T(8,128)(2,1)S(1)} %get-tuple-element.19.refs_1_.refs_2_.refs_11_, ...), custom_call_target="tpu_custom_call" | custom-call | tf_op jit(solution)/shard_map/pallas_call | solution.py:475
  65.7 1.3 %collective-permute-start.6 = (bf16[1056,128]{1,0:T(8,128)(2,1)S(1)}, bf16[1056,128]{1,0:T(8,128)(2,1)S(1)}, u32[]{:S(2)}, u32[]{:S(2)}) collective-permute-start(bf16[1056,128]{1,0:T(8,128)(2,1)S(1)} %get-tuple-element.23), channel_id=1, source_target_pairs={{0,4},{4,0},{8,12},{12,8},{16,20},{20,16},{24,28},{28,24},{1,5},{5... | collective-permute-start | bytes 811016 | tf_op jit(solution)/shard_map/ppermute | solution.py:588
  68.2 2.9 %collective-permute-done.6.own = bf16[1056,128]{1,0:T(8,128)(2,1)S(1)} collective-permute-done((bf16[1056,128]{1,0:T(8,128)(2,1)S(1)}, bf16[1056,128]{1,0:T(8,128)(2,1)S(1)}, u32[]{:S(2)}, u32[]{:S(2)}) %collective-permute-start.6) | collective-permute-done | bytes 270368 | tf_op jit(solution)/shard_map/ppermute | solution.py:588
  71.9 1.8 %collective-permute-start.13 = (bf16[1024,128]{1,0:T(8,128)(2,1)S(1)}, bf16[1024,128]{1,0:T(8,128)(2,1)S(1)}, u32[]{:S(2)}, u32[]{:S(2)}) collective-permute-start(bf16[1024,128]{1,0:T(8,128)(2,1)S(1)} %combine.2.refs_2_), channel_id=1, source_target_pairs={{0,2},{1,3},{2,0},{3,1},{4,6},{5,7},{6,4},{7,5},{8,10},{9,11},{10,... | collective-permute-start | bytes 786440 | tf_op jit(solution)/shard_map/ppermute | solution.py:591
  73.7 3.0 %collective-permute-start.23 = (bf16[1024,128]{1,0:T(8,128)(2,1)S(1)}, bf16[1024,128]{1,0:T(8,128)(2,1)S(1)}, u32[]{:S(2)}, u32[]{:S(2)}) collective-permute-start(bf16[1024,128]{1,0:T(8,128)(2,1)S(1)} %combine.3.refs_0_), channel_id=1, source_target_pairs={{0,1},{1,0},{2,3},{3,2},{4,5},{5,4},{6,7},{7,6},{8,9},{9,8},{10,11... | collective-permute-start | bytes 786440 | tf_op jit(solution)/shard_map/ppermute | solution.py:591
  76.8 4.2 %collective-permute-start.21 = (bf16[1024,128]{1,0:T(8,128)(2,1)S(1)}, bf16[1024,128]{1,0:T(8,128)(2,1)S(1)}, u32[]{:S(2)}, u32[]{:S(2)}) collective-permute-start(bf16[1024,128]{1,0:T(8,128)(2,1)S(1)} %collective-permute-done.20.refs_0_), channel_id=1, source_target_pairs={{0,1},{1,0},{2,3},{3,2},{4,5},{5,4},{6,7},{7,6},{8,9},{9,8},{10,11... | collective-permute-start | bytes 786440 | tf_op jit(solution)/shard_map/ppermute | solution.py:591
  81.0 2.8 %collective-permute-start.14 = (bf16[1024,128]{1,0:T(8,128)(2,1)S(1)}, bf16[1024,128]{1,0:T(8,128)(2,1)S(1)}, u32[]{:S(2)}, u32[]{:S(2)}) collective-permute-start(bf16[1024,128]{1,0:T(8,128)(2,1)S(1)} %collective-permute-done.13.refs_0_), channel_id=1, source_target_pairs={{0,1},{1,0},{2,3},{3,2},{4,5},{5,4},{6,7},{7,6},{8,9},{9,8},{10,11... | collective-permute-start | bytes 786440 | tf_op jit(solution)/shard_map/ppermute | solution.py:591
  83.8 1.3 %project.3.refs_4_ = f32[1024,1024]{1,0:T(8,128)S(1)} custom-call(s32[1,3]{1,0:T(1,128)S(1)} %add_bitcast_fusion.ids_ref, bf16[1024,1024]{1,0:T(8,128)(2,1)S(1)} %copy-done, bf16[1024,128]{1,0:T(8,128)(2,1)S(1)} %combine.3.refs_0_, bf16[1024,128]{1,0:T(8,128)(2,1)S(1)} %collective-permute-done.23.refs_1_), custom_call_target="tpu_custom_call" | custom-call | tf_op jit(solution)/shard_map/project/pallas_call | solution.py:561
  85.1 1.8 %project.4.refs_2_ = f32[1024,1024]{1,0:T(8,128)S(1)} custom-call(s32[1,3]{1,0:T(1,128)S(1)} %add_bitcast_fusion.ids_ref, bf16[1024,1024]{1,0:T(8,128)(2,1)S(1)} %copy-done, bf16[1024,128]{1,0:T(8,128)(2,1)S(1)} %collective-permute-done.20.refs_0_, bf16[1024,128]{1,0:T(8,128)(2,1)S(1)} %collective-permute-done.21.refs_1_, ...), custom_call_target="tpu_custom_call" | custom-call | tf_op jit(solution)/shard_map/project/pallas_call | solution.py:561
  87.0 2.4 %project.5 = bf16[1024,1024]{1,0:T(8,128)(2,1)} custom-call(s32[1,3]{1,0:T(1,128)S(1)} %add_bitcast_fusion.ids_ref, bf16[1024,1024]{1,0:T(8,128)(2,1)S(1)} %copy-done, bf16[1024,128]{1,0:T(8,128)(2,1)S(1)} %collective-permute-done.13.refs_0_, bf16[1024,128]{1,0:T(8,128)(2,1)S(1)} %collective-permute-done.14.refs_1_, f32[1024,1024]{1,0:T(8,128)S(1)} %project.4.refs_2_), custom_call_target="tpu_custom_call" | custom-call | tf_op jit(solution)/shard_map/project/pallas_call | solution.py:561
  (33 shorter events, 6.3 us)
Async XLA Ops:
  0.0 21.4 %copy-start.1 = (s32[2,64]{1,0:T(2,128)S(1)}, s32[2,64]{1,0:T(2,128)}, u32[]{:S(2)}) copy-start(s32[2,64]{1,0:T(2,128)} %table_ref.1) | copy-start | bytes 1540
  3.1 7.3 %collective-permute-start = (bf16[1024,128]{1,0:T(8,128)(2,1)S(1)}, bf16[1024,128]{1,0:T(8,128)(2,1)S(1)}, u32[]{:S(2)}, u32[]{:S(2)}) collective-permute-start(bf16[1024,128]{1,0:T(8,128)(2,1)S(1)} %get-tuple-element.20), channel_id=1, source_target_pairs={{0,4},{4,0},{8,12},{12,8},{16,20},{20,16},{24,28},{28,24},{1,5},{5... | collective-permute-start | bytes 786440 | tf_op jit(solution)/shard_map/ppermute | solution.py:588
  4.4 17.8 %collective-permute-start.3 = (bf16[2,1024,128]{2,1,0:T(8,128)(2,1)S(1)}, bf16[2,1024,128]{2,1,0:T(8,128)(2,1)S(1)}, u32[]{:S(2)}, u32[]{:S(2)}) collective-permute-start(bf16[2,1024,128]{2,1,0:T(8,128)(2,1)S(1)} %get-tuple-element.19.refs_1_.refs_2_.refs_11_), channel_id=1, source_target_pairs={{0,8},{4,12},{1,9},{5,13},{2,10},{6,14},{3,11},{7,15}} | collective-permute-start | bytes 1572872 | tf_op jit(solution)/shard_map/ppermute | solution.py:588
  5.7 10.3 %collective-permute-start.1 = (bf16[1024,128]{1,0:T(8,128)(2,1)S(1)}, bf16[1024,128]{1,0:T(8,128)(2,1)S(1)}, u32[]{:S(2)}, u32[]{:S(2)}) collective-permute-start(bf16[1024,128]{1,0:T(8,128)(2,1)S(1)} %get-tuple-element.21), channel_id=1, source_target_pairs={{0,4},{4,0},{8,12},{12,8},{16,20},{20,16},{24,28},{28,24},{1,5},{5... | collective-permute-start | bytes 786440 | tf_op jit(solution)/shard_map/ppermute | solution.py:588
  6.0 14.1 %collective-permute-start.15 = (bf16[1024,128]{1,0:T(8,128)(2,1)S(1)}, bf16[1024,128]{1,0:T(8,128)(2,1)S(1)}, u32[]{:S(2)}, u32[]{:S(2)}) collective-permute-start(bf16[1024,128]{1,0:T(8,128)(2,1)S(1)} %get-tuple-element.18.refs_0_), channel_id=1, source_target_pairs={{16,8},{20,12},{17,9},{21,13},{18,10},{22,14},{19,11},{23,15}} | collective-permute-start | bytes 786440 | tf_op jit(solution)/shard_map/ppermute | solution.py:588
  7.3 14.9 %collective-permute-start.16 = (bf16[1024,128]{1,0:T(8,128)(2,1)S(1)}, bf16[1024,128]{1,0:T(8,128)(2,1)S(1)}, u32[]{:S(2)}, u32[]{:S(2)}) collective-permute-start(bf16[1024,128]{1,0:T(8,128)(2,1)S(1)} %get-tuple-element.18.refs_0_), channel_id=1, source_target_pairs={{24,8},{28,12},{25,9},{29,13},{26,10},{30,14},{27,11},{31,15}} | collective-permute-start | bytes 786440 | tf_op jit(solution)/shard_map/ppermute | solution.py:588
  10.4 11.8 %collective-permute-start.2 = (bf16[1024,128]{1,0:T(8,128)(2,1)S(1)}, bf16[1024,128]{1,0:T(8,128)(2,1)S(1)}, u32[]{:S(2)}, u32[]{:S(2)}) collective-permute-start(bf16[1024,128]{1,0:T(8,128)(2,1)S(1)} %get-tuple-element.22), channel_id=1, source_target_pairs={{0,4},{4,0},{8,12},{12,8},{16,20},{20,16},{24,28},{28,24},{1,5},{5... | collective-permute-start | bytes 786440 | tf_op jit(solution)/shard_map/ppermute | solution.py:588
  16.0 11.5 %collective-permute-start.4 = (bf16[1024,128]{1,0:T(8,128)(2,1)S(1)}, bf16[1024,128]{1,0:T(8,128)(2,1)S(1)}, u32[]{:S(2)}, u32[]{:S(2)}) collective-permute-start(bf16[1024,128]{1,0:T(8,128)(2,1)S(1)} %collective-permute-done.refs_2_.refs_3_.refs_12_), channel_id=1, source_target_pairs={{0,8},{4,12},{1,9},{5,13},{2,10},{6,14},{3,11},{7,15}} | collective-permute-start | bytes 786440 | tf_op jit(solution)/shard_map/ppermute | solution.py:588
  20.1 10.2 %collective-permute-start.5 = (bf16[1024,128]{1,0:T(8,128)(2,1)S(1)}, bf16[1024,128]{1,0:T(8,128)(2,1)S(1)}, u32[]{:S(2)}, u32[]{:S(2)}) collective-permute-start(bf16[1024,128]{1,0:T(8,128)(2,1)S(1)} %collective-permute-done.1.refs_3_.refs_4_.refs_13_), channel_id=1, source_target_pairs={{0,8},{4,12},{1,9},{5,13},{2,10},{6,14},{3,11},{7,15}} | collective-permute-start | bytes 786440 | tf_op jit(solution)/shard_map/ppermute | solution.py:588
  34.0 31.8 %collective-permute-start.17 = (bf16[1056,128]{1,0:T(8,128)(2,1)S(1)}, bf16[1056,128]{1,0:T(8,128)(2,1)S(1)}, u32[]{:S(2)}, u32[]{:S(2)}) collective-permute-start(bf16[1056,128]{1,0:T(8,128)(2,1)S(1)} %get-tuple-element.29), channel_id=1, source_target_pairs={{8,16},{12,20},{9,17},{13,21},{10,18},{14,22},{11,19},{15,23}} | collective-permute-start | bytes 811016 | tf_op jit(solution)/shard_map/ppermute | solution.py:588
  35.3 4.0 %collective-permute-start.9 = (bf16[1024,128]{1,0:T(8,128)(2,1)S(1)}, bf16[1024,128]{1,0:T(8,128)(2,1)S(1)}, u32[]{:S(2)}, u32[]{:S(2)}) collective-permute-start(bf16[1024,128]{1,0:T(8,128)(2,1)S(1)} %get-tuple-element.18.refs_0_), channel_id=1, source_target_pairs={{24,16},{28,20},{25,17},{29,21},{26,18},{30,22},{27,19},{31,23}} | collective-permute-start | bytes 786440 | tf_op jit(solution)/shard_map/ppermute | solution.py:588
  36.0 8.2 %collective-permute-start.10 = (bf16[1024,128]{1,0:T(8,128)(2,1)S(1)}, bf16[1024,128]{1,0:T(8,128)(2,1)S(1)}, u32[]{:S(2)}, u32[]{:S(2)}) collective-permute-start(bf16[1024,128]{1,0:T(8,128)(2,1)S(1)} %collective-permute-done.refs_2_.refs_3_.refs_12_), channel_id=1, source_target_pairs={{24,16},{28,20},{25,17},{29,21},{26,18},{30,22},{27,19},{31,23}} | collective-permute-start | bytes 786440 | tf_op jit(solution)/shard_map/ppermute | solution.py:588
  36.7 13.5 %collective-permute-start.7 = (bf16[1024,128]{1,0:T(8,128)(2,1)S(1)}, bf16[1024,128]{1,0:T(8,128)(2,1)S(1)}, u32[]{:S(2)}, u32[]{:S(2)}) collective-permute-start(bf16[1024,128]{1,0:T(8,128)(2,1)S(1)} %collective-permute-done.refs_2_.refs_3_.refs_12_), channel_id=1, source_target_pairs={{16,8},{20,12},{17,9},{21,13},{18,10},{22,14},{19,11},{23,15}} | collective-permute-start | bytes 786440 | tf_op jit(solution)/shard_map/ppermute | solution.py:588
  38.0 12.2 %collective-permute-start.8 = (bf16[1024,128]{1,0:T(8,128)(2,1)S(1)}, bf16[1024,128]{1,0:T(8,128)(2,1)S(1)}, u32[]{:S(2)}, u32[]{:S(2)}) collective-permute-start(bf16[1024,128]{1,0:T(8,128)(2,1)S(1)} %collective-permute-done.refs_2_.refs_3_.refs_12_), channel_id=1, source_target_pairs={{24,8},{28,12},{25,9},{29,13},{26,10},{30,14},{27,11},{31,15}} | collective-permute-start | bytes 786440 | tf_op jit(solution)/shard_map/ppermute | solution.py:588
  39.3 27.8 %collective-permute-start.19 = (bf16[1056,128]{1,0:T(8,128)(2,1)S(1)}, bf16[1056,128]{1,0:T(8,128)(2,1)S(1)}, u32[]{:S(2)}, u32[]{:S(2)}) collective-permute-start(bf16[1056,128]{1,0:T(8,128)(2,1)S(1)} %get-tuple-element.30), channel_id=1, source_target_pairs={{8,24},{12,28},{9,25},{13,29},{10,26},{14,30},{11,27},{15,31}} | collective-permute-start | bytes 811016 | tf_op jit(solution)/shard_map/ppermute | solution.py:588
  56.1 10.9 %collective-permute-start.18 = (bf16[1056,128]{1,0:T(8,128)(2,1)S(1)}, bf16[1056,128]{1,0:T(8,128)(2,1)S(1)}, u32[]{:S(2)}, u32[]{:S(2)}) collective-permute-start(bf16[1056,128]{1,0:T(8,128)(2,1)S(1)} %get-tuple-element.25), channel_id=1, source_target_pairs={{16,24},{20,28},{17,25},{21,29},{18,26},{22,30},{19,27},{23,31}} | collective-permute-start | bytes 811016 | tf_op jit(solution)/shard_map/ppermute | solution.py:588
  56.8 11.4 %collective-permute-start.12 = (bf16[1056,128]{1,0:T(8,128)(2,1)S(1)}, bf16[1056,128]{1,0:T(8,128)(2,1)S(1)}, u32[]{:S(2)}, u32[]{:S(2)}) collective-permute-start(bf16[1056,128]{1,0:T(8,128)(2,1)S(1)} %get-tuple-element.25), channel_id=1, source_target_pairs={{8,28},{12,24},{9,29},{13,25},{10,30},{14,26},{11,31},{15,27}} | collective-permute-start | bytes 811016 | tf_op jit(solution)/shard_map/ppermute | solution.py:588
  58.1 25.7 %copy-start = (bf16[1024,1024]{1,0:T(8,128)(2,1)S(1)}, bf16[1024,1024]{1,0:T(8,128)(2,1)}, u32[]{:S(2)}) copy-start(bf16[1024,1024]{1,0:T(8,128)(2,1)} %weight_ref.5) | copy-start | bytes 6291460
  58.2 10.0 %collective-permute-start.11 = (bf16[1056,128]{1,0:T(8,128)(2,1)S(1)}, bf16[1056,128]{1,0:T(8,128)(2,1)S(1)}, u32[]{:S(2)}, u32[]{:S(2)}) collective-permute-start(bf16[1056,128]{1,0:T(8,128)(2,1)S(1)} %get-tuple-element.24), channel_id=1, source_target_pairs={{8,20},{12,16},{16,28},{20,24},{9,21},{13,17},{17,29},{21,25},{10,... | collective-permute-start | bytes 811016 | tf_op jit(solution)/shard_map/ppermute | solution.py:588
  65.7 5.4 %collective-permute-start.6 = (bf16[1056,128]{1,0:T(8,128)(2,1)S(1)}, bf16[1056,128]{1,0:T(8,128)(2,1)S(1)}, u32[]{:S(2)}, u32[]{:S(2)}) collective-permute-start(bf16[1056,128]{1,0:T(8,128)(2,1)S(1)} %get-tuple-element.23), channel_id=1, source_target_pairs={{0,4},{4,0},{8,12},{12,8},{16,20},{20,16},{24,28},{28,24},{1,5},{5... | collective-permute-start | bytes 811016 | tf_op jit(solution)/shard_map/ppermute | solution.py:588
  67.9 8.9 %collective-permute-start.20 = (bf16[1024,128]{1,0:T(8,128)(2,1)S(1)}, bf16[1024,128]{1,0:T(8,128)(2,1)S(1)}, u32[]{:S(2)}, u32[]{:S(2)}) collective-permute-start(bf16[1024,128]{1,0:T(8,128)(2,1)S(1)} %combine.3.refs_0_), channel_id=1, source_target_pairs={{0,2},{1,3},{2,0},{3,1},{4,6},{5,7},{6,4},{7,5},{8,10},{9,11},{10,... | collective-permute-start | bytes 786440 | tf_op jit(solution)/shard_map/ppermute | solution.py:591
  71.9 9.1 %collective-permute-start.13 = (bf16[1024,128]{1,0:T(8,128)(2,1)S(1)}, bf16[1024,128]{1,0:T(8,128)(2,1)S(1)}, u32[]{:S(2)}, u32[]{:S(2)}) collective-permute-start(bf16[1024,128]{1,0:T(8,128)(2,1)S(1)} %combine.2.refs_2_), channel_id=1, source_target_pairs={{0,2},{1,3},{2,0},{3,1},{4,6},{5,7},{6,4},{7,5},{8,10},{9,11},{10,... | collective-permute-start | bytes 786440 | tf_op jit(solution)/shard_map/ppermute | solution.py:591
  73.7 10.1 %collective-permute-start.23 = (bf16[1024,128]{1,0:T(8,128)(2,1)S(1)}, bf16[1024,128]{1,0:T(8,128)(2,1)S(1)}, u32[]{:S(2)}, u32[]{:S(2)}) collective-permute-start(bf16[1024,128]{1,0:T(8,128)(2,1)S(1)} %combine.3.refs_0_), channel_id=1, source_target_pairs={{0,1},{1,0},{2,3},{3,2},{4,5},{5,4},{6,7},{7,6},{8,9},{9,8},{10,11... | collective-permute-start | bytes 786440 | tf_op jit(solution)/shard_map/ppermute | solution.py:591
  76.8 8.3 %collective-permute-start.22 = (bf16[1024,128]{1,0:T(8,128)(2,1)S(1)}, bf16[1024,128]{1,0:T(8,128)(2,1)S(1)}, u32[]{:S(2)}, u32[]{:S(2)}) collective-permute-start(bf16[1024,128]{1,0:T(8,128)(2,1)S(1)} %combine.2.refs_2_), channel_id=1, source_target_pairs={{0,1},{1,0},{2,3},{3,2},{4,5},{5,4},{6,7},{7,6},{8,9},{9,8},{10,11... | collective-permute-start | bytes 786440 | tf_op jit(solution)/shard_map/ppermute | solution.py:591
  76.8 8.3 %collective-permute-start.21 = (bf16[1024,128]{1,0:T(8,128)(2,1)S(1)}, bf16[1024,128]{1,0:T(8,128)(2,1)S(1)}, u32[]{:S(2)}, u32[]{:S(2)}) collective-permute-start(bf16[1024,128]{1,0:T(8,128)(2,1)S(1)} %collective-permute-done.20.refs_0_), channel_id=1, source_target_pairs={{0,1},{1,0},{2,3},{3,2},{4,5},{5,4},{6,7},{7,6},{8,9},{9,8},{10,11... | collective-permute-start | bytes 786440 | tf_op jit(solution)/shard_map/ppermute | solution.py:591
  81.0 5.9 %collective-permute-start.14 = (bf16[1024,128]{1,0:T(8,128)(2,1)S(1)}, bf16[1024,128]{1,0:T(8,128)(2,1)S(1)}, u32[]{:S(2)}, u32[]{:S(2)}) collective-permute-start(bf16[1024,128]{1,0:T(8,128)(2,1)S(1)} %collective-permute-done.13.refs_0_), channel_id=1, source_target_pairs={{0,1},{1,0},{2,3},{3,2},{4,5},{5,4},{6,7},{7,6},{8,9},{9,8},{10,11... | collective-permute-start | bytes 786440 | tf_op jit(solution)/shard_map/ppermute | solution.py:591
